TPU v7x, 32 devices: a whole 2x2x4 slice. The times are simulated.
32 devices in a mesh: dp: 8 (over z, y), fsdp: 4 (over x, core).
Axes of the slice: x: 2, y: 2, z: 4, core: 2. Of those that a mesh axis runs over, the one named last changes fastest.
Arguments:
- pixels: bfloat16 [8, 512, 192], P('dp', 'fsdp'), may hold values from -6 to 6
- targets: bfloat16 [8, 512, 192], P('dp', 'fsdp'), may hold values from 2 to 6
- valid_mask: int32 [8, 512, 192], P('dp', 'fsdp'), may hold values 0 or 1
- lat_weight: float32 [8, 512], P('dp', 'fsdp'), may hold values from 0.1 to 1
- segment_ids: int32 [8, 512], P('dp'), may hold values from 0 to 3, never falling along the last dimension, each value on 1 to 256 neighbouring positions
- present_vars: int32 [8, 48], P('dp'), may hold values from 0 to 1, as said below
- lead_index: int32 [8], P('dp'), may hold values from 0 to 7
- step_count: int32 [1], replicated, may hold values from 1 to 20
- w_agg: float32 [1024, 3072], P(('dp', 'fsdp')), may hold values from -0.1875 to 0.1875
- w_attn: float32 [1024, 4096], P(('dp', 'fsdp')), may hold values from -0.1875 to 0.1875
- w_mlp: float32 [1024, 8192], P(('dp', 'fsdp')), may hold values from -0.1875 to 0.1875
- w_io: float32 [1024, 944], P(('dp', 'fsdp')), may hold values from -3 to 3
- w_small: float32 [1024, 9], P(('dp', 'fsdp')), may hold values from 0.5 to 1.5
- m_agg: float32 [1024, 3072], P(('dp', 'fsdp')), may hold values from -0.00390625 to 0.00390625
- m_attn: float32 [1024, 4096], P(('dp', 'fsdp')), may hold values from -0.00390625 to 0.00390625
- m_mlp: float32 [1024, 8192], P(('dp', 'fsdp')), may hold values from -0.00390625 to 0.00390625
- m_io: float32 [1024, 944], P(('dp', 'fsdp')), may hold values from -0.00390625 to 0.00390625
- m_small: float32 [1024, 9], P(('dp', 'fsdp')), may hold values from -0.015625 to 0.015625
- v_agg: float32 [1024, 3072], P(('dp', 'fsdp')), may hold values from 2.9932032e-08 to 4.789125e-07
- v_attn: float32 [1024, 4096], P(('dp', 'fsdp')), may hold values from 2.9932032e-08 to 4.789125e-07
- v_mlp: float32 [1024, 8192], P(('dp', 'fsdp')), may hold values from 2.9932032e-08 to 4.789125e-07
- v_io: float32 [1024, 944], P(('dp', 'fsdp')), may hold values from 2.9932032e-08 to 4.789125e-07
- v_small: float32 [1024, 9], P(('dp', 'fsdp')), may hold values from 4.789125e-07 to 7.6626e-06
Outputs:
- loss: float32 [], replicated
- grad_norm: float32 [], replicated
- new_agg: float32 [1024, 3072], P(('dp', 'fsdp'))
- new_attn: float32 [1024, 4096], P(('dp', 'fsdp'))
- new_mlp: float32 [1024, 8192], P(('dp', 'fsdp'))
- new_io: float32 [1024, 944], P(('dp', 'fsdp'))
- new_small: float32 [1024, 9], P(('dp', 'fsdp'))
- copy_agg: bfloat16 [1024, 3072], P(('dp', 'fsdp'))
- copy_attn: bfloat16 [1024, 4096], P(('dp', 'fsdp'))
- copy_mlp: bfloat16 [1024, 8192], P(('dp', 'fsdp'))
- copy_io: bfloat16 [1024, 944], P(('dp', 'fsdp'))
- copy_small: bfloat16 [1024, 9], P(('dp', 'fsdp'))
- moment_agg: float32 [1024, 3072], P(('dp', 'fsdp'))
- moment_attn: float32 [1024, 4096], P(('dp', 'fsdp'))
- moment_mlp: float32 [1024, 8192], P(('dp', 'fsdp'))
- moment_io: float32 [1024, 944], P(('dp', 'fsdp'))
- moment_small: float32 [1024, 9], P(('dp', 'fsdp'))
- square_agg: float32 [1024, 3072], P(('dp', 'fsdp'))
- square_attn: float32 [1024, 4096], P(('dp', 'fsdp'))
- square_mlp: float32 [1024, 8192], P(('dp', 'fsdp'))
- square_io: float32 [1024, 944], P(('dp', 'fsdp'))
- square_small: float32 [1024, 9], P(('dp', 'fsdp'))
Inputs may be any that keep to these rules, and one draw needn't show every extreme that they name: `present_vars`: every row has at least one present variable.
All inputs are finite; a program needn't handle non-finite values. No bound on the sum of `valid_mask` on one device may be relied on, other than what follows from the above.
Results may differ from a plain program's by a relative error of at most 0.0019.
The roundings to bfloat16 on the way count: a program that leaves them out, or rounds other values in their place, can miss the bound.
Values may be sent and summed in bfloat16 or wider, within the bound.
A program may use at most 384 MiB of HBM per device.

v0:
```python
import jax
import jax.numpy as jnp
from jax import lax
from jax.sharding import PartitionSpec as P

D = 1024
HEADS = 16
HEAD_DIM = 64
FF = 4096
VARS = 48
PIX = 4
LEAD_STEPS = 8


highest = lax.Precision.HIGHEST
norm_eps = 1e-05
clip_limit = 1.0
decay_rate = 0.05
adam_eps = 1e-08
learn_rates = (0.03, 0.03, 0.03, 0.2, 0.3)


def as_sent(array):

    def short(part):
        return part.astype(jnp.bfloat16) if part.dtype == jnp.float32 else part

    return jax.tree.map(short, array)


def to_bf_value(v):
    return lax.optimization_barrier(v.astype(jnp.bfloat16)).astype(jnp.float32)


def same_value(v):
    return v


def value_keep(v):
    return (to_bf_value(v), None)


def value_pass(kept, grad):
    return (grad,)


def grad_keep(v):
    return (v, None)


def grad_lower(kept, grad):
    return (to_bf_value(grad),)


def round_value(v):
    rounder = jax.custom_vjp(to_bf_value)
    rounder.defvjp(value_keep, value_pass)
    return rounder(v)


def round_grad(v):
    rounder = jax.custom_vjp(same_value)
    rounder.defvjp(grad_keep, grad_lower)
    return rounder(v)


def plain_product(left, right):
    return jnp.dot(
        left.astype(jnp.bfloat16), right.astype(jnp.bfloat16), preferred_element_type=jnp.float32
    )


def product_keep(left, right):
    return (plain_product(left, right), (left.astype(jnp.bfloat16), right.astype(jnp.bfloat16)))


def product_back(kept, grad):
    left_low, right_low = kept
    grad_low = grad.astype(jnp.bfloat16)
    return (
        jnp.dot(grad_low, right_low.T, preferred_element_type=jnp.float32),
        jnp.dot(left_low.T, grad_low, preferred_element_type=jnp.float32),
    )


def product(left, right):
    multiply = jax.custom_vjp(plain_product)
    multiply.defvjp(product_keep, product_back)
    return multiply(left, right)


def matmul(left, right):
    return round_grad(product(round_value(left), right))


def layer_norm(values, gain, offset):
    average = jnp.mean(values, axis=-1, keepdims=True)
    centred = values - average
    spread = jnp.mean(centred * centred, axis=-1, keepdims=True)
    return centred * lax.rsqrt(spread + norm_eps) * gain + offset


def softmax_rows(scores):
    top = jnp.max(scores, axis=-1, keepdims=True)
    powers = jnp.exp(scores - top)
    return powers / jnp.sum(powers, axis=-1, keepdims=True)


def positions(segment_row):
    places = jnp.arange(segment_row.shape[0], dtype=jnp.int32)
    starts = jnp.concatenate([jnp.ones((1,), dtype=jnp.bool_), segment_row[1:] != segment_row[:-1]])
    first = lax.cummax(jnp.where(starts, places, 0), axis=0)
    return places - first


def front_part(weights, pixel_rows, present_row, lead_value, pos_index):
    w_agg, w_attn, w_mlp, w_io, w_small = weights
    rows_here = pixel_rows.shape[0]
    width = VARS * PIX
    patch_w = w_io[:, :width].reshape(D, VARS, PIX)
    embedded = jnp.einsum(
        "lvp,dvp->lvd", pixel_rows.reshape(rows_here, VARS, PIX), patch_w, precision=highest
    )
    embedded = round_grad(embedded + w_io[:, 2 * width : 2 * width + VARS].T[None])
    pairs = round_value(matmul(embedded.reshape(rows_here * VARS, D), w_agg[:, : 2 * D]))
    pairs = pairs.reshape(rows_here, VARS, 2, HEADS, HEAD_DIM)
    queries = w_small[:, 0].reshape(HEADS, HEAD_DIM)
    scores = round_grad(
        jnp.einsum("he,lvhe->lhv", queries, pairs[:, :, 0], precision=highest)
    ) * HEAD_DIM ** (-0.5)
    scores = jnp.where(present_row[None, None, :] > 0, scores, -1000000000.0)
    attend = round_value(softmax_rows(scores))
    mixed = round_grad(
        jnp.einsum("lhv,lvhe->lhe", attend, pairs[:, :, 1], precision=highest)
    ).reshape(rows_here, D)
    pooled = matmul(mixed, w_agg[:, 2 * D :])
    lead_embed = lead_value * w_small[:, 7] + w_small[:, 8]
    state = pooled + jnp.take(w_io[:, 2 * width + VARS :].T, pos_index, axis=0) + lead_embed[None]
    normed = layer_norm(state, w_small[:, 1], w_small[:, 2])
    projected = round_value(matmul(normed, w_attn[:, : 3 * D]))
    return (projected[:, :D], projected[:, D:], state)


def rear_part(weights, queries, pairs_full, state, seg_query, seg_keys, target, pixel_weight):
    w_agg, w_attn, w_mlp, w_io, w_small = weights
    rows_here = queries.shape[0]
    keys_here = pairs_full.shape[0]
    width = VARS * PIX
    q_heads = queries.reshape(rows_here, HEADS, HEAD_DIM)
    key_heads = pairs_full[:, :D].reshape(keys_here, HEADS, HEAD_DIM)
    value_heads = pairs_full[:, D:].reshape(keys_here, HEADS, HEAD_DIM)
    scores = round_grad(
        jnp.einsum("qhe,khe->hqk", q_heads, key_heads, precision=highest)
    ) * HEAD_DIM ** (-0.5)
    same_crop = seg_query[:, None] == seg_keys[None, :]
    scores = jnp.where(same_crop[None], scores, -1000000000.0)
    attend = round_value(softmax_rows(scores))
    mixed = round_grad(jnp.einsum("hqk,khe->qhe", attend, value_heads, precision=highest)).reshape(
        rows_here, D
    )
    hidden = state + matmul(mixed, w_attn[:, 3 * D :])
    normed = layer_norm(hidden, w_small[:, 3], w_small[:, 4])
    lifted = jax.nn.gelu(matmul(normed, w_mlp[:, :FF]), approximate=False)
    hidden = hidden + matmul(lifted, w_mlp[:, FF:].T)
    normed = layer_norm(hidden, w_small[:, 5], w_small[:, 6])
    predicted = matmul(normed, w_io[:, width : 2 * width]) * D ** (-0.5)
    error = predicted - target
    return jnp.sum(pixel_weight * error * error)


def adamw(weight, grad, moment, second, step_value, learn_rate):
    moment = 0.5 * moment + 0.5 * grad
    second = 0.5 * second + 0.5 * grad * grad
    correct = 1.0 - jnp.power(jnp.float32(0.5), step_value)
    update = moment / correct / (jnp.sqrt(second / correct) + adam_eps) + decay_rate * weight
    fresh = weight - learn_rate * update
    return (fresh, fresh.astype(jnp.bfloat16), moment, second)


def local(
    pixels,
    targets,
    valid_mask,
    lat_weight,
    segment_ids,
    present_vars,
    lead_index,
    step_count,
    w_agg,
    w_attn,
    w_mlp,
    w_io,
    w_small,
    m_agg,
    m_attn,
    m_mlp,
    m_io,
    m_small,
    v_agg,
    v_attn,
    v_mlp,
    v_io,
    v_small,
):
    masters = (w_agg, w_attn, w_mlp, w_io, w_small)
    firsts = (m_agg, m_attn, m_mlp, m_io, m_small)
    seconds = (v_agg, v_attn, v_mlp, v_io, v_small)
    rows_here = pixels.shape[1]
    offset = lax.axis_index("fsdp") * rows_here
    seg_keys = segment_ids[0]
    seg_query = lax.dynamic_slice_in_dim(seg_keys, offset, rows_here)
    pos_index = lax.dynamic_slice_in_dim(positions(seg_keys), offset, rows_here)
    lead_value = (lead_index[0].astype(jnp.float32) + 1.0) / LEAD_STEPS
    pixel_rows = pixels[0].astype(jnp.float32)
    target = targets[0].astype(jnp.float32)
    present_row = present_vars[0]
    present_cols = jnp.repeat(present_row.astype(jnp.float32), PIX)
    pixel_weight = (
        lat_weight[0][:, None] * valid_mask[0].astype(jnp.float32) * present_cols[None, :]
    )
    local_weight = jnp.sum(pixel_weight)
    total_weight = lax.psum(local_weight, ("dp", "fsdp"))

    def front_fn(weights):
        return front_part(weights, pixel_rows, present_row, lead_value, pos_index)

    def rear_fn(weights, queries, pairs_full, state):
        return rear_part(
            weights, queries, pairs_full, state, seg_query, seg_keys, target, pixel_weight
        )

    shards = tuple((piece.astype(jnp.bfloat16) for piece in masters))
    gathered = (
        lax.all_gather(shards[0], ("dp", "fsdp"), axis=0, tiled=True),
        lax.all_gather(shards[1], ("dp", "fsdp"), axis=0, tiled=True),
        lax.all_gather(shards[2], ("dp", "fsdp"), axis=0, tiled=True),
        lax.all_gather(shards[3], ("dp", "fsdp"), axis=0, tiled=True),
        lax.all_gather(shards[4], ("dp", "fsdp"), axis=0, tiled=True),
    )
    whole = tuple((piece.astype(jnp.float32) for piece in gathered))
    queries, pairs, state = front_fn(whole)
    pairs_full = lax.all_gather(pairs.astype(jnp.bfloat16), "fsdp", axis=0, tiled=True).astype(
        jnp.float32
    )
    numerator = rear_fn(whole, queries, pairs_full, state)
    loss_sum = lax.psum(numerator, ("dp", "fsdp"))
    again = (
        lax.all_gather(shards[0], ("dp", "fsdp"), axis=0, tiled=True),
        lax.all_gather(shards[1], ("dp", "fsdp"), axis=0, tiled=True),
        lax.all_gather(shards[2], ("dp", "fsdp"), axis=0, tiled=True),
        lax.all_gather(shards[3], ("dp", "fsdp"), axis=0, tiled=True),
        lax.all_gather(shards[4], ("dp", "fsdp"), axis=0, tiled=True),
    )
    whole = tuple((piece.astype(jnp.float32) for piece in again))
    (queries, pairs, state), front_pull = jax.vjp(front_fn, whole)
    numerator, rear_pull = jax.vjp(rear_fn, whole, queries, pairs_full, state)
    cotangent = 1.0 / total_weight
    rear_grads, d_queries, d_pairs_full, d_state = rear_pull(cotangent)
    d_pairs = jax.tree.map(
        lambda part: part.astype(jnp.float32),
        lax.psum_scatter(as_sent(d_pairs_full), "fsdp", scatter_dimension=0, tiled=True),
    )
    (front_grads,) = front_pull((d_queries, d_pairs, d_state))
    local_grads = jax.tree.map(jnp.add, rear_grads, front_grads)
    reduced = (
        lax.psum_scatter(local_grads[0], ("dp", "fsdp"), scatter_dimension=0, tiled=True),
        lax.psum_scatter(local_grads[1], ("dp", "fsdp"), scatter_dimension=0, tiled=True),
        lax.psum_scatter(local_grads[2], ("dp", "fsdp"), scatter_dimension=0, tiled=True),
        lax.psum_scatter(local_grads[3], ("dp", "fsdp"), scatter_dimension=0, tiled=True),
        lax.psum_scatter(local_grads[4], ("dp", "fsdp"), scatter_dimension=0, tiled=True),
    )
    squares = sum((jnp.sum(piece * piece) for piece in reduced))
    total_squares = lax.psum(squares, ("dp", "fsdp"))
    grad_norm = jnp.sqrt(total_squares)
    factor = jnp.minimum(1.0, clip_limit / grad_norm)
    loss = loss_sum / total_weight
    step_value = step_count[0].astype(jnp.float32)
    results = [
        adamw(
            masters[index],
            reduced[index] * factor,
            firsts[index],
            seconds[index],
            step_value,
            learn_rates[index],
        )
        for index in range(5)
    ]
    news = tuple((entry[0] for entry in results))
    copies = tuple((entry[1] for entry in results))
    moments = tuple((entry[2] for entry in results))
    squared = tuple((entry[3] for entry in results))
    return (
        loss,
        grad_norm,
        news[0],
        news[1],
        news[2],
        news[3],
        news[4],
        copies[0],
        copies[1],
        copies[2],
        copies[3],
        copies[4],
        moments[0],
        moments[1],
        moments[2],
        moments[3],
        moments[4],
        squared[0],
        squared[1],
        squared[2],
        squared[3],
        squared[4],
    )


def solution(mesh):
    return jax.shard_map(
        local,
        mesh=mesh,
        in_specs=(
            P("dp", "fsdp", None),
            P("dp", "fsdp", None),
            P("dp", "fsdp", None),
            P("dp", "fsdp"),
            P("dp", None),
            P("dp", None),
            P("dp"),
            P(),
            P(("dp", "fsdp"), None),
            P(("dp", "fsdp"), None),
            P(("dp", "fsdp"), None),
            P(("dp", "fsdp"), None),
            P(("dp", "fsdp"), None),
            P(("dp", "fsdp"), None),
            P(("dp", "fsdp"), None),
            P(("dp", "fsdp"), None),
            P(("dp", "fsdp"), None),
            P(("dp", "fsdp"), None),
            P(("dp", "fsdp"), None),
            P(("dp", "fsdp"), None),
            P(("dp", "fsdp"), None),
            P(("dp", "fsdp"), None),
            P(("dp", "fsdp"), None),
        ),
        out_specs=(
            P(),
            P(),
            P(("dp", "fsdp"), None),
            P(("dp", "fsdp"), None),
            P(("dp", "fsdp"), None),
            P(("dp", "fsdp"), None),
            P(("dp", "fsdp"), None),
            P(("dp", "fsdp"), None),
            P(("dp", "fsdp"), None),
            P(("dp", "fsdp"), None),
            P(("dp", "fsdp"), None),
            P(("dp", "fsdp"), None),
            P(("dp", "fsdp"), None),
            P(("dp", "fsdp"), None),
            P(("dp", "fsdp"), None),
            P(("dp", "fsdp"), None),
            P(("dp", "fsdp"), None),
            P(("dp", "fsdp"), None),
            P(("dp", "fsdp"), None),
            P(("dp", "fsdp"), None),
            P(("dp", "fsdp"), None),
            P(("dp", "fsdp"), None),
        ),
        check_vma=False,
    )
```

profile of v0, /device:TPU:0, one launch (start us, length us, event | category | flops | bytes accessed | tf_op | source)
XLA Modules:
  0.0 1885.1 jit_solution(2741136301803360249)
XLA Ops:
  13.2 43.8 %all-gather = bf16[32,32,9]{1,2,0:T(8,128)(2,1)S(1)} all-gather(bf16[1,32,9]{1,2,0:T(8,128)(2,1)S(1)} %convert_bitcast_fusion), channel_id=1, replica_groups=mesh['dp'=8,'fsdp'=4] {'dp','fsdp'}, dimensions={0}, use_global_device_ids=true | all-gather | bytes 19008 | tf_op jit(solution)/shard_map/all_gather | solution.py:238
  60.8 9.8 all-gather.7.cloned.1.call-done
  81.0 22.2 %copy.122 = bf16[128,48,1024]{2,1,0:T(8,128)(2,1)} copy(bf16[128,48,1024]{2,0,1:T(8,128)(2,1)S(1)} %fusion) | data formatting | bytes 25165824 | tf_op jit(solution)/shard_map/convert_element_type | solution.py:32
  104.9 37.6 %all-gather.9.cloned.1.call-done = bf16[1024,3072]{1,0:T(8,128)(2,1)} async-done(((bf16[32,3072]{1,0:T(8,128)(2,1)}), bf16[1024,3072]{1,0:T(8,128)(2,1)}) %all-gather.9.cloned.1.call-update) | async-done | bytes 6291472 | tf_op jit(solution)/shard_map/all_gather | solution.py:234
  142.5 33.6 %convolution_convert_fusion = bf16[6144,2048]{1,0:T(8,128)(2,1)} fusion(bf16[6144,1024]{1,0:T(8,128)(2,1)} %bitcast.185, bf16[1024,3072]{1,0:T(8,128)(2,1)} %all-gather.9.cloned.1.call-done), kind=kOutput, calls=%fused_computation.12 | convolution fusion | flops 25782386688 | bytes 41943040 | tf_op jit(solution)/shard_map/dot_general | solution.py:68
  176.1 70.8 %reshape.346 = bf16[128,48,2,16,64]{4,3,2,1,0:T(8,128)(2,1)} reshape(bf16[6144,2048]{1,0:T(8,128)(2,1)} %convolution_convert_fusion) | data formatting | bytes 50331648 | tf_op jit(solution)/shard_map/reshape | solution.py:126
  246.9 18.8 multiply_reduce_fusion.3
  270.6 18.4 multiply_reduce_fusion.2
  307.3 14.7 all-gather.13.cloned.1.call-done
  342.5 97.6 %all-gather.15.cloned.1.call-done = bf16[1024,8192]{1,0:T(8,128)(2,1)} async-done(((bf16[32,8192]{1,0:T(8,128)(2,1)}), bf16[1024,8192]{1,0:T(8,128)(2,1)}) %all-gather.15.cloned.1.call-update) | async-done | bytes 16777232 | tf_op jit(solution)/shard_map/all_gather | solution.py:236
  440.1 8.9 multiply_convert_fusion.2
  455.1 38.9 %psum.22 = f32[]{:T(128)} all-reduce(f32[]{:T(128)} %get-tuple-element.119), channel_id=1, replica_groups=mesh['dp'=8,'fsdp'=4] {'dp','fsdp'}, use_global_device_ids=true, to_apply=%region_15.16 | all-reduce | flops 1 | bytes 8 | tf_op jit(solution)/shard_map/psum | solution.py:222
  501.4 8.4 add_convert_fusion.3
  543.2 26.4 %reduce-scatter.19.cloned.1.call-done = bf16[128,2048]{1,0:T(8,128)(2,1)} async-done(((bf16[512,2048]{1,0:T(8,128)(2,1)}), bf16[128,2048]{1,0:T(8,128)(2,1)}) %reduce-scatter.19.cloned.1.call-update) | async-done | bytes 524304
  572.9 6.1 multiply_reduce_fusion.7
  588.9 32.7 %multiply_bitcast_fusion.1 = (f32[128,48,1,16,64]{4,3,2,1,0:T(8,128)}, f32[128,16,48]{1,2,0:T(8,128)S(1)}) fusion(f32[128,16,48]{1,2,0:T(8,128)} %copy-done.3, f32[128,16,64]{2,1,0:T(8,128)} %copy.129, bf16[128,48,2,16,64]{4,3,2,1,0:T(8,128)(2,1)} %reshape.346), kind=kLoop, calls=%fused_computation.8 | loop fusion | flops 25067520 | bytes 39059456 | tf_op jit(solution)/shard_map/transpose(jvp())/broadcast_in_dim | solution.py:134
  628.1 26.3 %multiply_reduce_fusion = (f32[16,64]{1,0:T(8,128)S(1)}, f32[128,48,1,16,64]{4,3,2,1,0:T(8,128)}) fusion(f32[16,128,48]{0,2,1:T(8,128)S(1)} %bitcast_convert_fusion, bf16[128,48,2,16,64]{4,3,2,1,0:T(8,128)(2,1)} %reshape.346, f32[16,64]{1,0:T(8,128)S(1)} %copy-done.60), kind=kLoop, calls=%fused_computation.3 | loop fusion | flops 25164800 | bytes 38150144 | tf_op jit(solution)/shard_map/transpose(jvp(he,lvhe->lhv))/dot_general | solution.py:129
  654.3 48.4 %add_convert_fusion = bf16[128,48,2,16,64]{4,3,2,1,0:T(8,128)(2,1)} fusion(f32[128,48,1,16,64]{4,3,2,1,0:T(8,128)} %get-tuple-element.162, f32[128,48,1,16,64]{4,3,2,1,0:T(8,128)} %get-tuple-element.165), kind=kLoop, calls=%fused_computation.2 | loop fusion | flops 25165824 | bytes 75497472 | tf_op jit(solution)/shard_map/transpose(jvp())/convert_element_type | solution.py:64
  702.7 68.0 %convert_element_type.322 = bf16[6144,2048]{1,0:T(8,128)(2,1)} reshape(bf16[128,48,2,16,64]{4,3,2,1,0:T(8,128)(2,1)} %add_convert_fusion) | data formatting | bytes 50331648 | tf_op jit(solution)/shard_map/transpose(jvp())/convert_element_type | solution.py:64
  770.8 32.8 %convolution_convert_fusion.1 = bf16[6144,1024]{1,0:T(8,128)(2,1)} fusion(bf16[6144,2048]{1,0:T(8,128)(2,1)} %convert_element_type.322, bf16[1024,3072]{1,0:T(8,128)(2,1)} %all-gather.9.cloned.1.call-done), kind=kOutput, calls=%fused_computation.18 | convolution fusion | flops 25776095232 | bytes 41943040 | tf_op jit(solution)/shard_map/transpose(jvp())/dot_general | solution.py:89
  803.6 17.5 copy.130
  821.1 7.5 convert_reduce_fusion
  828.6 7.9 fusion.39
  851.4 32.7 %fusion.107 = f32[1024,2048]{1,0:T(8,128)S(1)} fusion(bf16[6144,1024]{1,0:T(8,128)(2,1)} %bitcast.186, bf16[6144,2048]{1,0:T(8,128)(2,1)} %convert_element_type.322), kind=kOutput, calls=%fused_computation.209 | convolution fusion | flops 25769803776 | bytes 46137344 | tf_op jit(solution)/shard_map/transpose(jvp())/dot_general | solution.py:89
  892.4 6.3 pad_add_fusion.1
  904.8 11.1 pad_add_fusion
  916.9 58.2 %reduce-scatter.23.cloned.1.call-done = f32[32,9]{1,0:T(8,128)} async-done(((f32[1024,9]{1,0:T(8,128)}), f32[32,9]{1,0:T(8,128)}) %reduce-scatter.23.cloned.1.call-update) | async-done | bytes 1168
  976.5 137.6 %reduce-scatter.21.cloned.1.call-done = f32[32,944]{1,0:T(8,128)} async-done(((f32[1024,944]{1,0:T(8,128)}), f32[32,944]{1,0:T(8,128)}) %reduce-scatter.21.cloned.1.call-update) | async-done | bytes 120848 | tf_op jit(solution)/shard_map/reduce_scatter | solution.py:269
  1115.9 156.0 %reduce-scatter.13.cloned.1.call-done = f32[32,3072]{1,0:T(8,128)} async-done(((f32[1024,3072]{1,0:T(8,128)}), f32[32,3072]{1,0:T(8,128)}) %reduce-scatter.13.cloned.1.call-update) | async-done | bytes 393232 | tf_op jit(solution)/shard_map/reduce_scatter | solution.py:266
  1273.6 182.5 %reduce-scatter.15.cloned.1.call-done = f32[32,4096]{1,0:T(8,128)} async-done(((f32[1024,4096]{1,0:T(8,128)}), f32[32,4096]{1,0:T(8,128)}) %reduce-scatter.15.cloned.1.call-update) | async-done | bytes 524304 | tf_op jit(solution)/shard_map/reduce_scatter | solution.py:267
  1459.3 355.2 %reduce-scatter.17.cloned.1.call-done = f32[32,8192]{1,0:T(8,128)} async-done(((f32[1024,8192]{1,0:T(8,128)}), f32[32,8192]{1,0:T(8,128)}) %reduce-scatter.17.cloned.1.call-update) | async-done | bytes 1048592 | tf_op jit(solution)/shard_map/reduce_scatter | solution.py:268
  1818.5 47.3 %all-reduce.25 = (f32[]{:T(128)}, f32[]{:T(128)}) all-reduce(f32[]{:T(128)} %get-tuple-element.120, f32[]{:T(128)S(6)} %add.341), channel_id=1, replica_groups=mesh['dp'=8,'fsdp'=4] {'dp','fsdp'}, use_global_device_ids=true, to_apply=%region_13.14 | all-reduce | flops 2 | bytes 16 | tf_op jit(solution)/shard_map/psum | solution.py:246
  (378 shorter events, 175.7 us)
Async XLA Ops:
  7.2 70.1 %copy-start = (bf16[1,128,192]{1,2,0:T(8,128)(2,1)S(1)}, bf16[1,128,192]{1,2,0:T(8,128)(2,1)}, u32[]{:S(2)}) copy-start(bf16[1,128,192]{1,2,0:T(8,128)(2,1)} %param.23) | copy-start | bytes 147460
  7.2 63.5 %all-gather.7.cloned.1.call-start = ((), (), s32[]{:S(2)}) async-start(), calls=%async_computation.6 | async-start | bytes 2162688 | tf_op jit(solution)/shard_map/all_gather | solution.py:237
  8.8 133.7 %all-gather.9.cloned.1.call-start = ((), (), s32[]{:S(2)}) async-start(), calls=%async_computation.7 | async-start | bytes 6488064 | tf_op jit(solution)/shard_map/all_gather | solution.py:234
  10.6 284.5 %all-gather.11.cloned.1.call-start = ((), (), s32[]{:S(2)}) async-start(), calls=%async_computation.8 | async-start | bytes 8650752 | tf_op jit(solution)/shard_map/all_gather | solution.py:235
  12.4 309.5 %all-gather.13.cloned.1.call-start = ((), (), s32[]{:S(2)}) async-start(), calls=%async_computation.9 | async-start | bytes 2621440 | tf_op jit(solution)/shard_map/all_gather | solution.py:242
  59.2 187.7 %copy-start.59 = (f32[16,64]{1,0:T(8,128)}, f32[16,64]{1,0:T(8,128)S(1)}, u32[]{:S(2)}) copy-start(f32[16,64]{1,0:T(8,128)S(1)} %convert.28) | copy-start | bytes 12292
  60.2 207.6 %copy-start.71 = (pred[48]{0:T(512)(128)(4,1)}, pred[48]{0:T(512)(128)(4,1)S(1)}, u32[]{:S(2)}) copy-start(pred[48]{0:T(512)(128)(4,1)S(1)} %compare_bitcast_fusion) | copy-start | bytes 148
  60.8 232.8 %copy-start.62 = (f32[1024,1]{0,1:T(1,128)}, f32[1024,1]{0,1:T(1,128)S(1)}, u32[]{:S(2)}) copy-start(f32[1024,1]{0,1:T(1,128)S(1)} %get-tuple-element.171) | copy-start | bytes 12292
  60.8 279.7 %copy-start.64 = (f32[1024,1]{0,1:T(1,128)}, f32[1024,1]{0,1:T(1,128)S(1)}, u32[]{:S(2)}) copy-start(f32[1024,1]{0,1:T(1,128)S(1)} %get-tuple-element.169) | copy-start | bytes 12292
  300.7 139.4 %all-gather.15.cloned.1.call-start = ((), (), s32[]{:S(2)}) async-start(), calls=%async_computation.10 | async-start | bytes 17301504 | tf_op jit(solution)/shard_map/all_gather | solution.py:236
  302.9 266.7 %reduce-scatter.19.cloned.1.call-start = ((), (), s32[]{:S(2)}) async-start(), calls=%async_computation.14 | async-start | bytes 2621440
  340.3 108.7 %copy-start.80 = (f32[128]{0:T(128)}, f32[128]{0:T(128)S(1)}, u32[]{:S(2)}) copy-start(f32[128]{0:T(128)S(1)} %broadcast_multiply_fusion.2) | copy-start | bytes 1540
  340.5 108.5 %copy-start.98 = (f32[128]{0:T(128)}, f32[128]{0:T(128)S(1)}, u32[]{:S(2)}) copy-start(f32[128]{0:T(128)S(1)} %multiply_reduce_fusion.15) | copy-start | bytes 1540
  340.5 108.5 %copy-start.92 = (f32[128]{0:T(128)}, f32[128]{0:T(128)S(1)}, u32[]{:S(2)}) copy-start(f32[128]{0:T(128)S(1)} %fusion.79) | copy-start | bytes 1540
  537.1 438.1 %reduce-scatter.23.cloned.1.call-start = ((), (), s32[]{:S(2)}) async-start(), calls=%async_computation.16 | async-start | bytes 540672
  539.7 33.2 %copy-start.63 = (f32[1024,1]{0,1:T(1,128)S(1)}, f32[1024,1]{0,1:T(1,128)}, u32[]{:S(2)}) copy-start(f32[1024,1]{0,1:T(1,128)} %copy-done.62) | copy-start | bytes 12292
  539.7 33.2 %copy-start.79 = (f32[128]{0:T(128)S(1)}, f32[128]{0:T(128)}, u32[]{:S(2)}) copy-start(f32[128]{0:T(128)} %copy-done.78) | copy-start | bytes 1540
  539.7 33.2 %copy-start.91 = (f32[128]{0:T(128)S(1)}, f32[128]{0:T(128)}, u32[]{:S(2)}) copy-start(f32[128]{0:T(128)} %copy-done.90) | copy-start | bytes 1540
  841.0 273.2 %reduce-scatter.21.cloned.1.call-start = ((), (), s32[]{:S(2)}) async-start(), calls=%async_computation.15 | async-start | bytes 4325376 | tf_op jit(solution)/shard_map/reduce_scatter | solution.py:269
  849.7 422.2 %reduce-scatter.13.cloned.1.call-start = ((), (), s32[]{:S(2)}) async-start(), calls=%async_computation.11 | async-start | bytes 12976128 | tf_op jit(solution)/shard_map/reduce_scatter | solution.py:266
  888.9 567.2 %reduce-scatter.15.cloned.1.call-start = ((), (), s32[]{:S(2)}) async-start(), calls=%async_computation.12 | async-start | bytes 17301504 | tf_op jit(solution)/shard_map/reduce_scatter | solution.py:267
  898.8 915.7 %reduce-scatter.17.cloned.1.call-start = ((), (), s32[]{:S(2)}) async-start(), calls=%async_computation.13 | async-start | bytes 34603008 | tf_op jit(solution)/shard_map/reduce_scatter | solution.py:268
  915.9 952.0 %copy-start.68 = (f32[32,9]{0,1:T(8,128)S(1)}, f32[32,9]{0,1:T(8,128)}, u32[]{:S(2)}) copy-start(f32[32,9]{0,1:T(8,128)} %param.35) | copy-start | bytes 3460
  915.9 952.0 %copy-start.76 = (f32[32,9]{0,1:T(8,128)S(1)}, f32[32,9]{0,1:T(8,128)}, u32[]{:S(2)}) copy-start(f32[32,9]{0,1:T(8,128)} %param.45) | copy-start | bytes 3460
  915.9 952.0 %copy-start.77 = (f32[32,9]{0,1:T(8,128)S(1)}, f32[32,9]{0,1:T(8,128)}, u32[]{:S(2)}) copy-start(f32[32,9]{0,1:T(8,128)} %param.40) | copy-start | bytes 3460
  915.9 952.6 %copy-start.34 = (f32[32,3072]{1,0:T(8,128)S(1)}, f32[32,3072]{1,0:T(8,128)}, u32[]{:S(2)}) copy-start(f32[32,3072]{1,0:T(8,128)} %param.31) | copy-start | bytes 1179652
  916.0 952.6 %copy-start.55 = (f32[32,3072]{1,0:T(8,128)S(1)}, f32[32,3072]{1,0:T(8,128)}, u32[]{:S(2)}) copy-start(f32[32,3072]{1,0:T(8,128)} %param.41) | copy-start | bytes 1179652
  916.0 952.6 %copy-start.56 = (f32[32,3072]{1,0:T(8,128)S(1)}, f32[32,3072]{1,0:T(8,128)}, u32[]{:S(2)}) copy-start(f32[32,3072]{1,0:T(8,128)} %param.36) | copy-start | bytes 1179652
  916.0 955.0 %copy-start.31 = (f32[32,4096]{1,0:T(8,128)S(1)}, f32[32,4096]{1,0:T(8,128)}, u32[]{:S(2)}) copy-start(f32[32,4096]{1,0:T(8,128)} %param.32) | copy-start | bytes 1572868
  916.0 955.0 %copy-start.50 = (f32[32,4096]{1,0:T(8,128)S(1)}, f32[32,4096]{1,0:T(8,128)}, u32[]{:S(2)}) copy-start(f32[32,4096]{1,0:T(8,128)} %param.42) | copy-start | bytes 1572868
  916.0 955.0 %copy-start.51 = (f32[32,4096]{1,0:T(8,128)S(1)}, f32[32,4096]{1,0:T(8,128)}, u32[]{:S(2)}) copy-start(f32[32,4096]{1,0:T(8,128)} %param.37) | copy-start | bytes 1572868
  1456.1 414.9 %copy-start.32 = (f32[32,4096]{1,0:T(8,128)S(1)}, f32[32,4096]{1,0:T(8,128)}, u32[]{:S(2)}) copy-start(f32[32,4096]{1,0:T(8,128)} %reduce-scatter.15.cloned.1.call-done) | copy-start | bytes 1572868
  (88 other events, 380.5 us)
Sparse Core Ops, SparseCore 0:
  11.5 59.1 all-gather.6
  74.1 68.3 all-gather.8
  145.9 75.9 all-gather.10
  300.8 21.0 all-gather.12
  325.2 114.8 all-gather.14
  537.2 32.3 reduce-scatter.18
  841.1 133.9 reduce-scatter.22
  977.4 136.6 reduce-scatter.20
  1120.1 151.7 reduce-scatter.12
  1274.2 181.9 reduce-scatter.14
  1458.6 355.8 reduce-scatter.16
where the time goes:
time: 1900 us; the launch traced here: 1890 us
  waiting for transfers between devices  1080 us (57%)
  other arithmetic  236 us (12%)
  local copies, waits for them, and re-layouts  235 us (12%)
  matrix products  182 us (10%)
  blocking collectives  130 us (7%)
  between operations  25.6 us (1%)
    reduce_scatter x1, waiting for transfers between devices, local(): lax.psum_scatter(local_grads[2], ('dp', 'fsdp'), scatter_dimension=0, til...  355 us
    reduce_scatter x1, waiting for transfers between devices, local(): lax.psum_scatter(local_grads[1], ('dp', 'fsdp'), scatter_dimension=0, til...  183 us
    reduce_scatter x1, waiting for transfers between devices, local(): lax.psum_scatter(local_grads[0], ('dp', 'fsdp'), scatter_dimension=0, til...  156 us
    reduce_scatter x1, waiting for transfers between devices, local(): lax.psum_scatter(local_grads[3], ('dp', 'fsdp'), scatter_dimension=0, til...  138 us
    dot_general x14, matrix products, product(): return multiply(left, right)  102 us
    all_gather x1, waiting for transfers between devices, local(): lax.all_gather(shards[2], ('dp', 'fsdp'), axis=0, tiled=True)  97.6 us
    unnamed x13, waiting for transfers between devices  84.8 us
    convert_element_type x3, local copies, waits for them, and re-layouts, round_grad(): return rounder(v)  71.6 us
  transfers between devices with their start and end apart: 11, of which 10 were waited for; matrix products, arithmetic and copies ran while one was open for 16% of the time, Pallas kernels for 0%

commit v1 on v0

v1 whole, which is shorter than its diff:
```python
import jax
import jax.numpy as jnp
from jax import lax
from jax.sharding import PartitionSpec as P

D = 1024
HEADS = 16
HEAD_DIM = 64
FF = 4096
VARS = 48
PIX = 4
LEAD_STEPS = 8
WIDTH = VARS * PIX
SPAN = 256
MIX = WIDTH + VARS
USED = 2 * WIDTH + VARS + SPAN

norm_eps = 1e-05
clip_limit = 1.0
decay_rate = 0.05
adam_eps = 1e-08
learn_rates = (0.03, 0.03, 0.03, 0.2, 0.3)
f32 = jnp.float32
bf16 = jnp.bfloat16
highest = lax.Precision.HIGHEST


def dot(left, right, dims):
    return lax.dot_general(left, right, (dims, ((), ())), preferred_element_type=f32)


def mm(left, right):
    return dot(left, right, ((1,), (0,)))


def mm_t(left, right):
    return dot(left, right, ((1,), (1,)))


def t_mm(left, right):
    return dot(left, right, ((0,), (0,)))


def exact(eq, left, right):
    return jnp.einsum(eq, left, right, precision=highest, preferred_element_type=f32)


def norm_forward(values, gain, offset):
    average = jnp.mean(values, axis=-1, keepdims=True)
    centred = values - average
    scale = lax.rsqrt(jnp.mean(centred * centred, axis=-1, keepdims=True) + norm_eps)
    unit = centred * scale
    return (unit * gain[None] + offset[None]).astype(bf16), unit, scale


def norm_backward(grad, unit, scale, gain):
    inner = grad * gain[None]
    mean_inner = jnp.mean(inner, axis=-1, keepdims=True)
    mean_product = jnp.mean(inner * unit, axis=-1, keepdims=True)
    back = scale * (inner - mean_inner - unit * mean_product)
    return back, jnp.sum(grad * unit, axis=0), jnp.sum(grad, axis=0)


def adamw(weight, grad, moment, second, step_value, learn_rate):
    moment = 0.5 * moment + 0.5 * grad
    second = 0.5 * second + 0.5 * grad * grad
    correct = 1.0 - jnp.power(f32(0.5), step_value)
    update = moment / correct / (jnp.sqrt(second / correct) + adam_eps) + decay_rate * weight
    fresh = weight - learn_rate * update
    return (fresh, fresh.astype(bf16), moment, second)


def ag(part):
    return lax.all_gather(part, "fsdp", axis=0, tiled=True)


def make_local(n_dp, n_f):
    def local(
        pixels, targets, valid_mask, lat_weight, segment_ids, present_vars, lead_index, step_count,
        w_agg, w_attn, w_mlp, w_io, w_small,
        m_agg, m_attn, m_mlp, m_io, m_small,
        v_agg, v_attn, v_mlp, v_io, v_small,
    ):
        masters = (w_agg, w_attn, w_mlp, w_io, w_small)
        firsts = (m_agg, m_attn, m_mlp, m_io, m_small)
        seconds = (v_agg, v_attn, v_mlp, v_io, v_small)
        rows = pixels.shape[1]
        row_len = segment_ids.shape[1]
        strip = w_agg.shape[0]
        own = lax.axis_index("fsdp")
        heads_here = HEADS // n_f
        wide = heads_here * HEAD_DIM

        seg = segment_ids[0]
        seg_own = lax.dynamic_slice_in_dim(seg, own * rows, rows)
        below = jnp.sum((seg[None, :] < seg_own[:, None]).astype(jnp.int32), axis=1)
        pos = own * rows + jnp.arange(rows, dtype=jnp.int32) - below
        onehot = (pos[:, None] == jnp.arange(SPAN, dtype=jnp.int32)[None, :]).astype(bf16)
        lead = (lead_index[0].astype(f32) + 1.0) / LEAD_STEPS
        pixel_rows = pixels[0]
        target = targets[0].astype(f32)
        present = present_vars[0]
        spread = (jnp.arange(MIX) // PIX)[None, :] == jnp.arange(VARS)[:, None]
        embed_col = (jnp.arange(MIX) - WIDTH)[None, :] == jnp.arange(VARS)[:, None]
        in_pixels = (jnp.arange(MIX) < WIDTH)[None, :]
        expand = jnp.where(in_pixels, spread, embed_col).astype(bf16)
        present_cols = jnp.repeat(present.astype(f32), PIX)
        pixel_weight = lat_weight[0][:, None] * valid_mask[0].astype(f32) * present_cols[None, :]
        total = lax.psum(jnp.sum(pixel_weight), ("dp", "fsdp"))

        pack = jnp.concatenate(
            [
                w_io[:, :USED].astype(bf16),
                w_small.astype(bf16),
                jnp.zeros((strip, 768 - USED - 9), bf16),
                w_agg.astype(bf16),
            ],
            axis=1,
        )
        head = lax.all_gather(pack, ("dp", "fsdp"), axis=0, tiled=True)
        attn = lax.all_gather(w_attn.astype(bf16), ("dp", "fsdp"), axis=0, tiled=True)
        mlp = lax.all_gather(w_mlp.astype(bf16), ("dp", "fsdp"), axis=0, tiled=True)
        w240 = jnp.concatenate([head[:, :WIDTH], head[:, 2 * WIDTH : 2 * WIDTH + VARS]], axis=1)
        w_pred = head[:, WIDTH : 2 * WIDTH]
        w_pos = head[:, 2 * WIDTH + VARS : USED]
        small = head[:, USED : USED + 9].astype(f32).T
        agg_kv = head[:, 768 : 768 + 2 * D]
        agg_out = head[:, 768 + 2 * D :]
        w_qkv = attn[:, : 3 * D]
        w_out = attn[:, 3 * D :]
        w_up = mlp[:, :FF]
        w_down = mlp[:, FF:]

        pix_t = jnp.concatenate([pixel_rows.T, jnp.ones((VARS, rows), bf16)], axis=0)
        table = t_mm(w240, agg_kv)
        table_k = table[:, :D].reshape(MIX, HEADS, HEAD_DIM)
        table_v = table[:, D:].reshape(MIX, HEADS, HEAD_DIM)
        query = small[0].reshape(HEADS, HEAD_DIM)
        folded = jnp.sum(table_k * query[None], axis=2)
        block = folded.T[:, None, :] * expand.astype(f32)[None]
        score = exact("xc,cl->xl", block.reshape(HEADS * VARS, MIX), pix_t.astype(f32))
        score = score.reshape(HEADS, VARS, rows) * HEAD_DIM ** (-0.5)
        score = jnp.where(present[None, :, None] > 0, score, -1000000000.0)
        top = jnp.max(score, axis=1, keepdims=True)
        power = jnp.exp(score - top)
        soft = power / jnp.sum(power, axis=1, keepdims=True)
        share = soft.astype(bf16)
        pix_f = pix_t.astype(f32)
        lifted_share = jnp.einsum("vc,hvl->hcl", expand, share, preferred_element_type=f32) * pix_f[None]
        mixed_a = exact("che,hcl->hel", table_v, lifted_share).reshape(D, rows).T.astype(bf16)
        lead_embed = lead * small[7] + small[8]
        h0 = mm(mixed_a, agg_out) + mm_t(onehot, w_pos) + lead_embed[None]
        norm0, unit0, scale0 = norm_forward(h0, small[1], small[2])
        qkv = mm(norm0, w_qkv).astype(bf16)
        part = qkv.reshape(rows, 3, n_f, wide)
        part = lax.all_to_all(part, "fsdp", split_axis=2, concat_axis=0, tiled=True)
        part = part.reshape(row_len, 3, heads_here, HEAD_DIM)
        q, k, v = (part[:, i].transpose(1, 0, 2) for i in range(3))
        att_score = jnp.einsum("hqe,hke->hqk", q, k, preferred_element_type=f32) * HEAD_DIM ** (-0.5)
        same = seg[:, None] == seg[None, :]
        att_score = jnp.where(same[None], att_score, -1000000000.0)
        att_top = jnp.max(att_score, axis=-1, keepdims=True)
        att_power = jnp.exp(att_score - att_top)
        att_soft = att_power / jnp.sum(att_power, axis=-1, keepdims=True)
        att = att_soft.astype(bf16)
        mixed_h = jnp.einsum("hqk,hke->qhe", att, v, preferred_element_type=f32)
        mixed_h = mixed_h.reshape(row_len, wide).astype(bf16)
        mixed_all = lax.all_gather(mixed_h, "fsdp", axis=1, tiled=True)
        mixed = lax.dynamic_slice_in_dim(mixed_all, own * rows, rows, axis=0)
        h1 = h0 + mm(mixed, w_out)
        norm1, unit1, scale1 = norm_forward(h1, small[3], small[4])
        up = mm(norm1, w_up)
        gate = 0.5 * (1.0 + lax.erf(up * (2.0**-0.5)))
        lifted = (up * gate).astype(bf16)
        h2 = h1 + mm_t(lifted, w_down)
        norm2, unit2, scale2 = norm_forward(h2, small[5], small[6])
        predicted = mm(norm2, w_pred) * D ** (-0.5)
        error = predicted - target
        weighted = pixel_weight * error
        numerator = lax.psum(jnp.sum(weighted * error), ("dp", "fsdp"))

        d_pred = (weighted * (2.0 * D ** (-0.5) / total)).astype(bf16)
        d_norm2 = mm_t(d_pred, w_pred)
        d_h2, d_gain2, d_off2 = norm_backward(d_norm2, unit2, scale2, small[5])
        d_out = d_h2.astype(bf16)
        slope = gate + up * jnp.exp(-0.5 * up * up) * 0.3989422804014327
        d_up = (mm(d_out, w_down) * slope).astype(bf16)
        d_norm1 = mm_t(d_up, w_up)
        d_in, d_gain1, d_off1 = norm_backward(d_norm1, unit1, scale1, small[3])
        d_h1 = d_h2 + d_in
        d_proj_all = ag(d_h1.astype(bf16))
        w_out_own = lax.dynamic_slice_in_dim(w_out, own * wide, wide, axis=0)
        d_mixed = mm_t(d_proj_all, w_out_own).astype(bf16).reshape(row_len, heads_here, HEAD_DIM).transpose(1, 0, 2)
        d_att = jnp.einsum("hqe,hke->hqk", d_mixed, v, preferred_element_type=f32)
        d_v = jnp.einsum("hqk,hqe->khe", att, d_mixed, preferred_element_type=f32)
        lean = jnp.sum(att_soft * d_att, axis=-1, keepdims=True)
        d_score = (att_soft * (d_att - lean) * HEAD_DIM ** (-0.5)).astype(bf16)
        d_q = jnp.einsum("hqk,hke->qhe", d_score, k, preferred_element_type=f32)
        d_k = jnp.einsum("hqk,hqe->khe", d_score, q, preferred_element_type=f32)
        d_part = jnp.stack([d_q, d_k, d_v], axis=1).astype(bf16).reshape(row_len, 3, 1, wide)
        d_qkv_all = lax.all_gather(d_part, "fsdp", axis=2, tiled=True).reshape(row_len, 3 * D)
        d_qkv = lax.dynamic_slice_in_dim(d_qkv_all, own * rows, rows, axis=0)
        d_norm0 = mm_t(d_qkv, w_qkv)
        d_in, d_gain0, d_off0 = norm_backward(d_norm0, unit0, scale0, small[1])
        d_h0 = d_h1 + d_in
        d_agg = d_h0.astype(bf16)
        d_mixed_a = mm_t(agg_out, d_agg).astype(bf16).reshape(HEADS, HEAD_DIM, rows)
        pulled = exact("che,hel->hcl", table_v, d_mixed_a.astype(f32)) * pix_f[None]
        d_share = exact("vc,hcl->hvl", expand.astype(f32), pulled)
        lean_a = jnp.sum(soft * d_share, axis=1, keepdims=True)
        d_score_a = (soft * (d_share - lean_a) * HEAD_DIM ** (-0.5)).astype(bf16)
        spread_score = jnp.einsum("vc,hvl->hcl", expand, d_score_a, preferred_element_type=f32)
        d_folded = jnp.sum(spread_score * pix_f[None], axis=2)
        d_table_v = exact("hcl,hel->che", lifted_share, d_mixed_a.astype(f32)).reshape(MIX, D)
        d_table_k = (d_folded.T[:, :, None] * query[None]).reshape(MIX, D)
        d_query = jnp.sum(d_folded.T[:, :, None] * table_k, axis=0).reshape(D)
        d_bias = jnp.sum(d_h0, axis=0)
        narrow = jnp.stack(
            [d_query, d_gain0, d_off0, d_gain1, d_off1, d_gain2, d_off2, lead * d_bias, d_bias]
            + [jnp.zeros((D,), f32)] * 7
        )
        d_table, narrow = lax.psum((jnp.concatenate([d_table_k, d_table_v], axis=1), narrow), "fsdp")

        def mine(array):
            whole = array.reshape(n_dp, n_f, strip, array.shape[1])
            return lax.dynamic_index_in_dim(whole, own, axis=1, keepdims=False).reshape(n_dp * strip, array.shape[1])

        source = jnp.arange(D)
        pick = (source // strip) % n_f == own
        place = (source // (strip * n_f)) * strip + source % strip
        choose = (pick[:, None] & (place[:, None] == jnp.arange(n_dp * strip)[None, :])).astype(bf16)

        def weight_grad(features, grads):
            return t_mm(mm(features, choose).astype(bf16), grads)

        d_agg_all = ag(d_agg)
        g_attn = jnp.concatenate(
            [weight_grad(ag(norm0), d_qkv_all), weight_grad(mixed_all, d_proj_all)], axis=1
        )
        g_mlp = jnp.concatenate(
            [weight_grad(ag(norm1), ag(d_up)), weight_grad(ag(d_out), ag(lifted))], axis=1
        )
        g_out = weight_grad(ag(mixed_a), d_agg_all)
        g_kv = exact("dc,cx->dx", mine(w240).astype(f32), d_table)
        g_240 = exact("dx,cx->dc", mine(agg_kv).astype(f32), d_table)
        g_pred = weight_grad(ag(norm2), ag(d_pred))
        g_pos = weight_grad(d_agg_all, ag(onehot))
        g_small = mine(narrow.T)[:, :9]
        g_agg = jnp.concatenate([g_kv, g_out], axis=1)
        g_misc = jnp.concatenate(
            [g_240[:, :WIDTH], g_pred, g_240[:, WIDTH:], g_pos, g_small, jnp.zeros((n_dp * strip, 768 - USED - 9), f32)],
            axis=1,
        )
        r_agg, r_attn, r_mlp, r_misc = (
            lax.psum_scatter(g, "dp", scatter_dimension=0, tiled=True) for g in (g_agg, g_attn, g_mlp, g_misc)
        )
        r_io = jnp.concatenate([r_misc[:, :USED], jnp.zeros((strip, w_io.shape[1] - USED), f32)], axis=1)
        reduced = (r_agg, r_attn, r_mlp, r_io, r_misc[:, USED : USED + 9])
        squares = lax.psum(sum(jnp.sum(piece * piece) for piece in reduced), ("dp", "fsdp"))
        grad_norm = jnp.sqrt(squares)
        factor = jnp.minimum(1.0, clip_limit / grad_norm)
        loss = numerator / total
        step_value = step_count[0].astype(f32)
        results = [
            adamw(masters[i], reduced[i] * factor, firsts[i], seconds[i], step_value, learn_rates[i]) for i in range(5)
        ]
        return (loss, grad_norm) + tuple(results[i][j] for j in range(4) for i in range(5))

    return local


def solution(mesh):
    flat = P(("dp", "fsdp"), None)
    tokens = P("dp", "fsdp", None)
    return jax.shard_map(
        make_local(mesh.shape["dp"], mesh.shape["fsdp"]),
        mesh=mesh,
        in_specs=(tokens, tokens, tokens, P("dp", "fsdp"), P("dp", None), P("dp", None), P("dp"), P()) + (flat,) * 15,
        out_specs=(P(), P()) + (flat,) * 20,
        check_vma=False,
    )
```

time: 1900 us -> 1200 us (0.63)
  waiting for transfers between devices: 1080 us -> 841 us
  local copies, waits for them, and re-layouts: 235 us -> 35.5 us
  other arithmetic: 236 us -> 58.3 us
  matrix products: 182 us -> 137 us
  blocking collectives: 130 us -> 93.6 us
    reduce_scatter x4, waiting for transfers between devices: 831 us -> 363 us  [local(): lax.psum_scatter(g, 'dp', scatter_dimension=0, tiled=True)]
    all_gather x5 -> x14, waiting for transfers between devices: 160 us -> 428 us  [the longest x9 146 us: ag(): return lax.all_gather(part, 'fsdp', axis=0, tiled=True)]
    convert_element_type x4 -> x1, local copies, waits for them, and re-layouts: 93.8 us -> 0.1 us  [local(): w_small.astype(bf16)]
    unnamed x13 -> x19, waiting for transfers between devices: 84.8 us -> 5.05 us
    reshape x4 -> x5, local copies, waits for them, and re-layouts: 71.3 us -> 8.09 us  [the longest x2 4.78 us: local(): part = qkv.reshape(rows, 3, n_f, wide)]
    convert_element_type x25 -> x19, other arithmetic: 75.6 us -> 25.1 us  [the longest x5 11.1 us: adamw(): return (fresh, fresh.astype(bf16), moment, second)]
    dot_general x29 -> x35, matrix products: 182 us -> 132 us  [the longest x21 87.7 us: dot(): lax.dot_general(left, right, (dims, ((), ())), preferred_element_type=f32)]
    dot_general x2 -> x0, other arithmetic: 45 us -> none  [front_part(): jnp.einsum('he,lvhe->lhv', queries, pairs[:, :, 0], precision=highest)]
  transfers between devices with their start and end apart: 11 -> 20, of which waited for: 10 -> 19; matrix products, arithmetic and copies ran while one was open for 16% -> 10% of each run, Pallas kernels for 0% -> 0%
where the time goes in v1:
time: 1200 us
  waiting for transfers between devices  841 us (70%)
  matrix products  137 us (11%)
  blocking collectives  93.6 us (8%)
  other arithmetic  58.3 us (5%)
  local copies, waits for them, and re-layouts  35.5 us (3%)
  between operations  25.1 us (2%)
    reduce_scatter x4, waiting for transfers between devices, local(): lax.psum_scatter(g, 'dp', scatter_dimension=0, tiled=True)  363 us
    all_gather x9, waiting for transfers between devices, ag(): return lax.all_gather(part, 'fsdp', axis=0, tiled=True)  146 us
    all_gather x1, waiting for transfers between devices, local(): mlp = lax.all_gather(w_mlp.astype(bf16), ('dp', 'fsdp'), axis=0, tiled=True)  114 us
    dot_general x21, matrix products, dot(): lax.dot_general(left, right, (dims, ((), ())), preferred_element_type=f32)  87.7 us
    all_gather x1, waiting for transfers between devices, local(): head = lax.all_gather(pack, ('dp', 'fsdp'), axis=0, tiled=True)  73.1 us
    all_gather x1, waiting for transfers between devices, local(): lax.all_gather(w_attn.astype(bf16), ('dp', 'fsdp'), axis=0, tiled=True)  56.2 us
    psum x1, blocking collectives, local(): numerator = lax.psum(jnp.sum(weighted * error), ('dp', 'fsdp'))  39.4 us
    psum x1, blocking collectives, local(): total = lax.psum(jnp.sum(pixel_weight), ('dp', 'fsdp'))  39 us
  transfers between devices with their start and end apart: 20, of which 19 were waited for; matrix products, arithmetic and copies ran while one was open for 10% of the time, Pallas kernels for 0%

profile of v1, /device:TPU:0, one launch (start us, length us, event | category | flops | bytes accessed | tf_op | source)
XLA Modules:
  0.0 1196.0 jit_solution(15080212584497687655)
XLA Ops:
  16.4 73.1 %all-gather.15.cloned.1.call-done = bf16[1024,3840]{1,0:T(8,128)(2,1)} async-done(((bf16[32,3840]{1,0:T(8,128)(2,1)}), bf16[1024,3840]{1,0:T(8,128)(2,1)}) %all-gather.15.cloned.1.call-update) | async-done | bytes 7864336 | tf_op jit(solution)/shard_map/all_gather | solution.py:120
  112.8 56.2 %all-gather.17.cloned.1.call-done = bf16[1024,4096]{1,0:T(8,128)(2,1)} async-done(((bf16[32,4096]{1,0:T(8,128)(2,1)}), bf16[1024,4096]{1,0:T(8,128)(2,1)}) %all-gather.17.cloned.1.call-update) | async-done | bytes 8388624 | tf_op jit(solution)/shard_map/all_gather | solution.py:121
  184.0 10.5 all-to-all-done
  212.7 10.5 all-gather.19.cloned.1.call-done
  227.2 114.3 %all-gather.21.cloned.1.call-done = bf16[1024,8192]{1,0:T(8,128)(2,1)} async-done(((bf16[32,8192]{1,0:T(8,128)(2,1)}), bf16[1024,8192]{1,0:T(8,128)(2,1)}) %all-gather.21.cloned.1.call-update) | async-done | bytes 16777232 | tf_op jit(solution)/shard_map/all_gather | solution.py:122
  341.4 6.7 multiply_convert_fusion.1
  348.1 6.7 fusion.225
  359.7 39.0 %psum.36 = f32[]{:T(128)} all-reduce(f32[]{:T(128)} %get-tuple-element.166), channel_id=1, replica_groups=mesh['dp'=8,'fsdp'=4] {'dp','fsdp'}, use_global_device_ids=true, to_apply=%region_15.16 | all-reduce | flops 1 | bytes 8 | tf_op jit(solution)/shard_map/psum | solution.py:109
  405.1 7.0 fusion.19
  412.2 7.5 multiply_reduce_fusion.5
  424.0 14.7 %all-gather.23.cloned.1.call-done = bf16[512,1024]{1,0:T(8,128)(2,1)} async-done(((bf16[128,1024]{1,0:T(8,128)(2,1)}), bf16[512,1024]{1,0:T(8,128)(2,1)}) %all-gather.23.cloned.1.call-update) | async-done | bytes 1048592 | tf_op jit(solution)/shard_map/all_gather | solution.py:74
  447.8 8.1 fusion.73
  456.0 8.5 fusion.70
  467.5 27.7 %all-gather.25.cloned.1.call-done = bf16[512,3,4,256]{0,3,2,1:T(8,128)(2,1)} async-done(((bf16[512,3,1,256]{0,3,2,1:T(8,128)(2,1)}), bf16[512,3,4,256]{0,3,2,1:T(8,128)(2,1)}) %all-gather.25.cloned.1.call-update) | async-done | bytes 3145744 | tf_op jit(solution)/shard_map/all_gather | solution.py:201
  523.0 7.3 all_gather.63
  532.7 7.9 all_gather.62
  542.6 34.1 %all-reduce.6.cloned.1.call-done = (f32[240,2048]{0,1:T(8,128)}, f32[8,4,32,16]{2,1,0,3:T(4,128)}) async-done(((f32[240,2048]{0,1:T(8,128)}, f32[8,4,32,16]{2,1,0,3:T(4,128)}), (f32[240,2048]{0,1:T(8,128)}, f32[8,4,32,16]{2,1,0,3:T(4,128)})) %all-reduce.6.cloned.1.call-update) | async-done | bytes 2031632 | tf_op jit(solution)/shard_map/psum | solution.py:222
  581.4 14.3 %all-gather.29.cloned.1.call-done = bf16[512,1024]{1,0:T(8,128)(2,1)} async-done(((bf16[128,1024]{1,0:T(8,128)(2,1)}), bf16[512,1024]{1,0:T(8,128)(2,1)}) %all-gather.29.cloned.1.call-update) | async-done | bytes 1048592 | tf_op jit(solution)/shard_map/all_gather | solution.py:74
  603.0 10.9 all-gather.27.cloned.1.call-done
  623.0 10.0 all-gather.31.cloned.1.call-done
  641.0 10.7 all-gather.37.cloned.1.call-done
  651.7 36.7 %all-gather.39.cloned.1.call-done = bf16[512,4096]{1,0:T(8,128)(2,1)} async-done(((bf16[128,4096]{1,0:T(8,128)(2,1)}), bf16[512,4096]{1,0:T(8,128)(2,1)}) %all-gather.39.cloned.1.call-update) | async-done | bytes 4194320 | tf_op jit(solution)/shard_map/all_gather | solution.py:74
  688.3 6.7 fusion.86
  695.1 12.0 %all-gather.33.cloned.1.call-done = bf16[512,1024]{1,0:T(8,128)(2,1)} async-done(((bf16[128,1024]{1,0:T(8,128)(2,1)}), bf16[512,1024]{1,0:T(8,128)(2,1)}) %all-gather.33.cloned.1.call-update) | async-done | bytes 1048592 | tf_op jit(solution)/shard_map/all_gather | solution.py:74
  707.1 36.5 %all-gather.35.cloned.1.call-done = bf16[512,4096]{1,0:T(8,128)(2,1)} async-done(((bf16[128,4096]{1,0:T(8,128)(2,1)}), bf16[512,4096]{1,0:T(8,128)(2,1)}) %all-gather.35.cloned.1.call-update) | async-done | bytes 4194320 | tf_op jit(solution)/shard_map/all_gather | solution.py:74
  743.6 6.7 fusion.85
  750.3 7.6 pad_maximum_fusion
  758.7 50.6 %reduce-scatter.13.cloned.1.call-done = f32[32,768]{1,0:T(8,128)} async-done(((f32[256,768]{1,0:T(8,128)}), f32[32,768]{1,0:T(8,128)}) %reduce-scatter.13.cloned.1.call-update) | async-done | bytes 98320 | tf_op jit(solution)/shard_map/reduce_scatter | solution.py:255
  812.3 74.4 %reduce-scatter.7.cloned.1.call-done = f32[32,3072]{1,0:T(8,128)} async-done(((f32[256,3072]{1,0:T(8,128)}), f32[32,3072]{1,0:T(8,128)}) %reduce-scatter.7.cloned.1.call-update) | async-done | bytes 393232 | tf_op jit(solution)/shard_map/reduce_scatter | solution.py:255
  888.3 89.3 %reduce-scatter.9.cloned.1.call-done = f32[32,4096]{1,0:T(8,128)} async-done(((f32[256,4096]{1,0:T(8,128)}), f32[32,4096]{1,0:T(8,128)}) %reduce-scatter.9.cloned.1.call-update) | async-done | bytes 524304 | tf_op jit(solution)/shard_map/reduce_scatter | solution.py:255
  980.8 149.3 %reduce-scatter.11.cloned.1.call-done = f32[32,8192]{1,0:T(8,128)} async-done(((f32[256,8192]{1,0:T(8,128)}), f32[32,8192]{1,0:T(8,128)}) %reduce-scatter.11.cloned.1.call-update) | async-done | bytes 1048592 | tf_op jit(solution)/shard_map/reduce_scatter | solution.py:255
  1134.2 39.4 %all-reduce.2 = (f32[]{:T(128)}, f32[]{:T(128)}) all-reduce(f32[]{:T(128)} %get-tuple-element.167, f32[]{:T(128)S(6)} %add.312), channel_id=1, replica_groups=mesh['dp'=8,'fsdp'=4] {'dp','fsdp'}, use_global_device_ids=true, to_apply=%region_13.14 | all-reduce | flops 2 | bytes 16 | tf_op jit(solution)/shard_map/psum | solution.py:180
  (280 shorter events, 176.0 us)
Async XLA Ops:
  7.2 82.3 %all-gather.15.cloned.1.call-start = ((), (), s32[]{:S(2)}) async-start(), calls=%async_computation.5 | async-start | bytes 8110080 | tf_op jit(solution)/shard_map/all_gather | solution.py:120
  10.8 158.2 %all-gather.17.cloned.1.call-start = ((), (), s32[]{:S(2)}) async-start(), calls=%async_computation.6 | async-start | bytes 8650752 | tf_op jit(solution)/shard_map/all_gather | solution.py:121
  13.3 79.7 %copy-start.37 = (pred[240]{0:T(512)(128)(4,1)}, pred[240]{0:T(512)(128)(4,1)S(1)}, u32[]{:S(2)}) copy-start(pred[240]{0:T(512)(128)(4,1)S(1)} %iota_compare_fusion.5) | copy-start | bytes 724
  14.0 79.0 %copy-start.28 = (s32[240]{0:T(256)}, s32[240]{0:T(256)S(1)}, u32[]{:S(2)}) copy-start(s32[240]{0:T(256)S(1)} %get-tuple-element.225) | copy-start | bytes 2884
  14.0 79.0 %copy-start.30 = (s32[240]{0:T(256)}, s32[240]{0:T(256)S(1)}, u32[]{:S(2)}) copy-start(s32[240]{0:T(256)S(1)} %get-tuple-element.226) | copy-start | bytes 2884
  14.8 91.1 %copy-start.12 = (f32[240,128]{1,0:T(8,128)}, f32[240,128]{1,0:T(8,128)S(1)}, u32[]{:S(2)}) copy-start(f32[240,128]{1,0:T(8,128)S(1)} %pad_convert_fusion) | copy-start | bytes 368644
  15.7 86.7 %copy-start.47 = (s32[128]{0:T(128)}, s32[128]{0:T(128)S(1)}, u32[]{:S(2)}) copy-start(s32[128]{0:T(128)S(1)} %add_subtract_fusion) | copy-start | bytes 1540
  178.5 15.9 %all-to-all-start = ((bf16[128,3,4,256]{3,0,1,2:T(8,128)(2,1)}), bf16[128,3,4,256]{3,0,1,2:T(8,128)(2,1)}, u32[]{:S(2)}, u32[]{:S(2)}) async-start(bf16[128,3,4,256]{3,0,1,2:T(8,128)(2,1)} %copy.178), calls=%async_computation | async-start | bytes 1572864 | tf_op jit(solution)/shard_map/all_to_all | solution.py:156
  182.8 40.5 %all-gather.19.cloned.1.call-start = ((), (), s32[]{:S(2)}) async-start(), calls=%async_computation.7 | async-start | bytes 1310720 | tf_op jit(solution)/shard_map/all_gather | solution.py:168
  207.8 133.6 %all-gather.21.cloned.1.call-start = ((), (), s32[]{:S(2)}) async-start(), calls=%async_computation.8 | async-start | bytes 17301504 | tf_op jit(solution)/shard_map/all_gather | solution.py:122
  209.9 228.7 %all-gather.23.cloned.1.call-start = ((), (), s32[]{:S(2)}) async-start(), calls=%async_computation.9 | async-start | bytes 1310720 | tf_op jit(solution)/shard_map/all_gather | solution.py:74
  420.8 74.4 %all-gather.25.cloned.1.call-start = ((), (), s32[]{:S(2)}) async-start(), calls=%async_computation.10 | async-start | bytes 3932160 | tf_op jit(solution)/shard_map/all_gather | solution.py:201
  455.9 39.3 %copy-start.50 = (f32[128]{0:T(128)S(1)}, f32[128]{0:T(128)}, u32[]{:S(2)}) copy-start(f32[128]{0:T(128)} %copy-done.49) | copy-start | bytes 1540
  466.5 74.1 %all-gather.41.cloned.1.call-start = ((), (), s32[]{:S(2)}) async-start(), calls=%async_computation.21 | async-start | bytes 1310720 | tf_op jit(solution)/shard_map/all_gather | solution.py:74
  467.3 109.5 %all-reduce.6.cloned.1.call-start = ((), (), s32[]{:S(2)}) async-start(), calls=%async_computation.23 | async-start | bytes 4718592 | tf_op jit(solution)/shard_map/psum | solution.py:222
  518.3 77.4 %all-gather.29.cloned.1.call-start = ((), (), s32[]{:S(2)}) async-start(), calls=%async_computation.12 | async-start | bytes 1310720 | tf_op jit(solution)/shard_map/all_gather | solution.py:74
  519.0 94.9 %all-gather.27.cloned.1.call-start = ((), (), s32[]{:S(2)}) async-start(), calls=%async_computation.11 | async-start | bytes 1310720 | tf_op jit(solution)/shard_map/all_gather | solution.py:74
  519.6 113.3 %all-gather.31.cloned.1.call-start = ((), (), s32[]{:S(2)}) async-start(), calls=%async_computation.14 | async-start | bytes 1310720 | tf_op jit(solution)/shard_map/all_gather | solution.py:74
  520.4 131.3 %all-gather.37.cloned.1.call-start = ((), (), s32[]{:S(2)}) async-start(), calls=%async_computation.18 | async-start | bytes 1310720 | tf_op jit(solution)/shard_map/all_gather | solution.py:74
  520.9 167.4 %all-gather.39.cloned.1.call-start = ((), (), s32[]{:S(2)}) async-start(), calls=%async_computation.19 | async-start | bytes 5242880 | tf_op jit(solution)/shard_map/all_gather | solution.py:74
  521.7 185.4 %all-gather.33.cloned.1.call-start = ((), (), s32[]{:S(2)}) async-start(), calls=%async_computation.16 | async-start | bytes 1310720 | tf_op jit(solution)/shard_map/all_gather | solution.py:74
  522.3 221.3 %all-gather.35.cloned.1.call-start = ((), (), s32[]{:S(2)}) async-start(), calls=%async_computation.17 | async-start | bytes 5242880 | tf_op jit(solution)/shard_map/all_gather | solution.py:74
  522.9 286.4 %reduce-scatter.13.cloned.1.call-start = ((), (), s32[]{:S(2)}) async-start(), calls=%async_computation.22 | async-start | bytes 884736 | tf_op jit(solution)/shard_map/reduce_scatter | solution.py:255
  599.2 287.4 %reduce-scatter.7.cloned.1.call-start = ((), (), s32[]{:S(2)}) async-start(), calls=%async_computation.13 | async-start | bytes 3538944 | tf_op jit(solution)/shard_map/reduce_scatter | solution.py:255
  618.9 358.7 %reduce-scatter.9.cloned.1.call-start = ((), (), s32[]{:S(2)}) async-start(), calls=%async_computation.15 | async-start | bytes 4718592 | tf_op jit(solution)/shard_map/reduce_scatter | solution.py:255
  640.6 489.4 %reduce-scatter.11.cloned.1.call-start = ((), (), s32[]{:S(2)}) async-start(), calls=%async_computation.20 | async-start | bytes 9437184 | tf_op jit(solution)/shard_map/reduce_scatter | solution.py:255
  757.9 419.8 %copy-start.23 = (f32[32,9]{0,1:T(8,128)S(1)}, f32[32,9]{0,1:T(8,128)}, u32[]{:S(2)}) copy-start(f32[32,9]{0,1:T(8,128)} %param.35) | copy-start | bytes 3460
  757.9 421.2 %copy-start.14 = (f32[32,3072]{1,0:T(8,128)S(1)}, f32[32,3072]{1,0:T(8,128)}, u32[]{:S(2)}) copy-start(f32[32,3072]{1,0:T(8,128)} %param.31) | copy-start | bytes 1179652
  757.9 423.7 %copy-start.8 = (f32[32,4096]{1,0:T(8,128)S(1)}, f32[32,4096]{1,0:T(8,128)}, u32[]{:S(2)}) copy-start(f32[32,4096]{1,0:T(8,128)} %param.32) | copy-start | bytes 1572868
  977.6 204.0 %copy-start.9 = (f32[32,4096]{1,0:T(8,128)S(1)}, f32[32,4096]{1,0:T(8,128)}, u32[]{:S(2)}) copy-start(f32[32,4096]{1,0:T(8,128)} %reduce-scatter.9.cloned.1.call-done) | copy-start | bytes 1572868
  1132.1 52.2 %copy-start.4 = (f32[32,8192]{1,0:T(8,128)S(1)}, f32[32,8192]{1,0:T(8,128)}, u32[]{:S(2)}) copy-start(f32[32,8192]{1,0:T(8,128)} %param.33) | copy-start | bytes 3145732
  1132.1 52.2 %copy-start.5 = (f32[32,8192]{1,0:T(8,128)S(1)}, f32[32,8192]{1,0:T(8,128)}, u32[]{:S(2)}) copy-start(f32[32,8192]{1,0:T(8,128)} %reduce-scatter.11.cloned.1.call-done) | copy-start | bytes 3145732
  (45 other events, 277.1 us)
Sparse Core Ops, SparseCore 0:
  11.5 77.9 all-gather.14
  92.9 76.0 all-gather.16
  207.9 15.2 all-gather.18
  226.5 114.8 all-gather.20
  420.9 17.6 all-gather.22
  466.6 28.5 all-gather.24
  497.3 16.7 all-gather.40
  518.4 58.2 all-reduce.5
  578.9 16.7 all-gather.28
  597.1 16.8 all-gather.26
  616.1 16.7 all-gather.30
  634.9 16.7 all-gather.36
  653.8 34.4 all-gather.38
  690.3 16.7 all-gather.32
  709.1 34.4 all-gather.34
  746.7 62.4 reduce-scatter.12
  813.1 73.4 reduce-scatter.6
  890.6 87.0 reduce-scatter.8
  981.2 148.7 reduce-scatter.10

commit v2 on v1

--- a/solution.py
+++ b/solution.py
@@ -1,6 +1,10 @@
+import functools
+
 import jax
 import jax.numpy as jnp
 from jax import lax
+from jax.experimental import pallas as pl
+from jax.experimental.pallas import tpu as pltpu
 from jax.sharding import PartitionSpec as P
 
 D = 1024
@@ -23,6 +27,13 @@
 f32 = jnp.float32
 bf16 = jnp.bfloat16
 highest = lax.Precision.HIGHEST
+MESH = pl.DeviceIdType.MESH
+STRIP = 32
+CHUNK = 512
+DEPTH = 2
+LAG = 2
+QUEUE = 2
+MISC = 1024
 
 
 def dot(left, right, dims):
@@ -70,11 +81,397 @@
     return (fresh, fresh.astype(bf16), moment, second)
 
 
+PIECES = (
+    (0, 0, 1920, "yzx"), (2, 0, 2688, "zxy"), (0, 1920, 1920, "yzx"), (2, 2688, 2816, "zxy"),
+    (1, 0, 1920, "yzx"), (2, 5504, 2688, "zxy"), (1, 1920, 2176, "zxy"),
+)
+
+
+def gather_kernel(*refs):
+    shards, num_ref, wholes, stat_ref = refs[0:3], refs[3], refs[4:7], refs[7]
+    quad_buf, line_buf, own_sem, s_send, s_recv, sends, arrive, pass_on = refs[8:]
+    dp, own = lax.axis_index("dp"), lax.axis_index("fsdp")
+    z, y, x, core = dp // 2, dp % 2, own // 2, own % 2
+    sibling = x * 2 + 1 - core
+    barrier = pltpu.get_barrier_semaphore()
+    for d in range(1, 8):
+        pl.semaphore_signal(barrier, inc=1, device_id=(lax.rem(dp + d, 8), own), device_id_type=MESH)
+    for d in range(1, 4):
+        pl.semaphore_signal(barrier, inc=1, device_id=(dp, lax.rem(own + d, 4)), device_id_type=MESH)
+    pl.semaphore_wait(barrier, 10)
+
+    def view(p, ident, plane):
+        a, start, width, order = PIECES[p]
+        row = pl.multiple_of(((ident // 2) * 4 + (ident % 2) * 2 + plane) * STRIP, STRIP)
+        return wholes[a].at[pl.ds(row, STRIP), pl.ds(start, width)]
+
+    def copy(p, ident, slot, to, mine=False):
+        a, start, width, order = PIECES[p]
+        src = shards[a].at[:, pl.ds(start, width)] if mine else view(p, ident, core)
+        sem = pass_on if slot == 4 else arrive
+        return pltpu.make_async_remote_copy(
+            src_ref=src, dst_ref=view(p, ident, core), send_sem=sends.at[p, ident, slot], recv_sem=sem.at[p, ident],
+            device_id=to, device_id_type=MESH,
+        )
+
+    def arrival(p, ident, plane, sem):
+        return pltpu.make_async_copy(view(p, ident, plane), view(p, ident, plane), sem.at[p, ident])
+
+    def targets(p, rx, ry, rz):
+        order = PIECES[p][3]
+        moved = {"x": rx != 0, "y": ry != 0, "z": rz is not None}
+        stage = max([k for k in range(3) if moved[order[k]]], default=-1)
+        found = []
+        if stage >= 0 and order[stage] == "z":
+            found.append((0, (rz < 0) & (z < 3), ((dp + 2) % 8, own)))
+            found.append((1, (rz > 0) & (z > 0), ((dp + 6) % 8, own)))
+        for k in range(stage + 1, 3):
+            if order[k] == "z":
+                found.append((0, z < 3, ((dp + 2) % 8, own)))
+                found.append((1, z > 0, ((dp + 6) % 8, own)))
+            elif order[k] == "x":
+                found.append((2, None, (dp, (1 - x) * 2 + core)))
+            else:
+                found.append((3, None, (z * 2 + 1 - y, own)))
+        found.append((4, None, (dp, sibling)))
+        return found
+
+    def source(rx, ry, rz):
+        sz = z if rz is None else z + rz
+        sy = 1 - y if ry else y
+        sx = 1 - x if rx else x
+        return sz, (sz * 2 + sy) * 2 + sx
+
+    def each(rx, ry, rz, act, mine=False):
+        sz, ident = source(rx, ry, rz)
+
+        def body():
+            for p in range(len(PIECES)):
+                if act == "send" and not mine:
+                    arrival(p, ident, core, arrive).wait()
+                for slot, when, to in targets(p, rx, ry, rz):
+                    def go(slot=slot, to=to):
+                        c = copy(p, ident, slot, to, mine)
+                        c.start() if act == "send" else c.wait_send()
+
+                    if when is None:
+                        go()
+                    else:
+                        pl.when(when)(go)
+
+        if rz is None:
+            body()
+        else:
+            pl.when((sz >= 0) & (sz < 4))(body)
+
+    def over_z(pairs, act):
+        def step(t, carry):
+            rz = ((t + 1) // 2) * (1 - 2 * (t % 2))
+            for rx, ry in pairs:
+                each(rx, ry, rz, act)
+            return carry
+
+        lax.fori_loop(1, 7, step, 0)
+
+    def sweep(act):
+        each(0, 0, None, act, mine=True)
+        if act == "send":
+            for a in range(3):
+                row = pl.multiple_of((dp * 4 + own) * STRIP, STRIP)
+                pltpu.make_async_copy(shards[a], wholes[a].at[pl.ds(row, STRIP), :], own_sem.at[a]).start()
+            scalars()
+        each(1, 0, None, act)
+        each(0, 1, None, act)
+        over_z([(0, 0)], act)
+        each(1, 1, None, act)
+        over_z([(1, 0), (0, 1)], act)
+        over_z([(1, 1)], act)
+
+    def share(buf, k, where, at):
+        return pltpu.make_async_remote_copy(
+            src_ref=buf.at[at], dst_ref=buf.at[at], send_sem=s_send.at[k], recv_sem=s_recv.at[k],
+            device_id=where, device_id_type=MESH,
+        )
+
+    def scalars():
+        quad_buf[own] = num_ref[...]
+        for d in range(1, 4):
+            share(quad_buf, d, (dp, lax.rem(own + d, 4)), own).start()
+
+    sweep("send")
+    for d in range(1, 4):
+        share(quad_buf, d, (dp, own), lax.rem(own + 4 - d, 4)).wait_recv()
+    line_buf[dp] = (quad_buf[0] + quad_buf[1]) + (quad_buf[2] + quad_buf[3])
+    for d in range(1, 8):
+        share(line_buf, 3 + d, (lax.rem(dp + d, 8), own), dp).start()
+
+    def closing(ident, carry):
+        for p in range(len(PIECES)):
+            arrival(p, ident, 1 - core, pass_on).wait()
+        return carry
+
+    lax.fori_loop(0, 16, closing, 0)
+    for a in range(3):
+        row = pl.multiple_of((dp * 4 + own) * STRIP, STRIP)
+        pltpu.make_async_copy(shards[a], wholes[a].at[pl.ds(row, STRIP), :], own_sem.at[a]).wait()
+    sweep("drain")
+    for d in range(1, 8):
+        share(line_buf, 3 + d, (dp, own), lax.rem(dp + 8 - d, 8)).wait_recv()
+    stat = line_buf[0]
+    for d in range(1, 8):
+        stat = stat + line_buf[d]
+    stat_ref[...] = stat
+    for d in range(1, 4):
+        share(quad_buf, d, (dp, own), own).wait_send()
+    for d in range(1, 8):
+        share(line_buf, 3 + d, (dp, own), dp).wait_send()
+
+
+def gather_weights(head, attn, mlp, number):
+    any_space = pl.BlockSpec(memory_space=pl.ANY)
+    vmem = pl.BlockSpec(memory_space=pltpu.VMEM)
+    n = len(PIECES)
+    return pl.pallas_call(
+        gather_kernel,
+        out_shape=[jax.ShapeDtypeStruct((D, a.shape[1]), bf16) for a in (head, attn, mlp)]
+        + [jax.ShapeDtypeStruct((8, 128), f32)],
+        in_specs=[any_space] * 3 + [vmem],
+        out_specs=[any_space] * 3 + [vmem],
+        scratch_shapes=[
+            pltpu.VMEM((4, 8, 128), f32),
+            pltpu.VMEM((8, 8, 128), f32),
+            pltpu.SemaphoreType.DMA((3,)),
+            pltpu.SemaphoreType.DMA((11,)),
+            pltpu.SemaphoreType.DMA((11,)),
+            pltpu.SemaphoreType.DMA((n, 16, 5)),
+            pltpu.SemaphoreType.DMA((n, 16)),
+            pltpu.SemaphoreType.DMA((n, 16)),
+        ],
+        compiler_params=pltpu.CompilerParams(collective_id=0, has_side_effects=True),
+        name="gather_weights",
+    )(head, attn, mlp, number)
+
+
+def reduce_kernel(widths, outs_at, *refs):
+    n_in = len(widths)
+    keep, give = refs[:n_in], refs[n_in : 2 * n_in]
+    num_ref = refs[2 * n_in]
+    outs = refs[2 * n_in + 1 : 2 * n_in + 1 + len(outs_at)]
+    stat_ref = refs[2 * n_in + 1 + len(outs_at)]
+    (own_buf, give_buf, got, rise, fall, done, tally, quad_buf, line_buf,
+     own_sem, give_sem, y_send, y_recv, z_send, z_recv, s_send, s_recv) = refs[2 * n_in + 2 + len(outs_at) :]
+    dp, own = lax.axis_index("dp"), lax.axis_index("fsdp")
+    z, y = dp // 2, dp % 2
+    over = z * 2 + 1 - y
+    barrier = pltpu.get_barrier_semaphore()
+    for d in range(1, 8):
+        pl.semaphore_signal(barrier, inc=1, device_id=(lax.rem(dp + d, 8), own), device_id_type=MESH)
+    for d in range(1, 4):
+        pl.semaphore_signal(barrier, inc=1, device_id=(dp, lax.rem(own + d, 4)), device_id_type=MESH)
+    pl.semaphore_wait(barrier, 10)
+    places = [(i, j) for i in range(n_in) for j in range(widths[i] // CHUNK)]
+    n = len(places)
+
+    def load(c):
+        i, j = places[c]
+        return pltpu.make_async_copy(keep[i].at[:, pl.ds(j * CHUNK, CHUNK)], own_buf.at[c], own_sem.at[c])
+
+    def stage(c):
+        i, j = places[c]
+        return pltpu.make_async_copy(give[i].at[:, pl.ds(j * CHUNK, CHUNK)], give_buf.at[c], give_sem.at[c])
+
+    def cross(c):
+        return pltpu.make_async_remote_copy(
+            src_ref=give_buf.at[c], dst_ref=got.at[c], send_sem=y_send.at[c],
+            recv_sem=y_recv.at[c], device_id=(over, own), device_id_type=MESH,
+        )
+
+    for c in range(n):
+        stage(c).start()
+    for c in range(n):
+        load(c).start()
+    for c in range(DEPTH):
+        stage(c).wait()
+        cross(c).start()
+    for c in range(DEPTH, n):
+        stage(c).wait()
+    tally[...] = jnp.zeros_like(tally)
+
+    def hop(buf, way, c, b, to):
+        return pltpu.make_async_remote_copy(
+            src_ref=buf.at[c, b], dst_ref=buf.at[c, b], send_sem=z_send.at[way, c, b], recv_sem=z_recv.at[way, c, b],
+            device_id=(to * 2 + y, own), device_id_type=MESH,
+        )
+
+    def here(c, b):
+        at = pl.ds(b * STRIP, STRIP)
+        return own_buf[c, at, :] + got[c, at, :].astype(f32)
+
+    early, late = LAG * jnp.minimum(z, 3 - z), LAG * jnp.maximum(z, 3 - z)
+
+    def step(t, carry):
+        first = t - early
+
+        @pl.when((first >= 0) & (first < n))
+        def _():
+            pltpu.make_async_copy(own_buf.at[first], own_buf.at[first], own_sem.at[first]).wait()
+            cross(first).wait()
+
+            @pl.when(first + DEPTH < n)
+            def _():
+                cross(first + DEPTH).start()
+
+        for way, buf, lag, to, back in ((0, rise, LAG * z, z + 1, z - 1), (1, fall, LAG * (3 - z), z - 1, z + 1)):
+            c = t - lag
+
+            @pl.when((c >= 0) & (c < n))
+            def _():
+                for b in range(4):
+                    beyond = (b > z) if way == 0 else (b < z)
+
+                    @pl.when(beyond & (lag == 0))
+                    def _():
+                        buf[c, b] = here(c, b)
+
+                    @pl.when(beyond & (lag > 0))
+                    def _():
+                        hop(buf, way, c, b, back).wait_recv()
+                        buf[c, b] = buf[c, b] + here(c, b)
+
+                    @pl.when(beyond & (c >= QUEUE))
+                    def _():
+                        hop(buf, way, c - QUEUE, b, to).wait_send()
+
+                    @pl.when(beyond)
+                    def _():
+                        hop(buf, way, c, b, to).start()
+
+        last = t - late
+
+        @pl.when((last >= 0) & (last < n))
+        def _():
+            at = pl.ds(pl.multiple_of(z * STRIP, STRIP), STRIP)
+            done[last] = own_buf[last, at, :] + got[last, at, :].astype(f32)
+
+            @pl.when(z > 0)
+            def _():
+                hop(rise, 0, last, z, z - 1).wait_recv()
+                done[last] = done[last] + rise[last, z]
+
+            @pl.when(z < 3)
+            def _():
+                hop(fall, 1, last, z, z + 1).wait_recv()
+                done[last] = done[last] + fall[last, z]
+
+            value = done[last]
+            square = value * value
+            total = square[0:8, 0:128]
+            for r in range(0, STRIP, 8):
+                for k in range(0, CHUNK, 128):
+                    if r or k:
+                        total = total + square[r : r + 8, k : k + 128]
+            tally[...] = tally[...] + total
+
+        return carry
+
+    lax.fori_loop(0, n + 3 * LAG, step, 0)
+    summed = jnp.sum(tally[...])
+    lane = lax.broadcasted_iota(jnp.int32, (8, 128), 1)
+    mine = jnp.where(lane == 0, summed, jnp.where(lane == 1, num_ref[...], 0.0))
+    quad_buf[own] = mine
+
+    def share(buf, k, where, at):
+        return pltpu.make_async_remote_copy(
+            src_ref=buf.at[at], dst_ref=buf.at[at], send_sem=s_send.at[k], recv_sem=s_recv.at[k],
+            device_id=where, device_id_type=MESH,
+        )
+
+    for d in range(1, 4):
+        share(quad_buf, d, (dp, lax.rem(own + d, 4)), own).start()
+    for (i, j), c in zip(places, range(n)):
+        target, base = outs_at_of(outs_at, i)
+        outs[target][:, base + j * CHUNK : base + (j + 1) * CHUNK] = done[c]
+    for d in range(1, 4):
+        share(quad_buf, d, (dp, own), lax.rem(own + 4 - d, 4)).wait_recv()
+    line_buf[dp] = (quad_buf[0] + quad_buf[1]) + (quad_buf[2] + quad_buf[3])
+    for d in range(1, 8):
+        share(line_buf, 3 + d, (lax.rem(dp + d, 8), own), dp).start()
+    for d in range(1, 8):
+        share(line_buf, 3 + d, (dp, own), lax.rem(dp + 8 - d, 8)).wait_recv()
+    stat = line_buf[0]
+    for d in range(1, 8):
+        stat = stat + line_buf[d]
+    stat_ref[...] = stat
+    for d in range(1, 4):
+        share(quad_buf, d, (dp, own), own).wait_send()
+    for d in range(1, 8):
+        share(line_buf, 3 + d, (dp, own), dp).wait_send()
+
+    def drain(c, carry):
+        for b in range(4):
+            @pl.when(b > z)
+            def _():
+                hop(rise, 0, c, b, z + 1).wait_send()
+
+            @pl.when(b < z)
+            def _():
+                hop(fall, 1, c, b, z - 1).wait_send()
+        return carry
+
+    lax.fori_loop(n - QUEUE, n, drain, 0)
+
+
+def outs_at_of(outs_at, i):
+    for target, members in enumerate(outs_at):
+        for index, base in members:
+            if index == i:
+                return target, base
+
+
+def reduce_blocks(keep, give, numerator, outs_at, out_widths):
+    widths = [a.shape[1] for a in keep]
+    n = sum(widths) // CHUNK
+    any_space = pl.BlockSpec(memory_space=pl.ANY)
+    vmem = pl.BlockSpec(memory_space=pltpu.VMEM)
+    half = 4 * STRIP
+    return pl.pallas_call(
+        functools.partial(reduce_kernel, tuple(widths), outs_at),
+        out_shape=[jax.ShapeDtypeStruct((STRIP, w), f32) for w in out_widths] + [jax.ShapeDtypeStruct((8, 128), f32)],
+        in_specs=[any_space] * (2 * len(keep)) + [vmem],
+        out_specs=[vmem] * (len(out_widths) + 1),
+        scratch_shapes=[
+            pltpu.VMEM((n, half, CHUNK), f32),
+            pltpu.VMEM((n, half, CHUNK), bf16),
+            pltpu.VMEM((n, half, CHUNK), bf16),
+            pltpu.VMEM((n, 4, STRIP, CHUNK), f32),
+            pltpu.VMEM((n, 4, STRIP, CHUNK), f32),
+            pltpu.VMEM((n, STRIP, CHUNK), f32),
+            pltpu.VMEM((8, 128), f32),
+            pltpu.VMEM((4, 8, 128), f32),
+            pltpu.VMEM((8, 8, 128), f32),
+            pltpu.SemaphoreType.DMA((n,)),
+            pltpu.SemaphoreType.DMA((n,)),
+            pltpu.SemaphoreType.DMA((n,)),
+            pltpu.SemaphoreType.DMA((n,)),
+            pltpu.SemaphoreType.DMA((2, n, 4)),
+            pltpu.SemaphoreType.DMA((2, n, 4)),
+            pltpu.SemaphoreType.DMA((11,)),
+            pltpu.SemaphoreType.DMA((11,)),
+        ],
+        compiler_params=pltpu.CompilerParams(
+            collective_id=1, has_side_effects=True, vmem_limit_bytes=52 * 2**20
+        ),
+        name="reduce_blocks",
+    )(*keep, *give, numerator)
+
+
 def ag(part):
     return lax.all_gather(part, "fsdp", axis=0, tiled=True)
 
 
 def make_local(n_dp, n_f):
+    fast = n_dp == 8 and n_f == 4
+
     def local(
         pixels, targets, valid_mask, lat_weight, segment_ids, present_vars, lead_index, step_count,
         w_agg, w_attn, w_mlp, w_io, w_small,
@@ -106,7 +503,7 @@
         expand = jnp.where(in_pixels, spread, embed_col).astype(bf16)
         present_cols = jnp.repeat(present.astype(f32), PIX)
         pixel_weight = lat_weight[0][:, None] * valid_mask[0].astype(f32) * present_cols[None, :]
-        total = lax.psum(jnp.sum(pixel_weight), ("dp", "fsdp"))
+        weight_sum = jnp.sum(pixel_weight)
 
         pack = jnp.concatenate(
             [
@@ -117,9 +514,16 @@
             ],
             axis=1,
         )
-        head = lax.all_gather(pack, ("dp", "fsdp"), axis=0, tiled=True)
-        attn = lax.all_gather(w_attn.astype(bf16), ("dp", "fsdp"), axis=0, tiled=True)
-        mlp = lax.all_gather(w_mlp.astype(bf16), ("dp", "fsdp"), axis=0, tiled=True)
+        if fast:
+            head, attn, mlp, stat = gather_weights(
+                pack, w_attn.astype(bf16), w_mlp.astype(bf16), jnp.full((8, 128), weight_sum, f32)
+            )
+            total = stat[0, 0]
+        else:
+            head = lax.all_gather(pack, ("dp", "fsdp"), axis=0, tiled=True)
+            attn = lax.all_gather(w_attn.astype(bf16), ("dp", "fsdp"), axis=0, tiled=True)
+            mlp = lax.all_gather(w_mlp.astype(bf16), ("dp", "fsdp"), axis=0, tiled=True)
+            total = lax.psum(weight_sum, ("dp", "fsdp"))
         w240 = jnp.concatenate([head[:, :WIDTH], head[:, 2 * WIDTH : 2 * WIDTH + VARS]], axis=1)
         w_pred = head[:, WIDTH : 2 * WIDTH]
         w_pos = head[:, 2 * WIDTH + VARS : USED]
@@ -177,7 +581,7 @@
         predicted = mm(norm2, w_pred) * D ** (-0.5)
         error = predicted - target
         weighted = pixel_weight * error
-        numerator = lax.psum(jnp.sum(weighted * error), ("dp", "fsdp"))
+        numerator = jnp.sum(weighted * error)
 
         d_pred = (weighted * (2.0 * D ** (-0.5) / total)).astype(bf16)
         d_norm2 = mm_t(d_pred, w_pred)
@@ -221,42 +625,74 @@
         )
         d_table, narrow = lax.psum((jnp.concatenate([d_table_k, d_table_v], axis=1), narrow), "fsdp")
 
-        def mine(array):
-            whole = array.reshape(n_dp, n_f, strip, array.shape[1])
-            return lax.dynamic_index_in_dim(whole, own, axis=1, keepdims=False).reshape(n_dp * strip, array.shape[1])
-
         source = jnp.arange(D)
         pick = (source // strip) % n_f == own
-        place = (source // (strip * n_f)) * strip + source % strip
+        if fast:
+            line, side = source // 256, (source // 128) % 2
+            here = lax.axis_index("dp") % 2
+            place = jnp.where(side == here, 0, 4 * strip) + line * strip + source % strip
+        else:
+            place = (source // (strip * n_f)) * strip + source % strip
         choose = (pick[:, None] & (place[:, None] == jnp.arange(n_dp * strip)[None, :])).astype(bf16)
 
+        def mine(array):
+            width = array.shape[1]
+            if not fast:
+                whole = array.reshape(n_dp, n_f, strip, width)
+                return (lax.dynamic_index_in_dim(whole, own, 1, False).reshape(n_dp * strip, width),)
+            whole = array.reshape(4, 2 * n_f, strip, width)
+            return tuple(
+                lax.dynamic_index_in_dim(whole, at * n_f + own, 1, False).reshape(4 * strip, width)
+                for at in (here, 1 - here)
+            )
+
+        def split(picked):
+            if not fast:
+                return (picked,)
+            return picked[:, : 4 * strip], picked[:, 4 * strip :]
+
         def weight_grad(features, grads):
-            return t_mm(mm(features, choose).astype(bf16), grads)
+            return tuple(t_mm(part, grads) for part in split(mm(features, choose).astype(bf16)))
 
         d_agg_all = ag(d_agg)
-        g_attn = jnp.concatenate(
-            [weight_grad(ag(norm0), d_qkv_all), weight_grad(mixed_all, d_proj_all)], axis=1
-        )
-        g_mlp = jnp.concatenate(
-            [weight_grad(ag(norm1), ag(d_up)), weight_grad(ag(d_out), ag(lifted))], axis=1
-        )
+        g_qkv = weight_grad(ag(norm0), d_qkv_all)
+        g_proj = weight_grad(mixed_all, d_proj_all)
+        g_up = weight_grad(ag(norm1), ag(d_up))
+        g_down = weight_grad(ag(d_out), ag(lifted))
         g_out = weight_grad(ag(mixed_a), d_agg_all)
-        g_kv = exact("dc,cx->dx", mine(w240).astype(f32), d_table)
-        g_240 = exact("dx,cx->dc", mine(agg_kv).astype(f32), d_table)
+        g_kv = tuple(exact("dc,cx->dx", part.astype(f32), d_table) for part in mine(w240))
+        g_240 = tuple(exact("dx,cx->dc", part.astype(f32), d_table) for part in mine(agg_kv))
         g_pred = weight_grad(ag(norm2), ag(d_pred))
         g_pos = weight_grad(d_agg_all, ag(onehot))
-        g_small = mine(narrow.T)[:, :9]
-        g_agg = jnp.concatenate([g_kv, g_out], axis=1)
-        g_misc = jnp.concatenate(
-            [g_240[:, :WIDTH], g_pred, g_240[:, WIDTH:], g_pos, g_small, jnp.zeros((n_dp * strip, 768 - USED - 9), f32)],
-            axis=1,
+        g_small = mine(narrow.T)
+        g_misc = tuple(
+            jnp.concatenate(
+                [a[:, :WIDTH], b, a[:, WIDTH:], c, d[:, :9], jnp.zeros((a.shape[0], MISC - USED - 9), f32)], axis=1
+            )
+            for a, b, c, d in zip(g_240, g_pred, g_pos, g_small)
         )
-        r_agg, r_attn, r_mlp, r_misc = (
-            lax.psum_scatter(g, "dp", scatter_dimension=0, tiled=True) for g in (g_agg, g_attn, g_mlp, g_misc)
-        )
+        groups = (g_kv, g_out, g_qkv, g_proj, g_up, g_down, g_misc)
+        if fast:
+            lane = lax.broadcasted_iota(jnp.int32, (8, 128), 1)
+            r_agg, r_attn, r_mlp, r_misc, stat = reduce_blocks(
+                [g[0] for g in groups],
+                [g[1].astype(bf16) for g in groups],
+                jnp.where(lane == 1, numerator, 0.0),
+                (((0, 0), (1, 2 * D)), ((2, 0), (3, 3 * D)), ((4, 0), (5, FF)), ((6, 0),)),
+                (3 * D, 4 * D, 2 * FF, MISC),
+            )
+            squares, numerator = stat[0, 0], stat[0, 1]
+        else:
+            r_kv, r_out, r_qkv, r_proj, r_up, r_down, r_misc = (
+                lax.psum_scatter(g[0], "dp", scatter_dimension=0, tiled=True) for g in groups
+            )
+            r_agg = jnp.concatenate([r_kv, r_out], axis=1)
+            r_attn = jnp.concatenate([r_qkv, r_proj], axis=1)
+            r_mlp = jnp.concatenate([r_up, r_down], axis=1)
+            local_squares = sum(jnp.sum(piece * piece) for piece in (r_agg, r_attn, r_mlp, r_misc))
+            squares, numerator = lax.psum((local_squares, numerator), ("dp", "fsdp"))
         r_io = jnp.concatenate([r_misc[:, :USED], jnp.zeros((strip, w_io.shape[1] - USED), f32)], axis=1)
         reduced = (r_agg, r_attn, r_mlp, r_io, r_misc[:, USED : USED + 9])
-        squares = lax.psum(sum(jnp.sum(piece * piece) for piece in reduced), ("dp", "fsdp"))
         grad_norm = jnp.sqrt(squares)
         factor = jnp.minimum(1.0, clip_limit / grad_norm)
         loss = numerator / total

time: 1200 us -> 781 us (0.65)
  waiting for transfers between devices: 841 us -> 179 us
  Pallas kernels: 0 us -> 309 us
  blocking collectives: 93.6 us -> 12.8 us
  other arithmetic: 58.3 us -> 38.9 us
  matrix products: 137 us -> 154 us
  local copies, waits for them, and re-layouts: 35.5 us -> 49.5 us
    reduce_scatter x4 -> x0, waiting for transfers between devices: 363 us -> none  [local(): lax.psum_scatter(g, 'dp', scatter_dimension=0, tiled=True)]
    pallas_call x0 -> x2, Pallas kernels: none -> 309 us  [the longest x1 166 us: reduce_blocks(): pl.pallas_call(functools.partial(reduce_kernel, tuple(widths), outs_at),...]
    all_gather x3 -> x0, waiting for transfers between devices: 244 us -> none  [the longest x1 114 us: local(): mlp = lax.all_gather(w_mlp.astype(bf16), ('dp', 'fsdp'), axis=0, tiled=True)]
    psum x2 -> x0, blocking collectives: 78.3 us -> none  [the longest x1 39.4 us: local(): numerator = lax.psum(jnp.sum(weighted * error), ('dp', 'fsdp'))]
    all_gather x9, waiting for transfers between devices: 146 us -> 72.6 us  [ag(): return lax.all_gather(part, 'fsdp', axis=0, tiled=True)]
    psum x1, waiting for transfers between devices: 34.1 us -> 50.7 us  [local(): lax.psum((jnp.concatenate([d_table_k, d_table_v], axis=1), narrow), 'fsdp')]
    dot_general x21 -> x35, matrix products: 87.7 us -> 102 us  [dot(): lax.dot_general(left, right, (dims, ((), ())), preferred_element_type=f32)]
    concatenate x3 -> x0, other arithmetic: 13 us -> none  [the longest x1 7.59 us: local(): jnp.concatenate([weight_grad(ag(norm1), ag(d_up)), weight_grad(ag(d_out),...]
  transfers between devices with their start and end apart: 20 -> 13, of which waited for: 19 -> 9; matrix products, arithmetic and copies ran while one was open for 10% -> 16% of each run, Pallas kernels for 0% -> 0%
where the time goes in v2:
time: 781 us; the launch traced here: 771 us
  Pallas kernels  309 us (40%)
  waiting for transfers between devices  179 us (23%)
  matrix products  154 us (20%)
  local copies, waits for them, and re-layouts  49.5 us (6%)
  other arithmetic  38.9 us (5%)
  between operations  22.2 us (3%)
  blocking collectives  12.8 us (2%)
    pallas_call x1, Pallas kernels, reduce_blocks(): pl.pallas_call(functools.partial(reduce_kernel, tuple(widths), outs_at),...  166 us
    pallas_call x1, Pallas kernels, gather_weights(): pl.pallas_call(gather_kernel, out_shape=[jax.ShapeDtypeStruct((D, a.shape...  143 us
    dot_general x35, matrix products, dot(): lax.dot_general(left, right, (dims, ((), ())), preferred_element_type=f32)  102 us
    all_gather x9, waiting for transfers between devices, ag(): return lax.all_gather(part, 'fsdp', axis=0, tiled=True)  72.6 us
    psum x1, waiting for transfers between devices, local(): lax.psum((jnp.concatenate([d_table_k, d_table_v], axis=1), narrow), 'fsdp')  50.7 us
    all_gather x1, waiting for transfers between devices, local(): lax.all_gather(d_part, 'fsdp', axis=2, tiled=True).reshape(row_len, 3 * D)  28.1 us
    dot_general x9, matrix products, exact(): jnp.einsum(eq, left, right, precision=highest, preferred_element_type=f32)  16.5 us
  transfers between devices with their start and end apart: 13, of which 9 were waited for; matrix products, arithmetic and copies ran while one was open for 16% of the time, Pallas kernels for 0%

profile of v2, /device:TPU:0, one launch (start us, length us, event | category | flops | bytes accessed | tf_op | source)
XLA Modules:
  0.0 770.6 jit_solution(15953729521080136327)
XLA Ops:
  18.3 143.4 %gather_weights.1 = (bf16[1024,3840]{1,0:T(8,128)(2,1)}, bf16[1024,4096]{1,0:T(8,128)(2,1)}, bf16[1024,8192]{1,0:T(8,128)(2,1)}, f32[8,128]{1,0:T(8,128)}) custom-call(bf16[32,3840]{1,0:T(8,128)(2,1)} %concatenate.30.refs_0_, bf16[32,4096]{1,0:T(8,128)(2,1)} %convert_element_type.203.refs_1_, bf16[32,8192]{1,0:T(8,128)(2,1)} %convert_element_type.204.refs_2_, ...), custom_call_target="tpu_custom_call" | custom-call | tf_op jit(solution)/shard_map/gather_weights/pallas_call | solution.py:234
  168.3 3.6 fusion.202
  187.8 4.8 fusion.23
  197.5 4.2 all-to-all-start
  202.7 10.7 %all-to-all-done = bf16[128,3,4,256]{3,0,1,2:T(8,128)(2,1)} async-done(((bf16[128,3,4,256]{3,0,1,2:T(8,128)(2,1)}), bf16[128,3,4,256]{3,0,1,2:T(8,128)(2,1)}, u32[]{:S(2)}, u32[]{:S(2)}) %all-to-all-start) | async-done | bytes 786464 | tf_op jit(solution)/shard_map/all_to_all | solution.py:560
  218.0 5.4 fusion.221
  223.4 3.4 convolution_convert_fusion.15
  228.8 13.4 %all-gather.12.cloned.1.call-done = bf16[512,1024]{0,1:T(8,128)(2,1)} async-done(((bf16[512,256]{0,1:T(8,128)(2,1)}), bf16[512,1024]{0,1:T(8,128)(2,1)}) %all-gather.12.cloned.1.call-update) | async-done | bytes 1048592 | tf_op jit(solution)/shard_map/all_gather | solution.py:572
  246.1 6.7 multiply_convert_fusion.1
  252.8 6.7 fusion.223
  268.3 7.0 fusion.19
  275.3 7.5 multiply_reduce_fusion.4
  285.9 3.1 slice.179
  289.5 11.3 %all-gather.14.cloned.1.call-done = bf16[512,1024]{1,0:T(8,128)(2,1)} async-done(((bf16[128,1024]{1,0:T(8,128)(2,1)}), bf16[512,1024]{1,0:T(8,128)(2,1)}) %all-gather.14.cloned.1.call-update) | async-done | bytes 1048592 | tf_op jit(solution)/shard_map/all_gather | solution.py:469
  303.4 3.6 fusion.129
  307.0 8.5 %fusion.73 = bf16[4,64,512]{2,1,0:T(8,128)(2,1)} fusion(f32[4,512,512]{1,2,0:T(8,128)} %fusion.129, bf16[512,3,4,64]{0,3,2,1:T(8,128)(2,1)} %reshape.464, f32[4,512,512]{1,2,0:T(8,128)} %get-tuple-element.235, f32[4,512]{1,0:T(4,128)S(1)} %copy-done.84), kind=kOutput, calls=%fused_computation.67 | convolution fusion | flops 141691392 | bytes 17317888 | tf_op jit(solution)/shard_map/hqk,hqe->khe/dot_general | solution.py:603
  315.5 8.5 %fusion.70 = bf16[4,64,512]{2,1,0:T(8,128)(2,1)} fusion(f32[4,512,512]{1,2,0:T(8,128)} %fusion.129, bf16[512,3,4,64]{0,3,2,1:T(8,128)(2,1)} %reshape.464, f32[4,512,512]{1,2,0:T(8,128)} %get-tuple-element.235, f32[4,512]{1,0:T(4,128)S(1)} %copy-done.84), kind=kOutput, calls=%fused_computation.66 | convolution fusion | flops 141691392 | bytes 17317888 | tf_op jit(solution)/shard_map/hqk,hke->qhe/dot_general | solution.py:602
  324.0 3.1 convolution_convert_fusion.13
  330.3 4.8 slice.164
  339.9 6.2 all_gather.51
  356.4 6.5 all_gather.50
  372.5 3.0 all-gather.24.cloned.1.call-done
  378.1 28.1 %all-gather.16.cloned.1.call-done = bf16[512,3,4,256]{0,3,2,1:T(8,128)(2,1)} async-done(((bf16[512,3,1,256]{0,3,2,1:T(8,128)(2,1)}), bf16[512,3,4,256]{0,3,2,1:T(8,128)(2,1)}) %all-gather.16.cloned.1.call-update) | async-done | bytes 3145744 | tf_op jit(solution)/shard_map/all_gather | solution.py:605
  406.2 6.0 multiply_reduce_fusion.5
  438.1 3.2 fusion.152.refs_2_
  441.3 20.5 %all-gather.26.cloned.1.call-done = bf16[512,4096]{1,0:T(8,128)(2,1)} async-done(((bf16[128,4096]{1,0:T(8,128)(2,1)}), bf16[512,4096]{1,0:T(8,128)(2,1)}) %all-gather.26.cloned.1.call-update) | async-done | bytes 4194320 | tf_op jit(solution)/shard_map/all_gather | solution.py:469
  461.8 4.6 fusion.148.refs_4_
  468.1 30.2 %all-gather.30.cloned.1.call-done = bf16[512,4096]{1,0:T(8,128)(2,1)} async-done(((bf16[128,4096]{1,0:T(8,128)(2,1)}), bf16[512,4096]{1,0:T(8,128)(2,1)}) %all-gather.30.cloned.1.call-update) | async-done | bytes 4194320 | tf_op jit(solution)/shard_map/all_gather | solution.py:469
  498.3 4.5 fusion.146.refs_5_
  506.5 50.7 %all-reduce.4.cloned.1.call-done = (f32[240,2048]{0,1:T(8,128)}, f32[4,8,32,16]{2,1,0,3:T(8,128)}) async-done(((f32[240,2048]{0,1:T(8,128)}, f32[4,8,32,16]{2,1,0,3:T(8,128)}), (f32[240,2048]{0,1:T(8,128)}, f32[4,8,32,16]{2,1,0,3:T(8,128)})) %all-reduce.4.cloned.1.call-update) | async-done | bytes 2031632 | tf_op jit(solution)/shard_map/psum | solution.py:626
  568.6 7.5 all-gather.20.cloned.1.call-done
  581.4 165.6 %reduce_blocks.1 = (f32[32,3072]{1,0:T(8,128)S(1)}, f32[32,4096]{1,0:T(8,128)S(1)}, f32[32,8192]{1,0:T(8,128)}, f32[32,1024]{1,0:T(8,128)S(1)}, f32[8,128]{1,0:T(8,128)S(1)}) custom-call(f32[128,2048]{1,0:T(8,128)} %fusion.225.refs_0_, f32[128,1024]{1,0:T(8,128)} %fusion.154.refs_1_, f32[128,3072]{1,0:T(8,128)} %fusion.152.refs_2_, ...), custom_call_target="tpu_custom_call" | custom-call | tf_op jit(solution)/shard_map/reduce_blocks/pallas_call | solution.py:437
  (336 shorter events, 152.0 us)
Async XLA Ops:
  7.2 157.7 %copy-start.81 = (s32[1,48]{1,0:T(1,128)S(1)}, s32[1,48]{1,0:T(1,128)}, u32[]{:S(2)}) copy-start(s32[1,48]{1,0:T(1,128)} %param.28) | copy-start | bytes 580
  7.2 158.3 %copy-start.50 = (s32[1,512]{1,0:T(1,128)S(1)}, s32[1,512]{1,0:T(1,128)}, u32[]{:S(2)}) copy-start(s32[1,512]{1,0:T(1,128)} %param.27) | copy-start | bytes 6148
  14.6 149.1 %copy-start.64 = (f32[192]{0:T(256)}, f32[192]{0:T(256)S(1)}, u32[]{:S(2)}) copy-start(f32[192]{0:T(256)S(1)} %mul.512) | copy-start | bytes 2308
  164.8 13.6 %copy-start.54 = (s32[240]{0:T(256)}, s32[240]{0:T(256)S(1)}, u32[]{:S(2)}) copy-start(s32[240]{0:T(256)S(1)} %get-tuple-element.245) | copy-start | bytes 2884
  164.8 13.6 %copy-start.56 = (s32[240]{0:T(256)}, s32[240]{0:T(256)S(1)}, u32[]{:S(2)}) copy-start(s32[240]{0:T(256)S(1)} %get-tuple-element.246) | copy-start | bytes 2884
  164.9 13.5 %copy-start.60 = (pred[240]{0:T(512)(128)(4,1)}, pred[240]{0:T(512)(128)(4,1)S(1)}, u32[]{:S(2)}) copy-start(pred[240]{0:T(512)(128)(4,1)S(1)} %iota_compare_fusion.5) | copy-start | bytes 724
  197.5 15.9 %all-to-all-start = ((bf16[128,3,4,256]{3,0,1,2:T(8,128)(2,1)}), bf16[128,3,4,256]{3,0,1,2:T(8,128)(2,1)}, u32[]{:S(2)}, u32[]{:S(2)}) async-start(bf16[128,3,4,256]{3,0,1,2:T(8,128)(2,1)} %copy.179), calls=%async_computation | async-start | bytes 1572864 | tf_op jit(solution)/shard_map/all_to_all | solution.py:560
  201.7 40.4 %all-gather.12.cloned.1.call-start = ((), (), s32[]{:S(2)}) async-start(), calls=%async_computation.1 | async-start | bytes 1310720 | tf_op jit(solution)/shard_map/all_gather | solution.py:572
  226.8 18.4 %copy-start.52 = (f32[1024]{0:T(1024)S(1)}, f32[1024]{0:T(1024)}, u32[]{:S(2)}) copy-start(f32[1024]{0:T(1024)} %get-tuple-element.185) | copy-start | bytes 12292
  226.8 74.0 %all-gather.14.cloned.1.call-start = ((), (), s32[]{:S(2)}) async-start(), calls=%async_computation.2 | async-start | bytes 1310720 | tf_op jit(solution)/shard_map/all_gather | solution.py:469
  284.0 67.2 %all-gather.18.cloned.1.call-start = ((), (), s32[]{:S(2)}) async-start(), calls=%async_computation.4 | async-start | bytes 1310720 | tf_op jit(solution)/shard_map/all_gather | solution.py:469
  284.7 69.1 %all-gather.22.cloned.1.call-start = ((), (), s32[]{:S(2)}) async-start(), calls=%async_computation.6 | async-start | bytes 1310720 | tf_op jit(solution)/shard_map/all_gather | solution.py:469
  285.3 81.4 %all-gather.32.cloned.1.call-start = ((), (), s32[]{:S(2)}) async-start(), calls=%async_computation.11 | async-start | bytes 1310720 | tf_op jit(solution)/shard_map/all_gather | solution.py:469
  285.9 89.7 %all-gather.24.cloned.1.call-start = ((), (), s32[]{:S(2)}) async-start(), calls=%async_computation.7 | async-start | bytes 1310720 | tf_op jit(solution)/shard_map/all_gather | solution.py:469
  289.0 18.0 %copy-start.84 = (f32[4,512]{1,0:T(4,128)S(1)}, f32[4,512]{1,0:T(4,128)}, u32[]{:S(2)}) copy-start(f32[4,512]{1,0:T(4,128)} %get-tuple-element.234) | copy-start | bytes 24580
  289.0 117.2 %all-gather.16.cloned.1.call-start = ((), (), s32[]{:S(2)}) async-start(), calls=%async_computation.3 | async-start | bytes 3932160 | tf_op jit(solution)/shard_map/all_gather | solution.py:605
  328.1 103.4 %all-gather.28.cloned.1.call-start = ((), (), s32[]{:S(2)}) async-start(), calls=%async_computation.9 | async-start | bytes 1310720 | tf_op jit(solution)/shard_map/all_gather | solution.py:469
  328.9 132.9 %all-gather.26.cloned.1.call-start = ((), (), s32[]{:S(2)}) async-start(), calls=%async_computation.8 | async-start | bytes 5242880 | tf_op jit(solution)/shard_map/all_gather | solution.py:469
  329.6 168.7 %all-gather.30.cloned.1.call-start = ((), (), s32[]{:S(2)}) async-start(), calls=%async_computation.10 | async-start | bytes 5242880 | tf_op jit(solution)/shard_map/all_gather | solution.py:469
  330.2 227.1 %all-reduce.4.cloned.1.call-start = ((), (), s32[]{:S(2)}) async-start(), calls=%async_computation.12 | async-start | bytes 4718592 | tf_op jit(solution)/shard_map/psum | solution.py:626
  429.9 146.2 %all-gather.20.cloned.1.call-start = ((), (), s32[]{:S(2)}) async-start(), calls=%async_computation.5 | async-start | bytes 1310720 | tf_op jit(solution)/shard_map/all_gather | solution.py:469
  506.5 57.7 %copy-start.35 = (bf16[4,1,32,240]{3,2,1,0:T(8,128)(2,1)S(1)}, bf16[4,1,32,240]{3,2,1,0:T(8,128)(2,1)}, u32[]{:S(2)}) copy-start(bf16[4,1,32,240]{3,2,1,0:T(8,128)(2,1)} %get-tuple-element.224) | copy-start | bytes 184324
  561.2 15.0 %copy-start.72 = (s32[1024]{0:T(1024)S(1)}, s32[1024]{0:T(1024)}, u32[]{:S(2)}) copy-start(s32[1024]{0:T(1024)} %fusion.181) | copy-start | bytes 12292
  561.2 15.0 %copy-start.83 = (pred[1024]{0:T(1024)(128)(4,1)S(1)}, pred[1024]{0:T(1024)(128)(4,1)}, u32[]{:S(2)}) copy-start(pred[1024]{0:T(1024)(128)(4,1)} %fusion.174) | copy-start | bytes 3076
  563.1 15.0 %copy-start.13 = (bf16[512,256]{1,0:T(8,128)(2,1)S(1)}, bf16[512,256]{1,0:T(8,128)(2,1)}, u32[]{:S(2)}) copy-start(bf16[512,256]{1,0:T(8,128)(2,1)} %all_gather.51) | copy-start | bytes 786436
  566.4 13.2 %copy-start.28 = (bf16[128,192]{1,0:T(8,128)(2,1)S(1)}, bf16[128,192]{1,0:T(8,128)(2,1)}, u32[]{:S(2)}) copy-start(bf16[128,192]{1,0:T(8,128)(2,1)} %copy.192) | copy-start | bytes 147460
  568.6 11.2 %copy-start.32 = (bf16[512,256]{1,0:T(8,128)(2,1)S(1)}, bf16[512,256]{1,0:T(8,128)(2,1)}, u32[]{:S(2)}) copy-start(bf16[512,256]{1,0:T(8,128)(2,1)} %convolution_convert_fusion.12) | copy-start | bytes 786436
  568.6 12.7 %copy-start.80 = (f32[128]{0:T(128)S(1)}, f32[128]{0:T(128)}, u32[]{:S(2)}) copy-start(f32[128]{0:T(128)} %compare_select_fusion) | copy-start | bytes 1540
  581.3 168.3 %copy-start.39 = (f32[32,9]{1,0:T(8,128)S(1)}, f32[32,9]{1,0:T(8,128)}, u32[]{:S(2)}) copy-start(f32[32,9]{1,0:T(8,128)} %copy.196) | copy-start | bytes 3460
  581.3 168.3 %copy-start.40 = (f32[32,9]{1,0:T(8,128)S(1)}, f32[32,9]{1,0:T(8,128)}, u32[]{:S(2)}) copy-start(f32[32,9]{1,0:T(8,128)} %copy.193) | copy-start | bytes 3460
  581.3 171.1 %copy-start.20 = (f32[32,3072]{1,0:T(8,128)S(1)}, f32[32,3072]{1,0:T(8,128)}, u32[]{:S(2)}) copy-start(f32[32,3072]{1,0:T(8,128)} %param.31) | copy-start | bytes 1179652
  581.3 173.6 %copy-start.14 = (f32[32,4096]{1,0:T(8,128)S(1)}, f32[32,4096]{1,0:T(8,128)}, u32[]{:S(2)}) copy-start(f32[32,4096]{1,0:T(8,128)} %param.32) | copy-start | bytes 1572868
  (66 other events, 290.3 us)
Sparse Core Ops, SparseCore 0:
  227.0 15.1 all-gather.11
  284.1 16.7 all-gather.13
  302.4 16.8 all-gather.17
  321.3 16.7 all-gather.21
  340.0 16.7 all-gather.31
  358.8 16.7 all-gather.23
  377.7 28.5 all-gather.15
  408.4 16.7 all-gather.27
  427.3 34.4 all-gather.25
  463.8 34.4 all-gather.29
  501.4 55.8 all-reduce.3
  559.3 16.8 all-gather.19

commit v3 on v2

--- a/solution.py
+++ b/solution.py
@@ -16,8 +16,8 @@
 LEAD_STEPS = 8
 WIDTH = VARS * PIX
 SPAN = 256
-MIX = WIDTH + VARS
-USED = 2 * WIDTH + VARS + SPAN
+MIX = 256
+HEAD = 896
 
 norm_eps = 1e-05
 clip_limit = 1.0
@@ -30,10 +30,8 @@
 MESH = pl.DeviceIdType.MESH
 STRIP = 32
 CHUNK = 512
-DEPTH = 2
 LAG = 2
 QUEUE = 2
-MISC = 1024
 
 
 def dot(left, right, dims):
@@ -82,7 +80,7 @@
 
 
 PIECES = (
-    (0, 0, 1920, "yzx"), (2, 0, 2688, "zxy"), (0, 1920, 1920, "yzx"), (2, 2688, 2816, "zxy"),
+    (0, 0, 1920, "yzx"), (2, 0, 2688, "zxy"), (0, 1920, 2048, "yzx"), (2, 2688, 2816, "zxy"),
     (1, 0, 1920, "yzx"), (2, 5504, 2688, "zxy"), (1, 1920, 2176, "zxy"),
 )
 
@@ -252,16 +250,20 @@
     )(head, attn, mlp, number)
 
 
-def reduce_kernel(widths, outs_at, *refs):
-    n_in = len(widths)
-    keep, give = refs[:n_in], refs[n_in : 2 * n_in]
-    num_ref = refs[2 * n_in]
-    outs = refs[2 * n_in + 1 : 2 * n_in + 1 + len(outs_at)]
-    stat_ref = refs[2 * n_in + 1 + len(outs_at)]
-    (own_buf, give_buf, got, rise, fall, done, tally, quad_buf, line_buf,
-     own_sem, give_sem, y_send, y_recv, z_send, z_recv, s_send, s_recv) = refs[2 * n_in + 2 + len(outs_at) :]
+SEGMENTS = ((0, 2, 0), (2, 8, 1), (8, 16, 2), (16, 24, 3), (24, 26, 4))
+N_STD, N_ALL, FIRST_SENT, AHEAD, BASE = 26, 32, 8, 4, 2
+
+
+def gradient_kernel(*refs):
+    (mixed_t, norm0_t, norm1_t, out_t, mixa_t, norm2_t, agg_t,
+     d_proj, d_qkv, d_up, lifted, d_agg, d_pred, onehot, d_table, narrow, head, num_ref) = refs[:18]
+    r_agg, r_attn, r_mlp, r_misc, stat_ref = refs[18:23]
+    (feats, ys, tabs, preds, hots, narrows, w240, wkv, acc240, own_buf, give_buf, got, rise, fall, tally, quad_buf,
+     line_buf, load_sem, feat_send, feat_recv, y_xsend, y_xrecv, tab_send, tab_recv, pred_send, pred_recv,
+     nar_send, nar_recv, y_send, y_recv, z_send, z_recv, s_send, s_recv) = refs[23:]
     dp, own = lax.axis_index("dp"), lax.axis_index("fsdp")
-    z, y = dp // 2, dp % 2
+    z, y, x, core = dp // 2, dp % 2, own // 2, own % 2
+    sibling, across, diagonal = x * 2 + 1 - core, (1 - x) * 2 + core, (1 - x) * 2 + 1 - core
     over = z * 2 + 1 - y
     barrier = pltpu.get_barrier_semaphore()
     for d in range(1, 8):
@@ -269,16 +271,179 @@
     for d in range(1, 4):
         pl.semaphore_signal(barrier, inc=1, device_id=(dp, lax.rem(own + d, 4)), device_id_type=MESH)
     pl.semaphore_wait(barrier, 10)
-    places = [(i, j) for i in range(n_in) for j in range(widths[i] // CHUNK)]
-    n = len(places)
-
-    def load(c):
-        i, j = places[c]
-        return pltpu.make_async_copy(keep[i].at[:, pl.ds(j * CHUNK, CHUNK)], own_buf.at[c], own_sem.at[c])
-
-    def stage(c):
-        i, j = places[c]
-        return pltpu.make_async_copy(give[i].at[:, pl.ds(j * CHUNK, CHUNK)], give_buf.at[c], give_sem.at[c])
+    n = N_ALL
+    row = pl.ds(pl.multiple_of(own * 128, 128), 128)
+    sent_feats = (norm0_t, norm1_t, out_t, mixa_t, norm2_t, agg_t)
+
+    def remote(src, dst, send, recv, to):
+        return pltpu.make_async_remote_copy(
+            src_ref=src, dst_ref=dst, send_sem=send, recv_sem=recv, device_id=(dp, to), device_id_type=MESH
+        )
+
+    loads = []
+
+    def load(src, dst):
+        copy = pltpu.make_async_copy(src, dst, load_sem.at[len(loads)])
+        copy.start()
+        loads.append(copy)
+
+    def feat_send_all(k, d):
+        to = lax.rem(own + d, 4)
+        for half in range(2):
+            side = y if half == 0 else 1 - y
+            remote(
+                sent_feats[k].at[:, side, to], feats.at[k + 1, half, :, :, row], feat_send.at[k, d, half],
+                feat_recv.at[k, d, half], to,
+            ).start()
+
+    for k in range(6):
+        for d in range(1, 4):
+            feat_send_all(k, d)
+    for half in range(2):
+        load(mixed_t.at[:, y if half == 0 else 1 - y, own], feats.at[0, half])
+    for c in range(2):
+        load(d_proj.at[:, pl.ds(c * CHUNK, CHUNK)], ys.at[c])
+    for k in range(6):
+        for half in range(2):
+            load(sent_feats[k].at[:, y if half == 0 else 1 - y, own], feats.at[k + 1, half, :, :, row])
+    for c in range(6):
+        load(d_qkv.at[:, pl.ds(c * CHUNK, CHUNK)], ys.at[2 + c])
+    staged = len(loads)
+    for source, width, at in ((d_up, FF, 8), (lifted, FF, 16), (d_agg, D, 24)):
+        for c in range(width // CHUNK):
+            load(source.at[:, pl.ds(c * CHUNK, CHUNK)], ys.at[at + c, row, :])
+    for v in range(4):
+        load(d_table.at[:, pl.ds(v * CHUNK, CHUNK)], tabs.at[v, own])
+    load(d_pred, preds.at[row, :])
+    load(onehot, hots)
+    for half in range(2):
+        side = y if half == 0 else 1 - y
+        load(narrow.at[:, side, own], narrows.at[own, half])
+        load(head.at[:, side, own, :, pl.ds(0, 256)], w240.at[half])
+        load(head.at[:, side, own, :, pl.ds(HEAD, 2 * D)], wkv.at[half])
+
+    def unit(u, who, slot, to):
+        block = ys.at[FIRST_SENT + u, pl.ds(pl.multiple_of(who * 128, 128), 128), :]
+        return remote(block, block, y_xsend.at[u, slot], y_xrecv.at[u, who], to)
+
+    def table(v, who, slot, to):
+        return remote(tabs.at[v, who], tabs.at[v, who], tab_send.at[v, slot], tab_recv.at[v, who], to)
+
+    for copy in loads[staged:]:
+        copy.wait()
+
+    def begin(u, carry):
+        unit(u, own, 0, across).start()
+        unit(u, own, 1, sibling).start()
+        return carry
+
+    lax.fori_loop(0, N_STD - FIRST_SENT, begin, 0)
+    for v in range(4):
+        table(v, own, 0, across).start()
+        table(v, own, 1, sibling).start()
+
+    def pred_copy(d, who, to):
+        block = preds.at[pl.ds(pl.multiple_of(who * 128, 128), 128), :]
+        return remote(block, block, pred_send.at[d], pred_recv.at[d], to)
+
+    def narrow_copy(d, half, who, to):
+        side = y if half == 0 else 1 - y
+        return remote(narrow.at[:, side, to], narrows.at[who, half], nar_send.at[d, half], nar_recv.at[d, half], to)
+
+    for d in range(1, 4):
+        pred_copy(d, own, lax.rem(own + d, 4)).start()
+        for half in range(2):
+            narrow_copy(d, half, own, lax.rem(own + d, 4)).start()
+    for copy in loads[:staged]:
+        copy.wait()
+    tally[...] = jnp.zeros_like(tally)
+    acc240[...] = jnp.zeros_like(acc240)
+
+    def feat_wait(k):
+        for d in range(1, 4):
+            for half in range(2):
+                place = feats.at[k + 1, half, :, :, row]
+                remote(place, place, feat_send.at[k, d, half], feat_recv.at[k, d, half], own).wait_recv()
+
+    def put(c, value):
+        own_buf[c] = value[:128]
+        give_buf[c] = value[128:].astype(bf16)
+
+    def feature(k):
+        return feats[k].reshape(256, 512)
+
+    def matmul(a, b):
+        return lax.dot_general(a, b, (((1,), (0,)), ((), ())), preferred_element_type=f32)
+
+    def two(value):
+        high = value.astype(bf16)
+        return high, (value - high.astype(f32)).astype(bf16)
+
+    def summed_table(v):
+        total = tabs[v, 0].astype(f32) + tabs[v, 1].astype(f32)
+        return two(total + tabs[v, 2].astype(f32) + tabs[v, 3].astype(f32))
+
+    def compute(c):
+        for low, high, k in SEGMENTS:
+            if k > 0:
+                pl.when(c == low)(functools.partial(feat_wait, k - 1))
+
+            @pl.when((c >= low) & (c < high))
+            def _():
+                if low >= FIRST_SENT:
+                    u = c - FIRST_SENT
+                    unit(u, sibling, 1, own).wait_recv()
+                    unit(u, diagonal, 2, own).wait_recv()
+                put(c, matmul(feature(k), ys[c]))
+
+        @pl.when((c >= N_STD) & (c < N_STD + 4))
+        def _():
+            v = c - N_STD
+            table(v, sibling, 1, own).wait_recv()
+            table(v, diagonal, 2, own).wait_recv()
+            high, low = summed_table(v)
+            rows = w240[...].reshape(256, 256)
+            put(c, matmul(rows, high) + matmul(rows, low))
+
+        for v in range(4):
+            @pl.when(c == N_STD + v)
+            def _():
+                high, low = summed_table(v)
+                rows = wkv[:, :, :, v * CHUNK : (v + 1) * CHUNK].reshape(256, CHUNK)
+                dims = (((1,), (1,)), ((), ()))
+                acc240[...] = (
+                    acc240[...]
+                    + lax.dot_general(rows, high, dims, preferred_element_type=f32)
+                    + lax.dot_general(rows, low, dims, preferred_element_type=f32)
+                )
+
+        @pl.when(c == N_STD + 4)
+        def _():
+            feat_wait(4)
+            for d in range(1, 4):
+                pred_copy(d, lax.rem(own + 4 - d, 4), own).wait_recv()
+            value = matmul(feature(5), preds[...])
+            own_buf[c, :, 0:256] = acc240[:128]
+            own_buf[c, :, 256:512] = value[:128]
+            give_buf[c, :, 0:256] = acc240[128:].astype(bf16)
+            give_buf[c, :, 256:512] = value[128:].astype(bf16)
+
+        @pl.when(c == N_STD + 5)
+        def _():
+            feat_wait(5)
+            for d in range(1, 4):
+                for half in range(2):
+                    place = narrows.at[lax.rem(own + 4 - d, 4), half]
+                    remote(place, place, nar_send.at[d, half], nar_recv.at[d, half], own).wait_recv()
+            value = matmul(feature(6), hots[...])
+            small = ((narrows[0] + narrows[1]) + (narrows[2] + narrows[3])).reshape(256, 128)
+            empty = jnp.zeros((128, 128), f32)
+            own_buf[c, :, 0:256] = value[:128]
+            own_buf[c, :, 256:384] = small[:128]
+            own_buf[c, :, 384:512] = empty
+            give_buf[c, :, 0:256] = value[128:].astype(bf16)
+            give_buf[c, :, 256:384] = small[128:].astype(bf16)
+            give_buf[c, :, 384:512] = empty.astype(bf16)
 
     def cross(c):
         return pltpu.make_async_remote_copy(
@@ -286,20 +451,10 @@
             recv_sem=y_recv.at[c], device_id=(over, own), device_id_type=MESH,
         )
 
-    for c in range(n):
-        stage(c).start()
-    for c in range(n):
-        load(c).start()
-    for c in range(DEPTH):
-        stage(c).wait()
-        cross(c).start()
-    for c in range(DEPTH, n):
-        stage(c).wait()
-    tally[...] = jnp.zeros_like(tally)
-
     def hop(buf, way, c, b, to):
+        at = b - 1 if way == 0 else b
         return pltpu.make_async_remote_copy(
-            src_ref=buf.at[c, b], dst_ref=buf.at[c, b], send_sem=z_send.at[way, c, b], recv_sem=z_recv.at[way, c, b],
+            src_ref=buf.at[c, at], dst_ref=buf.at[c, at], send_sem=z_send.at[way, c, at], recv_sem=z_recv.at[way, c, at],
             device_id=(to * 2 + y, own), device_id_type=MESH,
         )
 
@@ -310,33 +465,48 @@
     early, late = LAG * jnp.minimum(z, 3 - z), LAG * jnp.maximum(z, 3 - z)
 
     def step(t, carry):
-        first = t - early
+        u = t - AHEAD
+
+        @pl.when((u >= 0) & (u < N_STD - FIRST_SENT))
+        def _():
+            unit(u, across, 0, own).wait_recv()
+            unit(u, across, 2, sibling).start()
+
+        v = u - (N_STD - FIRST_SENT)
+
+        @pl.when((v >= 0) & (v < 4))
+        def _():
+            table(v, across, 0, own).wait_recv()
+            table(v, across, 2, sibling).start()
+
+        @pl.when(t < n)
+        def _():
+            compute(t)
+            cross(t).start()
+
+        first = t - BASE - early
 
         @pl.when((first >= 0) & (first < n))
         def _():
-            pltpu.make_async_copy(own_buf.at[first], own_buf.at[first], own_sem.at[first]).wait()
             cross(first).wait()
 
-            @pl.when(first + DEPTH < n)
-            def _():
-                cross(first + DEPTH).start()
-
         for way, buf, lag, to, back in ((0, rise, LAG * z, z + 1, z - 1), (1, fall, LAG * (3 - z), z - 1, z + 1)):
-            c = t - lag
+            c = t - BASE - lag
 
             @pl.when((c >= 0) & (c < n))
             def _():
-                for b in range(4):
+                for b in ((1, 2, 3) if way == 0 else (0, 1, 2)):
                     beyond = (b > z) if way == 0 else (b < z)
+                    at = b - 1 if way == 0 else b
 
                     @pl.when(beyond & (lag == 0))
                     def _():
-                        buf[c, b] = here(c, b)
+                        buf[c, at] = here(c, b)
 
                     @pl.when(beyond & (lag > 0))
                     def _():
                         hop(buf, way, c, b, back).wait_recv()
-                        buf[c, b] = buf[c, b] + here(c, b)
+                        buf[c, at] = buf[c, at] + here(c, b)
 
                     @pl.when(beyond & (c >= QUEUE))
                     def _():
@@ -346,24 +516,25 @@
                     def _():
                         hop(buf, way, c, b, to).start()
 
-        last = t - late
+        last = t - BASE - late
 
         @pl.when((last >= 0) & (last < n))
         def _():
             at = pl.ds(pl.multiple_of(z * STRIP, STRIP), STRIP)
-            done[last] = own_buf[last, at, :] + got[last, at, :].astype(f32)
+            value = own_buf[last, at, :] + got[last, at, :].astype(f32)
+            own_buf[last, 0:STRIP, :] = value
 
             @pl.when(z > 0)
             def _():
                 hop(rise, 0, last, z, z - 1).wait_recv()
-                done[last] = done[last] + rise[last, z]
+                own_buf[last, 0:STRIP, :] = own_buf[last, 0:STRIP, :] + rise[last, z - 1]
 
             @pl.when(z < 3)
             def _():
                 hop(fall, 1, last, z, z + 1).wait_recv()
-                done[last] = done[last] + fall[last, z]
-
-            value = done[last]
+                own_buf[last, 0:STRIP, :] = own_buf[last, 0:STRIP, :] + fall[last, z]
+
+            value = own_buf[last, 0:STRIP, :]
             square = value * value
             total = square[0:8, 0:128]
             for r in range(0, STRIP, 8):
@@ -374,11 +545,10 @@
 
         return carry
 
-    lax.fori_loop(0, n + 3 * LAG, step, 0)
+    lax.fori_loop(0, n + BASE + 3 * LAG, step, 0)
     summed = jnp.sum(tally[...])
     lane = lax.broadcasted_iota(jnp.int32, (8, 128), 1)
-    mine = jnp.where(lane == 0, summed, jnp.where(lane == 1, num_ref[...], 0.0))
-    quad_buf[own] = mine
+    quad_buf[own] = jnp.where(lane == 0, summed, jnp.where(lane == 1, num_ref[...], 0.0))
 
     def share(buf, k, where, at):
         return pltpu.make_async_remote_copy(
@@ -388,9 +558,12 @@
 
     for d in range(1, 4):
         share(quad_buf, d, (dp, lax.rem(own + d, 4)), own).start()
-    for (i, j), c in zip(places, range(n)):
-        target, base = outs_at_of(outs_at, i)
-        outs[target][:, base + j * CHUNK : base + (j + 1) * CHUNK] = done[c]
+    for out, base, low, high in (
+        (r_attn, 3 * D, 0, 2), (r_attn, 0, 2, 8), (r_mlp, 0, 8, 24), (r_agg, 2 * D, 24, 26), (r_agg, 0, 26, 30),
+        (r_misc, 0, 30, 32),
+    ):
+        for c in range(low, high):
+            out[:, base + (c - low) * CHUNK : base + (c - low + 1) * CHUNK] = own_buf[c, 0:STRIP, :]
     for d in range(1, 4):
         share(quad_buf, d, (dp, own), lax.rem(own + 4 - d, 4)).wait_recv()
     line_buf[dp] = (quad_buf[0] + quad_buf[1]) + (quad_buf[2] + quad_buf[3])
@@ -406,63 +579,89 @@
         share(quad_buf, d, (dp, own), own).wait_send()
     for d in range(1, 8):
         share(line_buf, 3 + d, (dp, own), dp).wait_send()
+    for k in range(6):
+        for d in range(1, 4):
+            for half in range(2):
+                place = feats.at[k + 1, half, :, :, row]
+                remote(place, place, feat_send.at[k, d, half], feat_recv.at[k, d, half], own).wait_send()
+    for d in range(1, 4):
+        pred_copy(d, own, own).wait_send()
+        for half in range(2):
+            narrow_copy(d, half, own, own).wait_send()
+    for v in range(4):
+        for slot, who in ((0, own), (1, own), (2, across)):
+            table(v, who, slot, own).wait_send()
+
+    def finish(u, carry):
+        for slot, who in ((0, own), (1, own), (2, across)):
+            unit(u, who, slot, own).wait_send()
+        return carry
+
+    lax.fori_loop(0, N_STD - FIRST_SENT, finish, 0)
 
     def drain(c, carry):
-        for b in range(4):
-            @pl.when(b > z)
-            def _():
-                hop(rise, 0, c, b, z + 1).wait_send()
-
-            @pl.when(b < z)
-            def _():
-                hop(fall, 1, c, b, z - 1).wait_send()
+        for b in (1, 2, 3):
+            pl.when(b > z)(lambda: hop(rise, 0, c, b, z).wait_send())
+        for b in (0, 1, 2):
+            pl.when(b < z)(lambda: hop(fall, 1, c, b, z).wait_send())
         return carry
 
     lax.fori_loop(n - QUEUE, n, drain, 0)
 
 
-def outs_at_of(outs_at, i):
-    for target, members in enumerate(outs_at):
-        for index, base in members:
-            if index == i:
-                return target, base
-
-
-def reduce_blocks(keep, give, numerator, outs_at, out_widths):
-    widths = [a.shape[1] for a in keep]
-    n = sum(widths) // CHUNK
+def gradient_blocks(operands, numbers):
     any_space = pl.BlockSpec(memory_space=pl.ANY)
     vmem = pl.BlockSpec(memory_space=pltpu.VMEM)
-    half = 4 * STRIP
+    n = N_ALL
+    units = N_STD - FIRST_SENT
+    dma = pltpu.SemaphoreType.DMA
+    widths = (3 * D, 4 * D, 2 * FF, 2 * CHUNK)
     return pl.pallas_call(
-        functools.partial(reduce_kernel, tuple(widths), outs_at),
-        out_shape=[jax.ShapeDtypeStruct((STRIP, w), f32) for w in out_widths] + [jax.ShapeDtypeStruct((8, 128), f32)],
-        in_specs=[any_space] * (2 * len(keep)) + [vmem],
-        out_specs=[vmem] * (len(out_widths) + 1),
+        gradient_kernel,
+        out_shape=[jax.ShapeDtypeStruct((STRIP, w), f32) for w in widths] + [jax.ShapeDtypeStruct((8, 128), f32)],
+        in_specs=[any_space] * 17 + [vmem],
+        out_specs=[vmem] * 5,
         scratch_shapes=[
-            pltpu.VMEM((n, half, CHUNK), f32),
-            pltpu.VMEM((n, half, CHUNK), bf16),
-            pltpu.VMEM((n, half, CHUNK), bf16),
-            pltpu.VMEM((n, 4, STRIP, CHUNK), f32),
-            pltpu.VMEM((n, 4, STRIP, CHUNK), f32),
-            pltpu.VMEM((n, STRIP, CHUNK), f32),
+            pltpu.VMEM((7, 2, 4, STRIP, 512), bf16),
+            pltpu.VMEM((N_STD, 512, CHUNK), bf16),
+            pltpu.VMEM((4, 4, 256, CHUNK), bf16),
+            pltpu.VMEM((512, 256), bf16),
+            pltpu.VMEM((512, 256), bf16),
+            pltpu.VMEM((4, 2, 4, STRIP, 128), f32),
+            pltpu.VMEM((2, 4, STRIP, 256), bf16),
+            pltpu.VMEM((2, 4, STRIP, 2 * D), bf16),
+            pltpu.VMEM((256, 256), f32),
+            pltpu.VMEM((n, 4 * STRIP, CHUNK), f32),
+            pltpu.VMEM((n, 4 * STRIP, CHUNK), bf16),
+            pltpu.VMEM((n, 4 * STRIP, CHUNK), bf16),
+            pltpu.VMEM((n, 3, STRIP, CHUNK), f32),
+            pltpu.VMEM((n, 3, STRIP, CHUNK), f32),
             pltpu.VMEM((8, 128), f32),
             pltpu.VMEM((4, 8, 128), f32),
             pltpu.VMEM((8, 8, 128), f32),
-            pltpu.SemaphoreType.DMA((n,)),
-            pltpu.SemaphoreType.DMA((n,)),
-            pltpu.SemaphoreType.DMA((n,)),
-            pltpu.SemaphoreType.DMA((n,)),
-            pltpu.SemaphoreType.DMA((2, n, 4)),
-            pltpu.SemaphoreType.DMA((2, n, 4)),
-            pltpu.SemaphoreType.DMA((11,)),
-            pltpu.SemaphoreType.DMA((11,)),
+            dma((56,)),
+            dma((6, 4, 2)),
+            dma((6, 4, 2)),
+            dma((units, 3)),
+            dma((units, 4)),
+            dma((4, 3)),
+            dma((4, 4)),
+            dma((4,)),
+            dma((4,)),
+            dma((4, 2)),
+            dma((4, 2)),
+            dma((n,)),
+            dma((n,)),
+            dma((2, n, 3)),
+            dma((2, n, 3)),
+            dma((11,)),
+            dma((11,)),
         ],
         compiler_params=pltpu.CompilerParams(
-            collective_id=1, has_side_effects=True, vmem_limit_bytes=52 * 2**20
+            collective_id=1, has_side_effects=True, vmem_limit_bytes=60 * 2**20
         ),
-        name="reduce_blocks",
-    )(*keep, *give, numerator)
+        name="gradient_blocks",
+    )(*operands, numbers)
 
 
 def ag(part):
@@ -489,10 +688,10 @@
         wide = heads_here * HEAD_DIM
 
         seg = segment_ids[0]
-        seg_own = lax.dynamic_slice_in_dim(seg, own * rows, rows)
-        below = jnp.sum((seg[None, :] < seg_own[:, None]).astype(jnp.int32), axis=1)
-        pos = own * rows + jnp.arange(rows, dtype=jnp.int32) - below
-        onehot = (pos[:, None] == jnp.arange(SPAN, dtype=jnp.int32)[None, :]).astype(bf16)
+        below = jnp.sum((seg[None, :] < seg[:, None]).astype(jnp.int32), axis=1)
+        pos = jnp.arange(row_len, dtype=jnp.int32) - below
+        onehot_all = (pos[:, None] == jnp.arange(SPAN, dtype=jnp.int32)[None, :]).astype(bf16)
+        onehot = lax.dynamic_slice_in_dim(onehot_all, own * rows, rows)
         lead = (lead_index[0].astype(f32) + 1.0) / LEAD_STEPS
         pixel_rows = pixels[0]
         target = targets[0].astype(f32)
@@ -505,11 +704,21 @@
         pixel_weight = lat_weight[0][:, None] * valid_mask[0].astype(f32) * present_cols[None, :]
         weight_sum = jnp.sum(pixel_weight)
 
+        def blank(width):
+            return jnp.zeros((strip, width), bf16)
+
+        io_low = w_io.astype(bf16)
+        emb = 2 * WIDTH + VARS
         pack = jnp.concatenate(
             [
-                w_io[:, :USED].astype(bf16),
+                io_low[:, :WIDTH],
+                io_low[:, 2 * WIDTH : emb],
+                blank(MIX - WIDTH - VARS),
+                io_low[:, WIDTH : 2 * WIDTH],
+                blank(256 - WIDTH),
+                io_low[:, emb : emb + SPAN],
                 w_small.astype(bf16),
-                jnp.zeros((strip, 768 - USED - 9), bf16),
+                blank(128 - w_small.shape[1]),
                 w_agg.astype(bf16),
             ],
             axis=1,
@@ -524,18 +733,20 @@
             attn = lax.all_gather(w_attn.astype(bf16), ("dp", "fsdp"), axis=0, tiled=True)
             mlp = lax.all_gather(w_mlp.astype(bf16), ("dp", "fsdp"), axis=0, tiled=True)
             total = lax.psum(weight_sum, ("dp", "fsdp"))
-        w240 = jnp.concatenate([head[:, :WIDTH], head[:, 2 * WIDTH : 2 * WIDTH + VARS]], axis=1)
-        w_pred = head[:, WIDTH : 2 * WIDTH]
-        w_pos = head[:, 2 * WIDTH + VARS : USED]
-        small = head[:, USED : USED + 9].astype(f32).T
-        agg_kv = head[:, 768 : 768 + 2 * D]
-        agg_out = head[:, 768 + 2 * D :]
+        w240 = head[:, :MIX]
+        w_pred = head[:, 256 : 256 + WIDTH]
+        w_pos = head[:, 512 : 512 + SPAN]
+        small = head[:, 768:777].astype(f32).T
+        agg_kv = head[:, HEAD : HEAD + 2 * D]
+        agg_out = head[:, HEAD + 2 * D :]
         w_qkv = attn[:, : 3 * D]
         w_out = attn[:, 3 * D :]
         w_up = mlp[:, :FF]
         w_down = mlp[:, FF:]
 
-        pix_t = jnp.concatenate([pixel_rows.T, jnp.ones((VARS, rows), bf16)], axis=0)
+        pix_t = jnp.concatenate(
+            [pixel_rows.T, jnp.ones((VARS, rows), bf16), jnp.zeros((MIX - WIDTH - VARS, rows), bf16)], axis=0
+        )
         table = t_mm(w240, agg_kv)
         table_k = table[:, :D].reshape(MIX, HEADS, HEAD_DIM)
         table_v = table[:, D:].reshape(MIX, HEADS, HEAD_DIM)
@@ -623,76 +834,63 @@
             [d_query, d_gain0, d_off0, d_gain1, d_off1, d_gain2, d_off2, lead * d_bias, d_bias]
             + [jnp.zeros((D,), f32)] * 7
         )
-        d_table, narrow = lax.psum((jnp.concatenate([d_table_k, d_table_v], axis=1), narrow), "fsdp")
-
-        source = jnp.arange(D)
-        pick = (source // strip) % n_f == own
+        d_table = jnp.concatenate([d_table_k, d_table_v], axis=1)
         if fast:
-            line, side = source // 256, (source // 128) % 2
-            here = lax.axis_index("dp") % 2
-            place = jnp.where(side == here, 0, 4 * strip) + line * strip + source % strip
-        else:
-            place = (source // (strip * n_f)) * strip + source % strip
-        choose = (pick[:, None] & (place[:, None] == jnp.arange(n_dp * strip)[None, :])).astype(bf16)
-
-        def mine(array):
-            width = array.shape[1]
-            if not fast:
-                whole = array.reshape(n_dp, n_f, strip, width)
-                return (lax.dynamic_index_in_dim(whole, own, 1, False).reshape(n_dp * strip, width),)
-            whole = array.reshape(4, 2 * n_f, strip, width)
-            return tuple(
-                lax.dynamic_index_in_dim(whole, at * n_f + own, 1, False).reshape(4 * strip, width)
-                for at in (here, 1 - here)
-            )
-
-        def split(picked):
-            if not fast:
-                return (picked,)
-            return picked[:, : 4 * strip], picked[:, 4 * strip :]
-
-        def weight_grad(features, grads):
-            return tuple(t_mm(part, grads) for part in split(mm(features, choose).astype(bf16)))
-
-        d_agg_all = ag(d_agg)
-        g_qkv = weight_grad(ag(norm0), d_qkv_all)
-        g_proj = weight_grad(mixed_all, d_proj_all)
-        g_up = weight_grad(ag(norm1), ag(d_up))
-        g_down = weight_grad(ag(d_out), ag(lifted))
-        g_out = weight_grad(ag(mixed_a), d_agg_all)
-        g_kv = tuple(exact("dc,cx->dx", part.astype(f32), d_table) for part in mine(w240))
-        g_240 = tuple(exact("dx,cx->dc", part.astype(f32), d_table) for part in mine(agg_kv))
-        g_pred = weight_grad(ag(norm2), ag(d_pred))
-        g_pos = weight_grad(d_agg_all, ag(onehot))
-        g_small = mine(narrow.T)
-        g_misc = tuple(
-            jnp.concatenate(
-                [a[:, :WIDTH], b, a[:, WIDTH:], c, d[:, :9], jnp.zeros((a.shape[0], MISC - USED - 9), f32)], axis=1
-            )
-            for a, b, c, d in zip(g_240, g_pred, g_pos, g_small)
-        )
-        groups = (g_kv, g_out, g_qkv, g_proj, g_up, g_down, g_misc)
-        if fast:
+
+            def sorted_rows(array):
+                return array.reshape(4, 2, n_f, strip, array.shape[1])
+
             lane = lax.broadcasted_iota(jnp.int32, (8, 128), 1)
-            r_agg, r_attn, r_mlp, r_misc, stat = reduce_blocks(
-                [g[0] for g in groups],
-                [g[1].astype(bf16) for g in groups],
+            r_agg, r_attn, r_mlp, r_misc, stat = gradient_blocks(
+                [sorted_rows(part.T) for part in (mixed_all, norm0, norm1, d_out, mixed_a, norm2, d_agg)]
+                + [d_proj_all, d_qkv_all, d_up, lifted, d_agg, jnp.pad(d_pred, ((0, 0), (0, 256 - WIDTH)))]
+                + [onehot_all, d_table.astype(bf16)]
+                + [sorted_rows(jnp.pad(narrow.T, ((0, 0), (0, 128 - narrow.shape[0])))), sorted_rows(head)],
                 jnp.where(lane == 1, numerator, 0.0),
-                (((0, 0), (1, 2 * D)), ((2, 0), (3, 3 * D)), ((4, 0), (5, FF)), ((6, 0),)),
-                (3 * D, 4 * D, 2 * FF, MISC),
             )
             squares, numerator = stat[0, 0], stat[0, 1]
         else:
-            r_kv, r_out, r_qkv, r_proj, r_up, r_down, r_misc = (
-                lax.psum_scatter(g[0], "dp", scatter_dimension=0, tiled=True) for g in groups
+            d_table, narrow = lax.psum((d_table, narrow), "fsdp")
+            source = jnp.arange(D)
+            pick = (source // strip) % n_f == own
+            place = (source // (strip * n_f)) * strip + source % strip
+            choose = (pick[:, None] & (place[:, None] == jnp.arange(n_dp * strip)[None, :])).astype(bf16)
+
+            def mine(array):
+                whole = array.reshape(n_dp, n_f, strip, array.shape[1])
+                return lax.dynamic_index_in_dim(whole, own, 1, False).reshape(n_dp * strip, array.shape[1])
+
+            def weight_grad(features, grads):
+                return t_mm(mm(features, choose).astype(bf16), grads)
+
+            def gap(width):
+                return jnp.zeros((n_dp * strip, width), f32)
+
+            d_agg_all = ag(d_agg)
+            g_kv = exact("dc,cx->dx", mine(w240).astype(f32), d_table)
+            g_240 = exact("dx,cx->dc", mine(agg_kv).astype(f32), d_table)
+            groups = (
+                (g_kv, weight_grad(ag(mixed_a), d_agg_all)),
+                (weight_grad(ag(norm0), d_qkv_all), weight_grad(mixed_all, d_proj_all)),
+                (weight_grad(ag(norm1), ag(d_up)), weight_grad(ag(d_out), ag(lifted))),
+                (
+                    g_240, weight_grad(ag(norm2), ag(d_pred)), gap(256 - WIDTH),
+                    weight_grad(d_agg_all, onehot_all), mine(narrow.T)[:, :9], gap(256 - 9),
+                ),
             )
-            r_agg = jnp.concatenate([r_kv, r_out], axis=1)
-            r_attn = jnp.concatenate([r_qkv, r_proj], axis=1)
-            r_mlp = jnp.concatenate([r_up, r_down], axis=1)
+            r_agg, r_attn, r_mlp, r_misc = (
+                lax.psum_scatter(jnp.concatenate(g, axis=1), "dp", scatter_dimension=0, tiled=True) for g in groups
+            )
             local_squares = sum(jnp.sum(piece * piece) for piece in (r_agg, r_attn, r_mlp, r_misc))
             squares, numerator = lax.psum((local_squares, numerator), ("dp", "fsdp"))
-        r_io = jnp.concatenate([r_misc[:, :USED], jnp.zeros((strip, w_io.shape[1] - USED), f32)], axis=1)
-        reduced = (r_agg, r_attn, r_mlp, r_io, r_misc[:, USED : USED + 9])
+        r_io = jnp.concatenate(
+            [
+                r_misc[:, :WIDTH], r_misc[:, 256 : 256 + WIDTH], r_misc[:, WIDTH : WIDTH + VARS],
+                r_misc[:, 512 : 512 + SPAN], jnp.zeros((strip, w_io.shape[1] - emb - SPAN), f32),
+            ],
+            axis=1,
+        )
+        reduced = (r_agg, r_attn, r_mlp, r_io, r_misc[:, 768:777])
         grad_norm = jnp.sqrt(squares)
         factor = jnp.minimum(1.0, clip_limit / grad_norm)
         loss = numerator / total

time: 781 us -> 605 us (0.77)
  waiting for transfers between devices: 179 us -> 55.6 us
  matrix products: 154 us -> 86.8 us
  local copies, waits for them, and re-layouts: 49.5 us -> 68.7 us
  blocking collectives: 12.8 us -> 0 us
  Pallas kernels: 309 us -> 321 us
    all_gather x9 -> x1, waiting for transfers between devices: 72.6 us -> 13.5 us  [ag(): return lax.all_gather(part, 'fsdp', axis=0, tiled=True)]
    dot_general x35 -> x14, matrix products: 102 us -> 45.5 us  [dot(): lax.dot_general(left, right, (dims, ((), ())), preferred_element_type=f32)]
    psum x1 -> x0, waiting for transfers between devices: 50.7 us -> none  [local(): lax.psum((jnp.concatenate([d_table_k, d_table_v], axis=1), narrow), 'fsdp')]
    all_gather x2 -> x0, blocking collectives: 12.8 us -> none  [ag(): return lax.all_gather(part, 'fsdp', axis=0, tiled=True)]
    pallas_call x1, Pallas kernels: 166 us -> 177 us  [gradient_blocks(): pl.pallas_call(gradient_kernel, out_shape=[jax.ShapeDtypeStruct((STRIP, w...]
    all_gather x1, waiting for transfers between devices: 28.1 us -> 17.3 us  [local(): lax.all_gather(d_part, 'fsdp', axis=2, tiled=True).reshape(row_len, 3 * D)]
    dot_general x9 -> x5, matrix products: 16.5 us -> 6.98 us  [exact(): jnp.einsum(eq, left, right, precision=highest, preferred_element_type=f32)]
  transfers between devices with their start and end apart: 13 -> 4, of which waited for: 9 -> 4; matrix products, arithmetic and copies ran while one was open for 16% -> 3% of each run, Pallas kernels for 0% -> 0%
where the time goes in v3:
time: 605 us; the launch traced here: 594 us
  Pallas kernels  321 us (53%)
  matrix products  86.8 us (14%)
  local copies, waits for them, and re-layouts  68.7 us (11%)
  waiting for transfers between devices  55.6 us (9%)
  other arithmetic  36.5 us (6%)
  between operations  21.7 us (4%)
    pallas_call x1, Pallas kernels, gradient_blocks(): pl.pallas_call(gradient_kernel, out_shape=[jax.ShapeDtypeStruct((STRIP, w...  177 us
    pallas_call x1, Pallas kernels, gather_weights(): pl.pallas_call(gather_kernel, out_shape=[jax.ShapeDtypeStruct((D, a.shape...  144 us
    dot_general x14, matrix products, dot(): lax.dot_general(left, right, (dims, ((), ())), preferred_element_type=f32)  45.5 us
    all_gather x1, waiting for transfers between devices, local(): lax.all_gather(d_part, 'fsdp', axis=2, tiled=True).reshape(row_len, 3 * D)  17.3 us
    all_gather x1, waiting for transfers between devices, ag(): return lax.all_gather(part, 'fsdp', axis=0, tiled=True)  13.5 us
    all_gather x1, waiting for transfers between devices, local(): mixed_all = lax.all_gather(mixed_h, 'fsdp', axis=1, tiled=True)  13.2 us
  transfers between devices with their start and end apart: 4, of which 4 were waited for; matrix products, arithmetic and copies ran while one was open for 3% of the time, Pallas kernels for 0%

profile of v3, /device:TPU:0, one launch (start us, length us, event | category | flops | bytes accessed | tf_op | source)
XLA Modules:
  0.0 594.5 jit_solution(17700293438111735050)
XLA Ops:
  19.2 144.1 %gather_weights.1 = (bf16[1024,3968]{1,0:T(8,128)(2,1)}, bf16[1024,4096]{1,0:T(8,128)(2,1)}, bf16[1024,8192]{1,0:T(8,128)(2,1)}, f32[8,128]{1,0:T(8,128)}) custom-call(bf16[32,3968]{1,0:T(8,128)(2,1)} %concatenate.25.refs_0_, bf16[32,4096]{1,0:T(8,128)(2,1)} %convert_element_type.187.refs_1_, bf16[32,8192]{1,0:T(8,128)(2,1)} %convert_element_type.188.refs_2_, ...), custom_call_target="tpu_custom_call" | custom-call | tf_op jit(solution)/shard_map/gather_weights/pallas_call | solution.py:232
  164.3 3.6 fusion.23
  168.7 2.7 slice_reduce_fusion.1
  179.7 2.3 fusion.80
  182.1 2.2 fusion.168
  185.1 4.7 fusion.25
  189.8 3.1 reshape.399
  195.1 4.2 all-to-all-start
  199.5 11.4 %all-to-all-done = bf16[128,3,4,256]{3,0,1,2:T(8,128)(2,1)} async-done(((bf16[128,3,4,256]{3,0,1,2:T(8,128)(2,1)}), bf16[128,3,4,256]{3,0,1,2:T(8,128)(2,1)}, u32[]{:S(2)}, u32[]{:S(2)}) %all-to-all-start) | async-done | bytes 786464 | tf_op jit(solution)/shard_map/all_to_all | solution.py:771
  211.0 2.2 copy.207
  213.1 2.3 reshape.400
  215.5 4.7 fusion.169
  220.8 3.5 convolution_convert_fusion.2
  226.4 13.2 %all-gather.4.cloned.1.call-done = bf16[512,1024]{0,1:T(8,128)(2,1)} async-done(((bf16[512,256]{0,1:T(8,128)(2,1)}), bf16[512,1024]{0,1:T(8,128)(2,1)}) %all-gather.4.cloned.1.call-update) | async-done | bytes 1048592 | tf_op jit(solution)/shard_map/all_gather | solution.py:783
  239.6 2.3 fusion.170
  242.2 4.6 multiply_convert_fusion.1
  246.8 7.1 %fusion.171 = (f32[128]{0:T(128)S(1)}, f32[128,1024]{1,0:T(8,128)S(1)}) fusion(f32[128,1024]{1,0:T(8,128)S(1)} %get-tuple-element.220, bf16[128,4096]{1,0:T(8,128)(2,1)S(1)} %get-tuple-element.221.refs_10_, bf16[1024,8192]{1,0:T(8,128)(2,1)} %get-tuple-element.33), kind=kOutput, calls=%fused_computation.242 | convolution fusion | flops 1074003840 | bytes 10486272 | tf_op jit(solution)/shard_map/dot_general | solution.py:38
  260.1 2.3 fusion.19.refs_9_
  262.4 3.6 multiply_reduce_fusion.4
  267.4 3.1 slice.131
  270.5 13.5 %all-gather.6.cloned.1.call-done.refs_7_ = bf16[512,1024]{1,0:T(8,128)(2,1)} async-done(((bf16[128,1024]{1,0:T(8,128)(2,1)}), bf16[512,1024]{1,0:T(8,128)(2,1)}) %all-gather.6.cloned.1.call-update) | async-done | bytes 1048592 | tf_op jit(solution)/shard_map/all_gather | solution.py:668
  286.6 3.6 fusion.111
  290.2 8.4 %fusion.73 = bf16[4,64,512]{2,1,0:T(8,128)(2,1)} fusion(f32[4,512,512]{1,2,0:T(8,128)} %fusion.111, bf16[512,3,4,64]{0,3,2,1:T(8,128)(2,1)} %reshape.400, f32[4,512,512]{1,2,0:T(8,128)} %get-tuple-element.218, f32[4,512]{1,0:T(4,128)S(1)} %copy-done.71), kind=kOutput, calls=%fused_computation.64 | convolution fusion | flops 141691392 | bytes 17317888 | tf_op jit(solution)/shard_map/hqk,hke->qhe/dot_general | solution.py:813
  298.6 8.1 %fusion.76 = bf16[4,64,512]{2,1,0:T(8,128)(2,1)} fusion(f32[4,512,512]{1,2,0:T(8,128)} %fusion.111, bf16[512,3,4,64]{0,3,2,1:T(8,128)(2,1)} %reshape.400, f32[4,512,512]{1,2,0:T(8,128)} %get-tuple-element.218, f32[4,512]{1,0:T(4,128)S(1)} %copy-done.71), kind=kOutput, calls=%fused_computation.65 | convolution fusion | flops 141691392 | bytes 17317888 | tf_op jit(solution)/shard_map/hqk,hqe->khe/dot_general | solution.py:814
  306.7 3.7 convolution_convert_fusion
  329.3 17.3 %all-gather.8.cloned.1.call-done = bf16[512,3,4,256]{3,0,1,2:T(8,128)(2,1)} async-done(((bf16[512,3,1,256]{3,0,1,2:T(8,128)(2,1)}), bf16[512,3,4,256]{3,0,1,2:T(8,128)(2,1)}) %all-gather.8.cloned.1.call-update) | async-done | bytes 3145744 | tf_op jit(solution)/shard_map/all_gather | solution.py:816
  346.6 6.0 %copy.221 = bf16[512,3,4,256]{3,2,1,0:T(4,128)(2,1)} copy(bf16[512,3,4,256]{3,0,1,2:T(8,128)(2,1)} %all-gather.8.cloned.1.call-done) | data formatting | bytes 6291456 | tf_op jit(solution)/shard_map/all_gather | solution.py:816
  352.7 6.6 %reshape.407.refs_8_ = bf16[512,3072]{1,0:T(8,128)(2,1)} reshape(bf16[512,3,4,256]{3,2,1,0:T(4,128)(2,1)} %copy.221) | data formatting | bytes 6291456 | tf_op jit(solution)/shard_map/reshape | solution.py:816
  359.4 6.1 %multiply_reduce_fusion.5 = (f32[1024]{0:T(1024)}, f32[128]{0:T(128)S(1)}, f32[128]{0:T(128)S(1)}, f32[1024]{0:T(1024)}, f32[128,1024]{1,0:T(8,128)S(1)}) fusion(f32[128,1024]{1,0:T(8,128)} %copy-done, f32[128]{0:T(128)S(1)} %copy-done.66, f32[128]{0:T(128)S(1)} %copy-done.62, f32[1024]{0:T(1024)S(1)} %copy-done.45, ...), kind=kOutput, calls=%fused_computation.116 | convolution fusion | flops 806483712 | bytes 8140804 | tf_op jit(solution)/shard_map/dot_general | solution.py:38
  367.1 2.4 fusion.70
  387.4 176.7 %gradient_blocks.1 = (f32[32,3072]{1,0:T(8,128)}, f32[32,4096]{1,0:T(8,128)}, f32[32,8192]{1,0:T(8,128)}, f32[32,1024]{1,0:T(8,128)}, f32[8,128]{1,0:T(8,128)}) custom-call(bf16[4,2,4,32,512]{4,3,2,1,0:T(8,128)(2,1)} %bitcast.170, bf16[4,2,4,32,128]{4,3,2,1,0:T(8,128)(2,1)} %bitcast.174, bf16[4,2,4,32,128]{4,3,2,1,0:T(8,128)(2,1)} %bitcast.171, ...), custom_call_target="tpu_custom_call" | custom-call | tf_op jit(solution)/shard_map/gradient_blocks/pallas_call | solution.py:619
  578.6 3.8 fusion.155
  (272 shorter events, 89.0 us)
Async XLA Ops:
  11.1 152.2 %copy-start.19 = (s32[1,128,192]{2,1,0:T(8,128)}, s32[1,128,192]{2,1,0:T(8,128)S(1)}, u32[]{:S(2)}) copy-start(s32[1,128,192]{2,1,0:T(8,128)S(1)} %copy.200) | copy-start | bytes 294916
  12.0 151.4 %copy-start.55 = (f32[192]{0:T(256)}, f32[192]{0:T(256)S(1)}, u32[]{:S(2)}) copy-start(f32[192]{0:T(256)S(1)} %mul.561) | copy-start | bytes 2308
  168.0 7.1 %copy-start.36 = (s32[256]{0:T(256)}, s32[256]{0:T(256)S(1)}, u32[]{:S(2)}) copy-start(s32[256]{0:T(256)S(1)} %get-tuple-element.227) | copy-start | bytes 3076
  168.0 7.1 %copy-start.39 = (s32[256]{0:T(256)}, s32[256]{0:T(256)S(1)}, u32[]{:S(2)}) copy-start(s32[256]{0:T(256)S(1)} %get-tuple-element.228) | copy-start | bytes 3076
  171.5 13.1 %copy-start.42 = (f32[1024]{0:T(1024)}, f32[1024]{0:T(1024)S(1)}, u32[]{:S(2)}) copy-start(f32[1024]{0:T(1024)S(1)} %get-tuple-element.165) | copy-start | bytes 12292
  171.5 13.1 %copy-start.44 = (f32[1024]{0:T(1024)}, f32[1024]{0:T(1024)S(1)}, u32[]{:S(2)}) copy-start(f32[1024]{0:T(1024)S(1)} %get-tuple-element.166) | copy-start | bytes 12292
  182.0 7.8 %copy-start.5 = (bf16[16,64,128]{2,1,0:T(8,128)(2,1)}, bf16[16,64,128]{2,1,0:T(8,128)(2,1)S(1)}, u32[]{:S(2)}) copy-start(bf16[16,64,128]{2,1,0:T(8,128)(2,1)S(1)} %fusion.80) | copy-start | bytes 786436
  195.1 15.9 %all-to-all-start = ((bf16[128,3,4,256]{3,0,1,2:T(8,128)(2,1)}), bf16[128,3,4,256]{3,0,1,2:T(8,128)(2,1)}, u32[]{:S(2)}, u32[]{:S(2)}) async-start(bf16[128,3,4,256]{3,0,1,2:T(8,128)(2,1)} %copy.206), calls=%async_computation | async-start | bytes 1572864 | tf_op jit(solution)/shard_map/all_to_all | solution.py:771
  199.2 40.3 %all-gather.4.cloned.1.call-start = ((), (), s32[]{:S(2)}) async-start(), calls=%async_computation.1 | async-start | bytes 1310720 | tf_op jit(solution)/shard_map/all_gather | solution.py:783
  224.3 17.8 %copy-start.47 = (f32[1024]{0:T(1024)S(1)}, f32[1024]{0:T(1024)}, u32[]{:S(2)}) copy-start(f32[1024]{0:T(1024)} %get-tuple-element.163) | copy-start | bytes 12292
  224.3 17.8 %copy-start.48 = (f32[1024]{0:T(1024)S(1)}, f32[1024]{0:T(1024)}, u32[]{:S(2)}) copy-start(f32[1024]{0:T(1024)} %get-tuple-element.164) | copy-start | bytes 12292
  224.3 59.7 %all-gather.6.cloned.1.call-start = ((), (), s32[]{:S(2)}) async-start(), calls=%async_computation.2 | async-start | bytes 1310720 | tf_op jit(solution)/shard_map/all_gather | solution.py:668
  242.1 17.9 %slice-start = ((s8[16777216]{0:T(1024)(128)(4,1)}), s8[4194304]{0:T(1024)(128)(4,1)S(1)}, s32[]{:S(2)}) async-start(s8[16777216]{0:T(1024)(128)(4,1)} %bitcast.202), calls=%async_computation.4 | async-start | bytes 8388608
  242.2 17.9 %slice-start.1 = ((s8[16777216]{0:T(1024)(128)(4,1)}), s8[4194304]{0:T(1024)(128)(4,1)S(1)}, s32[]{:S(2)}) async-start(s8[16777216]{0:T(1024)(128)(4,1)} %bitcast.202), calls=%async_computation.5 | async-start | bytes 8388608
  246.7 7.2 %copy-start.13 = (bf16[128,4096]{1,0:T(8,128)(2,1)}, bf16[128,4096]{1,0:T(8,128)(2,1)S(1)}, u32[]{:S(2)}) copy-start(bf16[128,4096]{1,0:T(8,128)(2,1)S(1)} %get-tuple-element.221.refs_10_) | copy-start | bytes 3145732
  246.7 7.4 %copy-start.20 = (s32[1,128,192]{2,1,0:T(8,128)S(1)}, s32[1,128,192]{2,1,0:T(8,128)}, u32[]{:S(2)}) copy-start(s32[1,128,192]{2,1,0:T(8,128)} %copy-done.19) | copy-start | bytes 294916
  246.7 7.4 %copy-start.49 = (f32[1024]{0:T(1024)S(1)}, f32[1024]{0:T(1024)}, u32[]{:S(2)}) copy-start(f32[1024]{0:T(1024)} %get-tuple-element.168) | copy-start | bytes 12292
  246.8 7.4 %copy-start.56 = (f32[192]{0:T(256)S(1)}, f32[192]{0:T(256)}, u32[]{:S(2)}) copy-start(f32[192]{0:T(256)} %copy-done.55) | copy-start | bytes 2308
  246.8 7.4 %copy-start.64 = (f32[1,128]{1,0:T(1,128)S(1)}, f32[1,128]{1,0:T(1,128)}, u32[]{:S(2)}) copy-start(f32[1,128]{1,0:T(1,128)} %param.26) | copy-start | bytes 1540
  246.8 13.3 %slice-start.2 = ((s8[16777216]{0:T(1024)(128)(4,1)}), s8[4194304]{0:T(1024)(128)(4,1)S(1)}, s32[]{:S(2)}) async-start(s8[16777216]{0:T(1024)(128)(4,1)} %bitcast.202), calls=%async_computation.6 | async-start | bytes 8388608
  246.8 13.3 %slice-start.3 = ((s8[16777216]{0:T(1024)(128)(4,1)}), s8[4194304]{0:T(1024)(128)(4,1)S(1)}, s32[]{:S(2)}) async-start(s8[16777216]{0:T(1024)(128)(4,1)} %bitcast.202), calls=%async_computation.7 | async-start | bytes 8388608
  267.1 79.5 %all-gather.8.cloned.1.call-start = ((), (), s32[]{:S(2)}) async-start(), calls=%async_computation.3 | async-start | bytes 3932160 | tf_op jit(solution)/shard_map/all_gather | solution.py:816
  270.5 19.7 %copy-start.71 = (f32[4,512]{1,0:T(4,128)S(1)}, f32[4,512]{1,0:T(4,128)}, u32[]{:S(2)}) copy-start(f32[4,512]{1,0:T(4,128)} %copy-done.70) | copy-start | bytes 24580
  367.1 17.7 %copy-start.6 = (bf16[128,1024]{1,0:T(8,128)(2,1)}, bf16[128,1024]{1,0:T(8,128)(2,1)S(1)}, u32[]{:S(2)}) copy-start(bf16[128,1024]{1,0:T(8,128)(2,1)S(1)} %get-tuple-element.191.refs_11_) | copy-start | bytes 786436
  378.1 8.6 %copy-start.68 = (f32[128]{0:T(128)S(1)}, f32[128]{0:T(128)}, u32[]{:S(2)}) copy-start(f32[128]{0:T(128)} %compare_select_fusion) | copy-start | bytes 1540
  387.3 183.0 %copy-start.27 = (f32[32,9]{1,0:T(8,128)S(1)}, f32[32,9]{1,0:T(8,128)}, u32[]{:S(2)}) copy-start(f32[32,9]{1,0:T(8,128)} %copy.230) | copy-start | bytes 3460
  387.3 183.0 %copy-start.28 = (f32[32,9]{1,0:T(8,128)S(1)}, f32[32,9]{1,0:T(8,128)}, u32[]{:S(2)}) copy-start(f32[32,9]{1,0:T(8,128)} %copy.233) | copy-start | bytes 3460
  387.3 189.3 %copy-start.18 = (f32[32,944]{1,0:T(8,128)S(1)}, f32[32,944]{1,0:T(8,128)}, u32[]{:S(2)}) copy-start(f32[32,944]{1,0:T(8,128)} %param.34) | copy-start | bytes 362500
  387.3 189.3 %copy-start.26 = (f32[32,944]{1,0:T(8,128)S(1)}, f32[32,944]{1,0:T(8,128)}, u32[]{:S(2)}) copy-start(f32[32,944]{1,0:T(8,128)} %param.44) | copy-start | bytes 362500
  387.3 191.2 %copy-start.4 = (f32[32,8192]{1,0:T(8,128)S(1)}, f32[32,8192]{1,0:T(8,128)}, u32[]{:S(2)}) copy-start(f32[32,8192]{1,0:T(8,128)} %param.33) | copy-start | bytes 3145732
  387.4 191.2 %copy-start.11 = (f32[32,8192]{1,0:T(8,128)S(1)}, f32[32,8192]{1,0:T(8,128)}, u32[]{:S(2)}) copy-start(f32[32,8192]{1,0:T(8,128)} %param.43) | copy-start | bytes 3145732
  387.4 191.2 %copy-start.12 = (f32[32,8192]{1,0:T(8,128)S(1)}, f32[32,8192]{1,0:T(8,128)}, u32[]{:S(2)}) copy-start(f32[32,8192]{1,0:T(8,128)} %param.38) | copy-start | bytes 3145732
  (48 other events, 223.9 us)
Sparse Core Ops, SparseCore 0:
  224.4 15.0 all-gather.3
  267.3 16.7 all-gather.5
  318.1 28.5 all-gather.7

commit v4 on v3

--- a/solution.py
+++ b/solution.py
@@ -250,16 +250,219 @@
     )(head, attn, mlp, number)
 
 
-SEGMENTS = ((0, 2, 0), (2, 8, 1), (8, 16, 2), (16, 24, 3), (24, 26, 4))
-N_STD, N_ALL, FIRST_SENT, AHEAD, BASE = 26, 32, 8, 4, 2
+def greet(dp, own):
+    barrier = pltpu.get_barrier_semaphore()
+    for d in range(1, 4):
+        pl.semaphore_signal(barrier, inc=1, device_id=(dp, lax.rem(own + d, 4)), device_id_type=MESH)
+    pl.semaphore_wait(barrier, 3)
+
+
+def turned_softmax(parts, seg_col, seg_row, h):
+    at = slice(h * HEAD_DIM, (h + 1) * HEAD_DIM)
+    q, k, v = (parts[i, :, at] for i in range(3))
+    score = lax.dot_general(k, q, (((1,), (1,)), ((), ())), preferred_element_type=f32) * HEAD_DIM ** (-0.5)
+    score = jnp.where(seg_col[:, 0:1] == seg_row[0:1, :], score, -1000000000.0)
+    power = jnp.exp(score - jnp.max(score, axis=0, keepdims=True))
+    soft = power / jnp.sum(power, axis=0, keepdims=True)
+    return q, k, v, soft, soft.astype(bf16)
+
+
+def attend_kernel(qkv, seg_col, seg_row, mixed, mixed_t, parts_out, parts, turned, whole, gathered,
+                  load_sem, in_send, in_recv, out_send, out_recv):
+    dp, own = lax.axis_index("dp"), lax.axis_index("fsdp")
+    greet(dp, own)
+    row = pl.ds(pl.multiple_of(own * 128, 128), 128)
+
+    def piece(i, to):
+        return qkv.at[:, pl.ds(pl.multiple_of(i * D + to * 256, 256), 256)]
+
+    def into(d, i):
+        to = lax.rem(own + d, 4)
+        return pltpu.make_async_remote_copy(
+            src_ref=piece(i, to), dst_ref=parts.at[i, row, :], send_sem=in_send.at[d, i], recv_sem=in_recv.at[d, i],
+            device_id=(dp, to), device_id_type=MESH,
+        )
+
+    for i in range(3):
+        for d in (2, 1, 3):
+            into(d, i).start()
+    for i in range(3):
+        pltpu.make_async_copy(piece(i, own), parts.at[i, row, :], load_sem.at[i]).start()
+    for i in range(3):
+        pltpu.make_async_copy(piece(i, own), parts.at[i, row, :], load_sem.at[i]).wait()
+        for d in range(1, 4):
+            into(d, i).wait_recv()
+    for h in range(4):
+        q, k, v, soft, share = turned_softmax(parts, seg_col, seg_row, h)
+        turned[h * HEAD_DIM : (h + 1) * HEAD_DIM, :] = lax.dot_general(
+            v, share, (((0,), (0,)), ((), ())), preferred_element_type=f32
+        )
+    whole[...] = turned[...].T.astype(bf16)
+    column = pl.ds(pl.multiple_of(own * 256, 256), 256)
+
+    def back(d):
+        to = lax.rem(own + d, 4)
+        return pltpu.make_async_remote_copy(
+            src_ref=whole.at[pl.ds(pl.multiple_of(to * 128, 128), 128), :], dst_ref=gathered.at[:, column],
+            send_sem=out_send.at[d], recv_sem=out_recv.at[d], device_id=(dp, to), device_id_type=MESH,
+        )
+
+    for d in (2, 1, 3):
+        back(d).start()
+    keep = pltpu.make_async_copy(whole.at[row, :], gathered.at[:, column], load_sem.at[3])
+    keep.start()
+    mixed_t[...] = turned[...].astype(bf16)
+    parts_out[...] = parts[...]
+    keep.wait()
+    for d in range(1, 4):
+        back(d).wait_recv()
+    mixed[...] = gathered[...]
+    for d in range(1, 4):
+        back(d).wait_send()
+        for i in range(3):
+            into(d, i).wait_send()
+
+
+def attend(qkv, seg_col, seg_row):
+    vmem = pl.BlockSpec(memory_space=pltpu.VMEM)
+    dma = pltpu.SemaphoreType.DMA
+    return pl.pallas_call(
+        attend_kernel,
+        out_shape=[
+            jax.ShapeDtypeStruct((128, D), bf16), jax.ShapeDtypeStruct((256, 512), bf16),
+            jax.ShapeDtypeStruct((3, 512, 256), bf16),
+        ],
+        in_specs=[pl.BlockSpec(memory_space=pl.ANY), vmem, vmem],
+        out_specs=[vmem] * 3,
+        scratch_shapes=[
+            pltpu.VMEM((3, 512, 256), bf16), pltpu.VMEM((256, 512), f32), pltpu.VMEM((512, 256), bf16),
+            pltpu.VMEM((128, D), bf16), dma((4,)), dma((4, 3)), dma((4, 3)), dma((4,)), dma((4,)),
+        ],
+        compiler_params=pltpu.CompilerParams(collective_id=2, has_side_effects=True, vmem_limit_bytes=40 * 2**20),
+        name="attend",
+    )(qkv, seg_col, seg_row)
+
+
+def attend_back_kernel(d_proj, attn, parts, seg_col, seg_row, d_own, d_parts_out, d_all_out, every, proj, d_mixed,
+                       d_parts, gathered, load_sem, up_send, up_recv, out_send, out_recv):
+    dp, own = lax.axis_index("dp"), lax.axis_index("fsdp")
+    x, core = own // 2, own % 2
+    sibling, across, diagonal = x * 2 + 1 - core, (1 - x) * 2 + core, (1 - x) * 2 + 1 - core
+    rows = pl.ds(pl.multiple_of(own * 256, 256), 256)
+    fetch = pltpu.make_async_copy(attn.at[rows, pl.ds(3 * D, D)], proj, load_sem.at[0])
+    fetch.start()
+    row = pl.ds(pl.multiple_of(own * 128, 128), 128)
+    mine = pltpu.make_async_copy(d_proj, every.at[row, :], load_sem.at[1])
+    mine.start()
+    greet(dp, own)
+    mine.wait()
+
+    def up(i, who, slot, to):
+        block = every.at[pl.ds(pl.multiple_of(who * 128, 128), 128), i * 512 : (i + 1) * 512]
+        return pltpu.make_async_remote_copy(
+            src_ref=block, dst_ref=block, send_sem=up_send.at[i, slot], recv_sem=up_recv.at[i, who],
+            device_id=(dp, to), device_id_type=MESH,
+        )
+
+    for i in range(2):
+        up(i, own, 0, across).start()
+    for i in range(2):
+        up(i, own, 1, sibling).start()
+    for i in range(2):
+        up(i, across, 0, own).wait_recv()
+        up(i, across, 2, sibling).start()
+    fetch.wait()
+    for i in range(2):
+        up(i, sibling, 1, own).wait_recv()
+        up(i, diagonal, 2, own).wait_recv()
+    d_mixed[...] = lax.dot_general(
+        every[...], proj[...], (((1,), (1,)), ((), ())), preferred_element_type=f32
+    ).astype(bf16)
+    for h in range(4):
+        at = slice(h * HEAD_DIM, (h + 1) * HEAD_DIM)
+        q, k, v, soft, share = turned_softmax(parts, seg_col, seg_row, h)
+        d_head = d_mixed[:, at]
+        d_soft = lax.dot_general(v, d_head, (((1,), (1,)), ((), ())), preferred_element_type=f32)
+        lean = jnp.sum(soft * d_soft, axis=0, keepdims=True)
+        d_score = (soft * (d_soft - lean) * HEAD_DIM ** (-0.5)).astype(bf16)
+        d_parts[2, :, at] = mm(share, d_head).astype(bf16)
+        d_parts[1, :, at] = mm(d_score, q).astype(bf16)
+        d_parts[0, :, at] = t_mm(d_score, k).astype(bf16)
+
+    def back(d, i):
+        to = lax.rem(own + d, 4)
+        return pltpu.make_async_remote_copy(
+            src_ref=d_parts.at[i, pl.ds(pl.multiple_of(to * 128, 128), 128), :],
+            dst_ref=gathered.at[:, pl.ds(pl.multiple_of(i * D + own * 256, 256), 256)],
+            send_sem=out_send.at[d, i], recv_sem=out_recv.at[d, i], device_id=(dp, to), device_id_type=MESH,
+        )
+
+    for i in range(3):
+        for d in (2, 1, 3):
+            back(d, i).start()
+    keeps = [
+        pltpu.make_async_copy(
+            d_parts.at[i, row, :], gathered.at[:, pl.ds(pl.multiple_of(i * D + own * 256, 256), 256)], load_sem.at[2 + i]
+        )
+        for i in range(3)
+    ]
+    for keep in keeps:
+        keep.start()
+    d_parts_out[...] = d_parts[...]
+    d_all_out[...] = every[...]
+    for keep in keeps:
+        keep.wait()
+    for i in range(3):
+        for d in range(1, 4):
+            back(d, i).wait_recv()
+    d_own[...] = gathered[...]
+    for d in range(1, 4):
+        for i in range(3):
+            back(d, i).wait_send()
+    for i in range(2):
+        for slot, who in ((0, own), (1, own), (2, across)):
+            up(i, who, slot, own).wait_send()
+
+
+def attend_back(d_proj, attn, parts, seg_col, seg_row):
+    vmem = pl.BlockSpec(memory_space=pltpu.VMEM)
+    any_space = pl.BlockSpec(memory_space=pl.ANY)
+    dma = pltpu.SemaphoreType.DMA
+    return pl.pallas_call(
+        attend_back_kernel,
+        out_shape=[
+            jax.ShapeDtypeStruct((128, 3 * D), bf16), jax.ShapeDtypeStruct((3, 512, 256), bf16),
+            jax.ShapeDtypeStruct((512, D), bf16),
+        ],
+        in_specs=[any_space, any_space, vmem, vmem, vmem],
+        out_specs=[vmem] * 3,
+        scratch_shapes=[
+            pltpu.VMEM((512, D), bf16), pltpu.VMEM((256, D), bf16), pltpu.VMEM((512, 256), bf16),
+            pltpu.VMEM((3, 512, 256), bf16), pltpu.VMEM((128, 3 * D), bf16),
+            dma((5,)), dma((2, 3)), dma((2, 4)), dma((4, 3)), dma((4, 3)),
+        ],
+        compiler_params=pltpu.CompilerParams(collective_id=3, has_side_effects=True, vmem_limit_bytes=40 * 2**20),
+        name="attend_back",
+    )(d_proj, attn, parts, seg_col, seg_row)
+
+
+SEGMENTS = ((0, 8, 0), (8, 16, 1), (16, 22, 2), (22, 24, 3), (24, 26, 4))
+N_STD, N_ALL, SHIFT, BASE = 26, 32, 2, 2
+
+
+FAR = ({2: 0, 3: 1}, {0: 0, 1: 1})
+
+
+def preds_at(preds, who):
+    return preds.at[pl.ds(pl.multiple_of(who * 128, 128), 128), :]
 
 
 def gradient_kernel(*refs):
-    (mixed_t, norm0_t, norm1_t, out_t, mixa_t, norm2_t, agg_t,
-     d_proj, d_qkv, d_up, lifted, d_agg, d_pred, onehot, d_table, narrow, head, num_ref) = refs[:18]
+    (norm1_t, out_t, norm0_t, mixed_t, mixa_t, norm2_t, agg_t,
+     d_proj, d_parts, d_up, lifted, d_agg, d_pred, onehot, d_table, narrow, head, num_ref) = refs[:18]
     r_agg, r_attn, r_mlp, r_misc, stat_ref = refs[18:23]
-    (feats, ys, tabs, preds, hots, narrows, w240, wkv, acc240, own_buf, give_buf, got, rise, fall, tally, quad_buf,
-     line_buf, load_sem, feat_send, feat_recv, y_xsend, y_xrecv, tab_send, tab_recv, pred_send, pred_recv,
+    (feats, ys, tabs, pairs, preds, hots, narrows, w240, wkv, acc240, own_buf, give_buf, got, rise, fall, far, tally,
+     quad_buf, line_buf, load_sem, feat_send, feat_recv, y_xsend, y_xrecv, part_send, part_recv, tab_send, tab_recv, pred_send, pred_recv,
      nar_send, nar_recv, y_send, y_recv, z_send, z_recv, s_send, s_recv) = refs[23:]
     dp, own = lax.axis_index("dp"), lax.axis_index("fsdp")
     z, y, x, core = dp // 2, dp % 2, own // 2, own % 2
@@ -273,97 +476,129 @@
     pl.semaphore_wait(barrier, 10)
     n = N_ALL
     row = pl.ds(pl.multiple_of(own * 128, 128), 128)
-    sent_feats = (norm0_t, norm1_t, out_t, mixa_t, norm2_t, agg_t)
+    sent_feats = {0: norm1_t, 1: out_t, 2: norm0_t, 4: mixa_t, 5: norm2_t, 6: agg_t}
 
     def remote(src, dst, send, recv, to):
         return pltpu.make_async_remote_copy(
             src_ref=src, dst_ref=dst, send_sem=send, recv_sem=recv, device_id=(dp, to), device_id_type=MESH
         )
 
-    loads = []
-
-    def load(src, dst):
+    def feat_copy(k, d, half, to):
+        side = y if half == 0 else 1 - y
+        if k == 3:
+            src, dst = mixed_t.at[side, to], feats.at[3, half, own]
+        else:
+            src, dst = sent_feats[k].at[:, side, to], feats.at[k, half, :, :, row]
+        return remote(src, dst, feat_send.at[k, d, half], feat_recv.at[k, d, half], to)
+
+    def feat_start(k):
+        for d in (2, 1, 3):
+            for half in range(2):
+                feat_copy(k, d, half, lax.rem(own + d, 4)).start()
+
+    def unit_block(c, who):
+        return ys.at[c, pl.ds(pl.multiple_of(who * 128, 128), 128), :]
+
+    def unit(c, who, slot, to):
+        return remote(unit_block(c, who), unit_block(c, who), y_xsend.at[c, slot], y_xrecv.at[c, who], to)
+
+    def part_block(i, who):
+        return ys.at[16 + i * 2 + who // 2, :, pl.ds(pl.multiple_of((who % 2) * 256, 256), 256)]
+
+    def part(i, who, slot, to):
+        return remote(part_block(i, who), part_block(i, who), part_send.at[i, slot], part_recv.at[i, who], to)
+
+    def table_raw(v, to):
+        return remote(tabs.at[0, v], tabs.at[1, v], tab_send.at[v, 0], tab_recv.at[v, 0], to)
+
+    def table(v, who, slot, to):
+        return remote(pairs.at[who, v], pairs.at[who, v], tab_send.at[v, slot], tab_recv.at[v, 1 + who], to)
+
+    def pred_copy(d, who, to):
+        return remote(preds_at(preds, who), preds_at(preds, who), pred_send.at[d], pred_recv.at[d], to)
+
+    def narrow_copy(d, who, to):
+        return remote(narrows.at[who], narrows.at[who], nar_send.at[d], nar_recv.at[d], to)
+
+    loads = {}
+
+    def load(name, src, dst):
         copy = pltpu.make_async_copy(src, dst, load_sem.at[len(loads)])
         copy.start()
-        loads.append(copy)
-
-    def feat_send_all(k, d):
-        to = lax.rem(own + d, 4)
+        loads[name] = copy
+
+    for c in range(8):
+        load(("u", c), d_up.at[:, pl.ds(c * CHUNK, CHUNK)], unit_block(c, own))
+    for c in range(8):
+        load(("u", 8 + c), lifted.at[:, pl.ds(c * CHUNK, CHUNK)], unit_block(8 + c, own))
+    for i in range(3):
+        load(("p", i), d_parts.at[i], part_block(i, own))
+    for c in range(2):
+        load(("u", 24 + c), d_agg.at[:, pl.ds(c * CHUNK, CHUNK)], unit_block(24 + c, own))
+    for v in range(4):
+        load(("t", v), d_table.at[:, pl.ds(v * CHUNK, CHUNK)], tabs.at[0, v])
+    load("pred", d_pred, preds_at(preds, own))
+    load("narrow", narrow, narrows.at[own])
+    count = len(loads)
+    for k in range(7):
         for half in range(2):
             side = y if half == 0 else 1 - y
-            remote(
-                sent_feats[k].at[:, side, to], feats.at[k + 1, half, :, :, row], feat_send.at[k, d, half],
-                feat_recv.at[k, d, half], to,
-            ).start()
-
-    for k in range(6):
-        for d in range(1, 4):
-            feat_send_all(k, d)
-    for half in range(2):
-        load(mixed_t.at[:, y if half == 0 else 1 - y, own], feats.at[0, half])
+            if k == 3:
+                load(("f", k, half), mixed_t.at[side, own], feats.at[3, half, own])
+            else:
+                load(("f", k, half), sent_feats[k].at[:, side, own], feats.at[k, half, :, :, row])
     for c in range(2):
-        load(d_proj.at[:, pl.ds(c * CHUNK, CHUNK)], ys.at[c])
-    for k in range(6):
-        for half in range(2):
-            load(sent_feats[k].at[:, y if half == 0 else 1 - y, own], feats.at[k + 1, half, :, :, row])
-    for c in range(6):
-        load(d_qkv.at[:, pl.ds(c * CHUNK, CHUNK)], ys.at[2 + c])
-    staged = len(loads)
-    for source, width, at in ((d_up, FF, 8), (lifted, FF, 16), (d_agg, D, 24)):
-        for c in range(width // CHUNK):
-            load(source.at[:, pl.ds(c * CHUNK, CHUNK)], ys.at[at + c, row, :])
-    for v in range(4):
-        load(d_table.at[:, pl.ds(v * CHUNK, CHUNK)], tabs.at[v, own])
-    load(d_pred, preds.at[row, :])
-    load(onehot, hots)
+        load(("j", c), d_proj.at[:, pl.ds(c * CHUNK, CHUNK)], ys.at[22 + c])
+    load("hot", onehot, hots)
     for half in range(2):
         side = y if half == 0 else 1 - y
-        load(narrow.at[:, side, own], narrows.at[own, half])
-        load(head.at[:, side, own, :, pl.ds(0, 256)], w240.at[half])
-        load(head.at[:, side, own, :, pl.ds(HEAD, 2 * D)], wkv.at[half])
-
-    def unit(u, who, slot, to):
-        block = ys.at[FIRST_SENT + u, pl.ds(pl.multiple_of(who * 128, 128), 128), :]
-        return remote(block, block, y_xsend.at[u, slot], y_xrecv.at[u, who], to)
-
-    def table(v, who, slot, to):
-        return remote(tabs.at[v, who], tabs.at[v, who], tab_send.at[v, slot], tab_recv.at[v, who], to)
-
-    for copy in loads[staged:]:
-        copy.wait()
-
-    def begin(u, carry):
-        unit(u, own, 0, across).start()
-        unit(u, own, 1, sibling).start()
-        return carry
-
-    lax.fori_loop(0, N_STD - FIRST_SENT, begin, 0)
-    for v in range(4):
-        table(v, own, 0, across).start()
-        table(v, own, 1, sibling).start()
-
-    def pred_copy(d, who, to):
-        block = preds.at[pl.ds(pl.multiple_of(who * 128, 128), 128), :]
-        return remote(block, block, pred_send.at[d], pred_recv.at[d], to)
-
-    def narrow_copy(d, half, who, to):
-        side = y if half == 0 else 1 - y
-        return remote(narrow.at[:, side, to], narrows.at[who, half], nar_send.at[d, half], nar_recv.at[d, half], to)
-
-    for d in range(1, 4):
+        load(("w", half), head.at[:, side, own, :, pl.ds(0, 256)], w240.at[half])
+        load(("k", half), head.at[:, side, own, :, pl.ds(HEAD, 2 * D)], wkv.at[half])
+    feat_start(0)
+    names = list(loads)
+    for name in names[:count]:
+        loads[name].wait()
+
+    def begin(first):
+        def body(c, carry):
+            unit(c, own, 0, across).start()
+            unit(c, own, 1, sibling).start()
+            return carry
+
+        return body
+
+    lax.fori_loop(0, 8, begin(0), 0)
+    feat_start(1)
+    lax.fori_loop(8, 16, begin(8), 0)
+    feat_start(2)
+    for i in range(3):
+        part(i, own, 0, across).start()
+        part(i, own, 1, sibling).start()
+    feat_start(3)
+    feat_start(4)
+    lax.fori_loop(24, 26, begin(24), 0)
+    for w in range(2):
+        table_raw((1 - core) * 2 + w, sibling).start()
+    feat_start(5)
+    feat_start(6)
+    for d in (2, 1, 3):
         pred_copy(d, own, lax.rem(own + d, 4)).start()
-        for half in range(2):
-            narrow_copy(d, half, own, lax.rem(own + d, 4)).start()
-    for copy in loads[:staged]:
-        copy.wait()
+        narrow_copy(d, own, lax.rem(own + d, 4)).start()
+    for name in names[count:]:
+        loads[name].wait()
     tally[...] = jnp.zeros_like(tally)
     acc240[...] = jnp.zeros_like(acc240)
+    for w in range(2):
+        v = core * 2 + w
+        table_raw(v, own).wait_recv()
+        pairs[x, v] = (tabs[0, v].astype(f32) + tabs[1, v].astype(f32)).astype(bf16)
+        table(v, x, 1, across).start()
+        table(v, x, 2, sibling).start()
 
     def feat_wait(k):
         for d in range(1, 4):
             for half in range(2):
-                place = feats.at[k + 1, half, :, :, row]
-                remote(place, place, feat_send.at[k, d, half], feat_recv.at[k, d, half], own).wait_recv()
+                feat_copy(k, d, half, own).wait_recv()
 
     def put(c, value):
         own_buf[c] = value[:128]
@@ -380,27 +615,34 @@
         return high, (value - high.astype(f32)).astype(bf16)
 
     def summed_table(v):
-        total = tabs[v, 0].astype(f32) + tabs[v, 1].astype(f32)
-        return two(total + tabs[v, 2].astype(f32) + tabs[v, 3].astype(f32))
+        return two(pairs[0, v].astype(f32) + pairs[1, v].astype(f32))
 
     def compute(c):
+        for i in range(3):
+            @pl.when(c == 16 + i * 2)
+            def _():
+                part(i, sibling, 1, own).wait_recv()
+                part(i, diagonal, 2, own).wait_recv()
+
         for low, high, k in SEGMENTS:
-            if k > 0:
-                pl.when(c == low)(functools.partial(feat_wait, k - 1))
+            pl.when(c == low)(functools.partial(feat_wait, k))
 
             @pl.when((c >= low) & (c < high))
             def _():
-                if low >= FIRST_SENT:
-                    u = c - FIRST_SENT
-                    unit(u, sibling, 1, own).wait_recv()
-                    unit(u, diagonal, 2, own).wait_recv()
+                if k in (0, 1, 4):
+                    unit(c, sibling, 1, own).wait_recv()
+                    unit(c, diagonal, 2, own).wait_recv()
                 put(c, matmul(feature(k), ys[c]))
 
         @pl.when((c >= N_STD) & (c < N_STD + 4))
         def _():
             v = c - N_STD
-            table(v, sibling, 1, own).wait_recv()
-            table(v, diagonal, 2, own).wait_recv()
+
+            @pl.when(v // 2 != core)
+            def _():
+                table(v, x, 2, own).wait_recv()
+                table(v, 1 - x, 3, own).wait_recv()
+
             high, low = summed_table(v)
             rows = w240[...].reshape(256, 256)
             put(c, matmul(rows, high) + matmul(rows, low))
@@ -419,7 +661,7 @@
 
         @pl.when(c == N_STD + 4)
         def _():
-            feat_wait(4)
+            feat_wait(5)
             for d in range(1, 4):
                 pred_copy(d, lax.rem(own + 4 - d, 4), own).wait_recv()
             value = matmul(feature(5), preds[...])
@@ -430,13 +672,27 @@
 
         @pl.when(c == N_STD + 5)
         def _():
-            feat_wait(5)
+            feat_wait(6)
             for d in range(1, 4):
-                for half in range(2):
-                    place = narrows.at[lax.rem(own + 4 - d, 4), half]
-                    remote(place, place, nar_send.at[d, half], nar_recv.at[d, half], own).wait_recv()
+                narrow_copy(d, lax.rem(own + 4 - d, 4), own).wait_recv()
             value = matmul(feature(6), hots[...])
-            small = ((narrows[0] + narrows[1]) + (narrows[2] + narrows[3])).reshape(256, 128)
+            place = lax.broadcasted_iota(jnp.int32, (256, D), 0)
+            source = lax.broadcasted_iota(jnp.int32, (256, D), 1)
+            side = jnp.where(place < 128, y, 1 - y)
+            wanted = ((place >> 5) & 3) * 256 + side * 128 + own * STRIP + (place & 31)
+            choose = jnp.where(source == wanted, 1.0, 0.0).astype(bf16)
+            total = (narrows[0] + narrows[1]) + (narrows[2] + narrows[3])
+            total = jnp.concatenate([total, jnp.zeros((112, D), f32)], axis=0)
+            high = total.astype(bf16)
+            rest = total - high.astype(f32)
+            middle = rest.astype(bf16)
+            low = (rest - middle.astype(f32)).astype(bf16)
+            dims = (((1,), (1,)), ((), ()))
+            small = (
+                lax.dot_general(choose, high, dims, preferred_element_type=f32)
+                + lax.dot_general(choose, middle, dims, preferred_element_type=f32)
+                + lax.dot_general(choose, low, dims, preferred_element_type=f32)
+            )
             empty = jnp.zeros((128, 128), f32)
             own_buf[c, :, 0:256] = value[:128]
             own_buf[c, :, 256:384] = small[:128]
@@ -458,6 +714,13 @@
             device_id=(to * 2 + y, own), device_id_type=MESH,
         )
 
+    def far_hop(way, c, b, to):
+        at = FAR[way][b]
+        return pltpu.make_async_remote_copy(
+            src_ref=far.at[way, c, at], dst_ref=far.at[way, c, at], send_sem=z_send.at[way, c, 3 + at],
+            recv_sem=z_recv.at[way, c, 3 + at], device_id=(to * 2 + y, own), device_id_type=MESH,
+        )
+
     def here(c, b):
         at = pl.ds(b * STRIP, STRIP)
         return own_buf[c, at, :] + got[c, at, :].astype(f32)
@@ -465,33 +728,41 @@
     early, late = LAG * jnp.minimum(z, 3 - z), LAG * jnp.maximum(z, 3 - z)
 
     def step(t, carry):
-        u = t - AHEAD
-
-        @pl.when((u >= 0) & (u < N_STD - FIRST_SENT))
+        @pl.when(t < 16)
         def _():
-            unit(u, across, 0, own).wait_recv()
-            unit(u, across, 2, sibling).start()
-
-        v = u - (N_STD - FIRST_SENT)
-
-        @pl.when((v >= 0) & (v < 4))
+            unit(t, across, 0, own).wait_recv()
+            unit(t, across, 2, sibling).start()
+
+        for i in range(3):
+            @pl.when(t == 16 + i)
+            def _():
+                part(i, across, 0, own).wait_recv()
+                part(i, across, 2, sibling).start()
+
+        @pl.when((t == 19) | (t == 20))
         def _():
-            table(v, across, 0, own).wait_recv()
-            table(v, across, 2, sibling).start()
-
-        @pl.when(t < n)
+            unit(t + 5, across, 0, own).wait_recv()
+            unit(t + 5, across, 2, sibling).start()
+
+        @pl.when((t == 21) | (t == 22))
         def _():
-            compute(t)
-            cross(t).start()
-
-        first = t - BASE - early
+            v = core * 2 + t - 21
+            table(v, 1 - x, 1, own).wait_recv()
+            table(v, 1 - x, 3, sibling).start()
+
+        @pl.when((t >= SHIFT) & (t < n + SHIFT))
+        def _():
+            compute(t - SHIFT)
+            cross(t - SHIFT).start()
+
+        first = t - SHIFT - BASE - early
 
         @pl.when((first >= 0) & (first < n))
         def _():
             cross(first).wait()
 
         for way, buf, lag, to, back in ((0, rise, LAG * z, z + 1, z - 1), (1, fall, LAG * (3 - z), z - 1, z + 1)):
-            c = t - BASE - lag
+            c = t - SHIFT - BASE - lag
 
             @pl.when((c >= 0) & (c < n))
             def _():
@@ -501,22 +772,51 @@
 
                     @pl.when(beyond & (lag == 0))
                     def _():
-                        buf[c, at] = here(c, b)
+                        if b == (1 if way == 0 else 2):
+                            buf[c, at] = here(c, b)
+                        else:
+                            far[way, c, FAR[way][b]] = here(c, b).astype(bf16)
 
                     @pl.when(beyond & (lag > 0))
                     def _():
-                        hop(buf, way, c, b, back).wait_recv()
-                        buf[c, at] = buf[c, at] + here(c, b)
+                        if b == (1 if way == 0 else 2):
+                            hop(buf, way, c, b, back).wait_recv()
+                            buf[c, at] = buf[c, at] + here(c, b)
+                        else:
+                            @pl.when(lag == LAG)
+                            def _():
+                                far_hop(way, c, b, back).wait_recv()
+                                buf[c, at] = far[way, c, FAR[way][b]].astype(f32) + here(c, b)
+
+                            @pl.when(lag > LAG)
+                            def _():
+                                hop(buf, way, c, b, back).wait_recv()
+                                buf[c, at] = buf[c, at] + here(c, b)
+
+                    def send(c, act):
+                        if b == (1 if way == 0 else 2):
+                            copy = hop(buf, way, c, b, to)
+                            copy.start() if act else copy.wait_send()
+                        else:
+                            @pl.when(lag == 0)
+                            def _():
+                                copy = far_hop(way, c, b, to)
+                                copy.start() if act else copy.wait_send()
+
+                            @pl.when(lag > 0)
+                            def _():
+                                copy = hop(buf, way, c, b, to)
+                                copy.start() if act else copy.wait_send()
 
                     @pl.when(beyond & (c >= QUEUE))
                     def _():
-                        hop(buf, way, c - QUEUE, b, to).wait_send()
+                        send(c - QUEUE, False)
 
                     @pl.when(beyond)
                     def _():
-                        hop(buf, way, c, b, to).start()
-
-        last = t - BASE - late
+                        send(c, True)
+
+        last = t - SHIFT - BASE - late
 
         @pl.when((last >= 0) & (last < n))
         def _():
@@ -545,7 +845,7 @@
 
         return carry
 
-    lax.fori_loop(0, n + BASE + 3 * LAG, step, 0)
+    lax.fori_loop(0, n + SHIFT + BASE + 3 * LAG, step, 0)
     summed = jnp.sum(tally[...])
     lane = lax.broadcasted_iota(jnp.int32, (8, 128), 1)
     quad_buf[own] = jnp.where(lane == 0, summed, jnp.where(lane == 1, num_ref[...], 0.0))
@@ -559,7 +859,7 @@
     for d in range(1, 4):
         share(quad_buf, d, (dp, lax.rem(own + d, 4)), own).start()
     for out, base, low, high in (
-        (r_attn, 3 * D, 0, 2), (r_attn, 0, 2, 8), (r_mlp, 0, 8, 24), (r_agg, 2 * D, 24, 26), (r_agg, 0, 26, 30),
+        (r_mlp, 0, 0, 16), (r_attn, 0, 16, 22), (r_attn, 3 * D, 22, 24), (r_agg, 2 * D, 24, 26), (r_agg, 0, 26, 30),
         (r_misc, 0, 30, 32),
     ):
         for c in range(low, high):
@@ -579,31 +879,38 @@
         share(quad_buf, d, (dp, own), own).wait_send()
     for d in range(1, 8):
         share(line_buf, 3 + d, (dp, own), dp).wait_send()
-    for k in range(6):
-        for d in range(1, 4):
+    for d in range(1, 4):
+        for k in range(7):
             for half in range(2):
-                place = feats.at[k + 1, half, :, :, row]
-                remote(place, place, feat_send.at[k, d, half], feat_recv.at[k, d, half], own).wait_send()
-    for d in range(1, 4):
+                feat_copy(k, d, half, own).wait_send()
         pred_copy(d, own, own).wait_send()
-        for half in range(2):
-            narrow_copy(d, half, own, own).wait_send()
-    for v in range(4):
-        for slot, who in ((0, own), (1, own), (2, across)):
-            table(v, who, slot, own).wait_send()
-
-    def finish(u, carry):
-        for slot, who in ((0, own), (1, own), (2, across)):
-            unit(u, who, slot, own).wait_send()
+        narrow_copy(d, own, own).wait_send()
+    for w in range(2):
+        table_raw((1 - core) * 2 + w, own).wait_send()
+        for slot, who in ((1, x), (2, x), (3, 1 - x)):
+            table(core * 2 + w, who, slot, own).wait_send()
+    relays = ((0, own), (1, own), (2, across))
+    for i in range(3):
+        for slot, who in relays:
+            part(i, who, slot, own).wait_send()
+
+    def finish(c, carry):
+        for slot, who in relays:
+            unit(c, who, slot, own).wait_send()
         return carry
 
-    lax.fori_loop(0, N_STD - FIRST_SENT, finish, 0)
+    lax.fori_loop(0, 16, finish, 0)
+    lax.fori_loop(24, 26, finish, 0)
 
     def drain(c, carry):
-        for b in (1, 2, 3):
-            pl.when(b > z)(lambda: hop(rise, 0, c, b, z).wait_send())
-        for b in (0, 1, 2):
-            pl.when(b < z)(lambda: hop(fall, 1, c, b, z).wait_send())
+        for way, buf, inner, outer in ((0, rise, z > 0, z == 0), (1, fall, z < 3, z == 3)):
+            for b in ((1, 2, 3) if way == 0 else (0, 1, 2)):
+                beyond = (b > z) if way == 0 else (b < z)
+                if b == (1 if way == 0 else 2):
+                    pl.when(beyond)(lambda: hop(buf, way, c, b, z).wait_send())
+                else:
+                    pl.when(beyond & inner)(lambda: hop(buf, way, c, b, z).wait_send())
+                    pl.when(beyond & outer)(lambda: far_hop(way, c, b, z).wait_send())
         return carry
 
     lax.fori_loop(n - QUEUE, n, drain, 0)
@@ -613,7 +920,6 @@
     any_space = pl.BlockSpec(memory_space=pl.ANY)
     vmem = pl.BlockSpec(memory_space=pltpu.VMEM)
     n = N_ALL
-    units = N_STD - FIRST_SENT
     dma = pltpu.SemaphoreType.DMA
     widths = (3 * D, 4 * D, 2 * FF, 2 * CHUNK)
     return pl.pallas_call(
@@ -624,10 +930,11 @@
         scratch_shapes=[
             pltpu.VMEM((7, 2, 4, STRIP, 512), bf16),
             pltpu.VMEM((N_STD, 512, CHUNK), bf16),
-            pltpu.VMEM((4, 4, 256, CHUNK), bf16),
+            pltpu.VMEM((2, 4, 256, CHUNK), bf16),
+            pltpu.VMEM((2, 4, 256, CHUNK), bf16),
             pltpu.VMEM((512, 256), bf16),
             pltpu.VMEM((512, 256), bf16),
-            pltpu.VMEM((4, 2, 4, STRIP, 128), f32),
+            pltpu.VMEM((4, 16, D), f32),
             pltpu.VMEM((2, 4, STRIP, 256), bf16),
             pltpu.VMEM((2, 4, STRIP, 2 * D), bf16),
             pltpu.VMEM((256, 256), f32),
@@ -636,29 +943,32 @@
             pltpu.VMEM((n, 4 * STRIP, CHUNK), bf16),
             pltpu.VMEM((n, 3, STRIP, CHUNK), f32),
             pltpu.VMEM((n, 3, STRIP, CHUNK), f32),
+            pltpu.VMEM((2, n, 2, STRIP, CHUNK), bf16),
             pltpu.VMEM((8, 128), f32),
             pltpu.VMEM((4, 8, 128), f32),
             pltpu.VMEM((8, 8, 128), f32),
             dma((56,)),
-            dma((6, 4, 2)),
-            dma((6, 4, 2)),
-            dma((units, 3)),
-            dma((units, 4)),
+            dma((7, 4, 2)),
+            dma((7, 4, 2)),
+            dma((N_STD, 3)),
+            dma((N_STD, 4)),
+            dma((3, 3)),
+            dma((3, 4)),
+            dma((4, 4)),
             dma((4, 3)),
-            dma((4, 4)),
             dma((4,)),
             dma((4,)),
-            dma((4, 2)),
-            dma((4, 2)),
+            dma((4,)),
+            dma((4,)),
             dma((n,)),
             dma((n,)),
-            dma((2, n, 3)),
-            dma((2, n, 3)),
+            dma((2, n, 5)),
+            dma((2, n, 5)),
             dma((11,)),
             dma((11,)),
         ],
         compiler_params=pltpu.CompilerParams(
-            collective_id=1, has_side_effects=True, vmem_limit_bytes=60 * 2**20
+            collective_id=1, has_side_effects=True, vmem_limit_bytes=62 * 2**20
         ),
         name="gradient_blocks",
     )(*operands, numbers)
@@ -736,7 +1046,7 @@
         w240 = head[:, :MIX]
         w_pred = head[:, 256 : 256 + WIDTH]
         w_pos = head[:, 512 : 512 + SPAN]
-        small = head[:, 768:777].astype(f32).T
+        small = lax.optimization_barrier(head[:, 768:896])[:, :9].astype(f32).T
         agg_kv = head[:, HEAD : HEAD + 2 * D]
         agg_out = head[:, HEAD + 2 * D :]
         w_qkv = attn[:, : 3 * D]
@@ -767,21 +1077,26 @@
         h0 = mm(mixed_a, agg_out) + mm_t(onehot, w_pos) + lead_embed[None]
         norm0, unit0, scale0 = norm_forward(h0, small[1], small[2])
         qkv = mm(norm0, w_qkv).astype(bf16)
-        part = qkv.reshape(rows, 3, n_f, wide)
-        part = lax.all_to_all(part, "fsdp", split_axis=2, concat_axis=0, tiled=True)
-        part = part.reshape(row_len, 3, heads_here, HEAD_DIM)
-        q, k, v = (part[:, i].transpose(1, 0, 2) for i in range(3))
-        att_score = jnp.einsum("hqe,hke->hqk", q, k, preferred_element_type=f32) * HEAD_DIM ** (-0.5)
-        same = seg[:, None] == seg[None, :]
-        att_score = jnp.where(same[None], att_score, -1000000000.0)
-        att_top = jnp.max(att_score, axis=-1, keepdims=True)
-        att_power = jnp.exp(att_score - att_top)
-        att_soft = att_power / jnp.sum(att_power, axis=-1, keepdims=True)
-        att = att_soft.astype(bf16)
-        mixed_h = jnp.einsum("hqk,hke->qhe", att, v, preferred_element_type=f32)
-        mixed_h = mixed_h.reshape(row_len, wide).astype(bf16)
-        mixed_all = lax.all_gather(mixed_h, "fsdp", axis=1, tiled=True)
-        mixed = lax.dynamic_slice_in_dim(mixed_all, own * rows, rows, axis=0)
+        if fast:
+            seg_col = jnp.broadcast_to(seg[:, None], (row_len, 128))
+            seg_row = jnp.broadcast_to(seg[None, :], (8, row_len))
+            mixed, mixed_t, parts = attend(qkv, seg_col, seg_row)
+        else:
+            part = qkv.reshape(rows, 3, n_f, wide)
+            part = lax.all_to_all(part, "fsdp", split_axis=2, concat_axis=0, tiled=True)
+            part = part.reshape(row_len, 3, heads_here, HEAD_DIM)
+            q, k, v = (part[:, i].transpose(1, 0, 2) for i in range(3))
+            att_score = jnp.einsum("hqe,hke->hqk", q, k, preferred_element_type=f32) * HEAD_DIM ** (-0.5)
+            same = seg[:, None] == seg[None, :]
+            att_score = jnp.where(same[None], att_score, -1000000000.0)
+            att_top = jnp.max(att_score, axis=-1, keepdims=True)
+            att_power = jnp.exp(att_score - att_top)
+            att_soft = att_power / jnp.sum(att_power, axis=-1, keepdims=True)
+            att = att_soft.astype(bf16)
+            mixed_h = jnp.einsum("hqk,hke->qhe", att, v, preferred_element_type=f32)
+            mixed_h = mixed_h.reshape(row_len, wide).astype(bf16)
+            mixed_all = lax.all_gather(mixed_h, "fsdp", axis=1, tiled=True)
+            mixed = lax.dynamic_slice_in_dim(mixed_all, own * rows, rows, axis=0)
         h1 = h0 + mm(mixed, w_out)
         norm1, unit1, scale1 = norm_forward(h1, small[3], small[4])
         up = mm(norm1, w_up)
@@ -803,18 +1118,21 @@
         d_norm1 = mm_t(d_up, w_up)
         d_in, d_gain1, d_off1 = norm_backward(d_norm1, unit1, scale1, small[3])
         d_h1 = d_h2 + d_in
-        d_proj_all = ag(d_h1.astype(bf16))
-        w_out_own = lax.dynamic_slice_in_dim(w_out, own * wide, wide, axis=0)
-        d_mixed = mm_t(d_proj_all, w_out_own).astype(bf16).reshape(row_len, heads_here, HEAD_DIM).transpose(1, 0, 2)
-        d_att = jnp.einsum("hqe,hke->hqk", d_mixed, v, preferred_element_type=f32)
-        d_v = jnp.einsum("hqk,hqe->khe", att, d_mixed, preferred_element_type=f32)
-        lean = jnp.sum(att_soft * d_att, axis=-1, keepdims=True)
-        d_score = (att_soft * (d_att - lean) * HEAD_DIM ** (-0.5)).astype(bf16)
-        d_q = jnp.einsum("hqk,hke->qhe", d_score, k, preferred_element_type=f32)
-        d_k = jnp.einsum("hqk,hqe->khe", d_score, q, preferred_element_type=f32)
-        d_part = jnp.stack([d_q, d_k, d_v], axis=1).astype(bf16).reshape(row_len, 3, 1, wide)
-        d_qkv_all = lax.all_gather(d_part, "fsdp", axis=2, tiled=True).reshape(row_len, 3 * D)
-        d_qkv = lax.dynamic_slice_in_dim(d_qkv_all, own * rows, rows, axis=0)
+        if fast:
+            d_qkv, d_parts, d_proj_all = attend_back(d_h1.astype(bf16), attn, parts, seg_col, seg_row)
+        else:
+            d_proj_all = ag(d_h1.astype(bf16))
+            w_out_own = lax.dynamic_slice_in_dim(w_out, own * wide, wide, axis=0)
+            d_mixed = mm_t(d_proj_all, w_out_own).astype(bf16).reshape(row_len, heads_here, HEAD_DIM).transpose(1, 0, 2)
+            d_att = jnp.einsum("hqe,hke->hqk", d_mixed, v, preferred_element_type=f32)
+            d_v = jnp.einsum("hqk,hqe->khe", att, d_mixed, preferred_element_type=f32)
+            lean = jnp.sum(att_soft * d_att, axis=-1, keepdims=True)
+            d_score = (att_soft * (d_att - lean) * HEAD_DIM ** (-0.5)).astype(bf16)
+            d_q = jnp.einsum("hqk,hke->qhe", d_score, k, preferred_element_type=f32)
+            d_k = jnp.einsum("hqk,hqe->khe", d_score, q, preferred_element_type=f32)
+            d_part = jnp.stack([d_q, d_k, d_v], axis=1).astype(bf16).reshape(row_len, 3, 1, wide)
+            d_qkv_all = lax.all_gather(d_part, "fsdp", axis=2, tiled=True).reshape(row_len, 3 * D)
+            d_qkv = lax.dynamic_slice_in_dim(d_qkv_all, own * rows, rows, axis=0)
         d_norm0 = mm_t(d_qkv, w_qkv)
         d_in, d_gain0, d_off0 = norm_backward(d_norm0, unit0, scale0, small[1])
         d_h0 = d_h1 + d_in
@@ -842,10 +1160,11 @@
 
             lane = lax.broadcasted_iota(jnp.int32, (8, 128), 1)
             r_agg, r_attn, r_mlp, r_misc, stat = gradient_blocks(
-                [sorted_rows(part.T) for part in (mixed_all, norm0, norm1, d_out, mixed_a, norm2, d_agg)]
-                + [d_proj_all, d_qkv_all, d_up, lifted, d_agg, jnp.pad(d_pred, ((0, 0), (0, 256 - WIDTH)))]
-                + [onehot_all, d_table.astype(bf16)]
-                + [sorted_rows(jnp.pad(narrow.T, ((0, 0), (0, 128 - narrow.shape[0])))), sorted_rows(head)],
+                [sorted_rows(part.T) for part in (norm1, d_out, norm0)]
+                + [mixed_t.reshape(2, n_f, strip, row_len)]
+                + [sorted_rows(part.T) for part in (mixed_a, norm2, d_agg)]
+                + [d_proj_all, d_parts, d_up, lifted, d_agg, jnp.pad(d_pred, ((0, 0), (0, 256 - WIDTH)))]
+                + [onehot_all, d_table.astype(bf16), narrow, sorted_rows(head)],
                 jnp.where(lane == 1, numerator, 0.0),
             )
             squares, numerator = stat[0, 0], stat[0, 1]

time: 605 us -> 515 us (0.85); the launches traced: 594 us -> 511 us
  Pallas kernels: 321 us -> 377 us
  waiting for transfers between devices: 55.6 us -> 0 us
  matrix products: 86.8 us -> 54.3 us
  local copies, waits for them, and re-layouts: 68.7 us -> 40.6 us
  between operations: 21.7 us -> 8.55 us
  other arithmetic: 36.5 us -> 30 us
    pallas_call x0 -> x2, Pallas kernels: none -> 55.5 us  [the longest x1 36.6 us: attend_back(): pl.pallas_call(attend_back_kernel, out_shape=[jax.ShapeDtypeStruct((128,...]
    all_gather x3 -> x0, waiting for transfers between devices: 44.1 us -> none  [the longest x1 17.3 us: local(): lax.all_gather(d_part, 'fsdp', axis=2, tiled=True).reshape(row_len, 3 * D)]
    dot_general x5 -> x0, matrix products: 27.4 us -> none  [the longest x1 8.42 us: local(): d_q = jnp.einsum('hqk,hke->qhe', d_score, k, preferred_element_type=f32)]
    reshape x4 -> x0, local copies, waits for them, and re-layouts: 14.2 us -> none  [the longest x1 6.63 us: local(): lax.all_gather(d_part, 'fsdp', axis=2, tiled=True).reshape(row_len, 3 * D)]
    pallas_call x0 -> x1, local copies, waits for them, and re-layouts: none -> 11.6 us  [gather_weights(): pl.pallas_call(gather_kernel, out_shape=[jax.ShapeDtypeStruct((D, a.shape...]
    all_to_all x1 -> x0, waiting for transfers between devices: 11.4 us -> none  [local(): part = lax.all_to_all(part, 'fsdp', split_axis=2, concat_axis=0, tiled=True)]
    dot_general x14 -> x13, matrix products: 45.5 us -> 45.1 us  [dot(): lax.dot_general(left, right, (dims, ((), ())), preferred_element_type=f32)]
  transfers between devices with their start and end apart: 4 -> 0, of which waited for: 4 -> 0; matrix products, arithmetic and copies ran while one was open for 3% -> 0% of each run, Pallas kernels for 0% -> 0%
where the time goes in v4:
time: 515 us; the launch traced here: 511 us
  Pallas kernels  377 us (73%)
  matrix products  54.3 us (11%)
  local copies, waits for them, and re-layouts  40.6 us (8%)
  other arithmetic  30 us (6%)
  between operations  8.55 us (2%)
    pallas_call x1, Pallas kernels, gradient_blocks(): pl.pallas_call(gradient_kernel, out_shape=[jax.ShapeDtypeStruct((STRIP, w...  178 us
    pallas_call x1, Pallas kernels, gather_weights(): pl.pallas_call(gather_kernel, out_shape=[jax.ShapeDtypeStruct((D, a.shape...  144 us
    dot_general x13, matrix products, dot(): lax.dot_general(left, right, (dims, ((), ())), preferred_element_type=f32)  45.1 us
    pallas_call x1, Pallas kernels, attend_back(): pl.pallas_call(attend_back_kernel, out_shape=[jax.ShapeDtypeStruct((128,...  36.6 us
    pallas_call x1, Pallas kernels, attend(): pl.pallas_call(attend_kernel, out_shape=[jax.ShapeDtypeStruct((128, D), b...  18.9 us
    pallas_call x1, local copies, waits for them, and re-layouts, gather_weights(): pl.pallas_call(gather_kernel, out_shape=[jax.ShapeDtypeStruct((D, a.shape...  11.6 us

profile of v4, /device:TPU:0, one launch (start us, length us, event | category | flops | bytes accessed | tf_op | source)
XLA Modules:
  0.0 510.7 jit_solution(11167807476744447384)
XLA Ops:
  6.4 1.4 fusion.92
  10.6 144.1 %gather_weights.1 = (bf16[1024,3968]{1,0:T(8,128)(2,1)}, bf16[1024,4096]{1,0:T(8,128)(2,1)}, bf16[1024,8192]{1,0:T(8,128)(2,1)}, f32[8,128]{1,0:T(8,128)}) custom-call(bf16[32,3968]{1,0:T(8,128)(2,1)} %concatenate.17.refs_0_, bf16[32,4096]{1,0:T(8,128)(2,1)} %convert_element_type.159.refs_1_, bf16[32,8192]{1,0:T(8,128)(2,1)} %convert_element_type.160.refs_2_, ...), custom_call_target="tpu_custom_call" | custom-call | tf_op jit(solution)/shard_map/gather_weights/pallas_call | solution.py:232
  154.7 11.6 %copy.128 = bf16[1024,3968]{0,1:T(8,128)(2,1)} copy(bf16[1024,3968]{1,0:T(8,128)(2,1)} %get-tuple-element.37) | data formatting | bytes 16252928 | tf_op jit(solution)/shard_map/gather_weights/pallas_call | solution.py:232
  168.6 3.6 fusion.20
  176.7 1.6 copy.126
  178.6 2.3 fusion.62
  182.8 1.3 fusion.74
  184.2 2.3 fusion.131
  186.8 4.0 fusion.22.qkv
  191.0 18.9 %attend.1 = (bf16[128,1024]{1,0:T(8,128)(2,1)S(1)}, bf16[256,512]{1,0:T(8,128)(2,1)S(1)}, bf16[3,512,256]{2,1,0:T(8,128)(2,1)S(1)}) custom-call(bf16[128,3072]{1,0:T(8,128)(2,1)S(1)} %fusion.22.qkv, s32[512,128]{1,0:T(8,128)S(1)} %broadcast_in_dim.108.seg_col, s32[8,512]{1,0:T(8,128)S(1)} %broadcast_in_dim.109.seg_row), custom_call_target="tpu_custom_call" | custom-call | tf_op jit(solution)/shard_map/attend/pallas_call | solution.py:329
  210.0 2.3 fusion.132
  212.5 6.5 %multiply_convert_fusion = (bf16[128,4096]{1,0:T(8,128)(2,1)S(1)}, f32[128,4096]{1,0:T(8,128)}) fusion(bf16[1024,8192]{1,0:T(8,128)(2,1)} %get-tuple-element.40, f32[128,1024]{1,0:T(8,128)S(1)} %get-tuple-element.209, f32[1024]{0:T(1024)S(1)} %bitcast.146, f32[1024]{0:T(1024)S(1)} %bitcast.148, f32[128]{0:T(128)S(1)} %add_rsqrt_fusion.1, ...), kind=kOutput, calls=%fused_computation.29 | convolution fusion | flops 1077018624 | bytes 12067840 | tf_op jit(solution)/shard_map/dot_general | solution.py:38
  219.1 3.0 fusion.133
  225.7 2.3 multiply_reduce_fusion.15
  228.0 1.5 fusion.77
  229.5 2.2 multiply_reduce_fusion.2
  231.8 1.6 convert_bitcast_fusion
  233.4 5.6 %fusion.17.refs_9_ = bf16[128,4096]{1,0:T(8,128)(2,1)S(1)} fusion(bf16[1024,8192]{1,0:T(8,128)(2,1)} %get-tuple-element.40, f32[128,4096]{1,0:T(8,128)S(1)} %copy-done.79, f32[128,1024]{1,0:T(8,128)S(1)} %get-tuple-element.177), kind=kOutput, calls=%fused_computation.15 | convolution fusion | flops 1079115776 | bytes 12058624 | tf_op jit(solution)/shard_map/dot_general | solution.py:38
  239.1 7.4 %multiply_reduce_fusion.3 = (f32[1024]{0:T(1024)}, f32[128]{0:T(128)S(1)}, f32[128]{0:T(128)S(1)}, f32[1024]{0:T(1024)}, f32[128,1024]{1,0:T(8,128)S(1)}) fusion(f32[128,1024]{1,0:T(8,128)S(1)} %copy-done.11, f32[128]{0:T(128)S(1)} %copy-done.77, f32[128]{0:T(128)S(1)} %copy-done.73, f32[1024]{0:T(1024)S(1)} %bitcast.149, ...), kind=kOutput, calls=%fused_computation.81 | convolution fusion | flops 1074919168 | bytes 10500096 | tf_op jit(solution)/shard_map/dot_general | solution.py:38
  247.5 36.6 %attend_back.1 = (bf16[128,3072]{1,0:T(8,128)(2,1)S(1)}, bf16[3,512,256]{2,1,0:T(8,128)(2,1)S(1)}, bf16[512,1024]{1,0:T(8,128)(2,1)S(1)}) custom-call(bf16[128,1024]{1,0:T(8,128)(2,1)S(1)} %get-tuple-element.174.d_proj, bf16[1024,4096]{1,0:T(8,128)(2,1)S(1)} %bitcast.111, bf16[3,512,256]{2,1,0:T(8,128)(2,1)S(1)} %get-tuple-element.43.parts, ...), custom_call_target="tpu_custom_call" | custom-call | tf_op jit(solution)/shard_map/attend_back/pallas_call | solution.py:431
  284.2 2.9 multiply_reduce_fusion.4
  288.0 2.4 fusion.58
  292.9 1.6 fusion.29
  295.6 1.6 copy.140
  297.2 2.8 multiply_reduce_fusion
  300.0 2.8 stack.37.refs_15_
  302.8 1.9 fusion.40
  312.2 177.6 %gradient_blocks.1 = (f32[32,3072]{1,0:T(8,128)}, f32[32,4096]{1,0:T(8,128)}, f32[32,8192]{1,0:T(8,128)}, f32[32,1024]{1,0:T(8,128)}, f32[8,128]{1,0:T(8,128)}) custom-call(bf16[4,2,4,32,128]{4,3,2,1,0:T(8,128)(2,1)} %bitcast.123, bf16[4,2,4,32,128]{4,3,2,1,0:T(8,128)(2,1)} %bitcast.124, bf16[4,2,4,32,128]{4,3,2,1,0:T(8,128)(2,1)} %bitcast.121, ...), custom_call_target="tpu_custom_call" | custom-call | tf_op jit(solution)/shard_map/gradient_blocks/pallas_call | solution.py:925
  489.8 1.4 fusion.129
  499.7 4.1 fusion.117
  503.8 1.5 fusion.119
  505.6 1.3 fusion.121
  (267 shorter events, 40.3 us)
Async XLA Ops:
  0.7 8.3 %copy-start.12 = (f32[32,8192]{1,0:T(8,128)S(1)}, f32[32,8192]{1,0:T(8,128)}, u32[]{:S(2)}) copy-start(f32[32,8192]{1,0:T(8,128)} %param.33) | copy-start | bytes 3145732
  0.7 9.2 %copy-start.16 = (f32[32,4096]{1,0:T(8,128)S(1)}, f32[32,4096]{1,0:T(8,128)}, u32[]{:S(2)}) copy-start(f32[32,4096]{1,0:T(8,128)} %param.32) | copy-start | bytes 1572868
  5.5 160.8 %copy-start.32 = (s32[1,128,192]{2,1,0:T(8,128)}, s32[1,128,192]{2,1,0:T(8,128)S(1)}, u32[]{:S(2)}) copy-start(s32[1,128,192]{2,1,0:T(8,128)S(1)} %copy.125) | copy-start | bytes 294916
  6.4 159.9 %copy-start.68 = (f32[192]{0:T(256)}, f32[192]{0:T(256)S(1)}, u32[]{:S(2)}) copy-start(f32[192]{0:T(256)S(1)} %mul.544) | copy-start | bytes 2308
  184.2 34.8 %slice-start.2 = ((s8[16777216]{0:T(1024)(128)(4,1)}), s8[4194304]{0:T(1024)(128)(4,1)S(1)}, s32[]{:S(2)}) async-start(s8[16777216]{0:T(1024)(128)(4,1)} %bitcast.163), calls=%async_computation.2 | async-start | bytes 8388608
  186.5 23.4 %copy-start.5 = (f32[128,1024]{1,0:T(8,128)}, f32[128,1024]{1,0:T(8,128)S(1)}, u32[]{:S(2)}) copy-start(f32[128,1024]{1,0:T(8,128)S(1)} %get-tuple-element.207) | copy-start | bytes 1572868
  186.8 32.3 %slice-start.3 = ((s8[16777216]{0:T(1024)(128)(4,1)}), s8[4194304]{0:T(1024)(128)(4,1)S(1)}, s32[]{:S(2)}) async-start(s8[16777216]{0:T(1024)(128)(4,1)} %bitcast.163), calls=%async_computation.3 | async-start | bytes 8388608
  209.9 9.1 %copy-start.2 = (bf16[256,512]{1,0:T(8,128)(2,1)}, bf16[256,512]{1,0:T(8,128)(2,1)S(1)}, u32[]{:S(2)}) copy-start(bf16[256,512]{1,0:T(8,128)(2,1)S(1)} %get-tuple-element.42) | copy-start | bytes 786436
  209.9 9.1 %slice-start.4 = ((s8[16777216]{0:T(1024)(128)(4,1)}), s8[4194304]{0:T(1024)(128)(4,1)S(1)}, s32[]{:S(2)}) async-start(s8[16777216]{0:T(1024)(128)(4,1)} %bitcast.163), calls=%async_computation.4 | async-start | bytes 8388608
  212.2 6.8 %copy-start.10 = (f32[128,1024]{1,0:T(8,128)}, f32[128,1024]{1,0:T(8,128)S(1)}, u32[]{:S(2)}) copy-start(f32[128,1024]{1,0:T(8,128)S(1)} %get-tuple-element.209) | copy-start | bytes 1572868
  212.2 6.8 %copy-start.72 = (f32[128]{0:T(128)}, f32[128]{0:T(128)S(1)}, u32[]{:S(2)}) copy-start(f32[128]{0:T(128)S(1)} %broadcast_multiply_fusion.8) | copy-start | bytes 1540
  212.5 6.6 %copy-start.76 = (f32[128]{0:T(128)}, f32[128]{0:T(128)S(1)}, u32[]{:S(2)}) copy-start(f32[128]{0:T(128)S(1)} %add_rsqrt_fusion.1) | copy-start | bytes 1540
  212.5 6.6 %slice-start.5 = ((s8[16777216]{0:T(1024)(128)(4,1)}), s8[4194304]{0:T(1024)(128)(4,1)S(1)}, s32[]{:S(2)}) async-start(s8[16777216]{0:T(1024)(128)(4,1)} %bitcast.163), calls=%async_computation.5 | async-start | bytes 8388608
  219.1 6.6 %copy-start.33 = (s32[1,128,192]{2,1,0:T(8,128)S(1)}, s32[1,128,192]{2,1,0:T(8,128)}, u32[]{:S(2)}) copy-start(s32[1,128,192]{2,1,0:T(8,128)} %copy-done.32) | copy-start | bytes 294916
  233.4 14.1 %slice-start = ((s8[8388608]{0:T(1024)(128)(4,1)}), s8[4194304]{0:T(1024)(128)(4,1)S(1)}, s32[]{:S(2)}) async-start(s8[8388608]{0:T(1024)(128)(4,1)} %bitcast.110), calls=%async_computation | async-start | bytes 8388608
  233.4 14.0 %slice-start.1 = ((s8[8388608]{0:T(1024)(128)(4,1)}), s8[4194304]{0:T(1024)(128)(4,1)S(1)}, s32[]{:S(2)}) async-start(s8[8388608]{0:T(1024)(128)(4,1)} %bitcast.110), calls=%async_computation.1 | async-start | bytes 8388608
  239.1 7.4 %copy-start.22 = (bf16[128,4096]{1,0:T(8,128)(2,1)}, bf16[128,4096]{1,0:T(8,128)(2,1)S(1)}, u32[]{:S(2)}) copy-start(bf16[128,4096]{1,0:T(8,128)(2,1)S(1)} %fusion.17.refs_9_) | copy-start | bytes 3145732
  239.1 7.4 %copy-start.58 = (f32[1,1024]{1,0:T(1,128)S(1)}, f32[1,1024]{1,0:T(1,128)}, u32[]{:S(2)}) copy-start(f32[1,1024]{1,0:T(1,128)} %get-tuple-element.192) | copy-start | bytes 12292
  247.5 36.6 %copy-start.6 = (f32[128,1024]{1,0:T(8,128)S(1)}, f32[128,1024]{1,0:T(8,128)}, u32[]{:S(2)}) copy-start(f32[128,1024]{1,0:T(8,128)} %copy-done.5) | copy-start | bytes 1572868
  247.5 36.7 %copy-start.56 = (f32[1,1024]{1,0:T(1,128)S(1)}, f32[1,1024]{1,0:T(1,128)}, u32[]{:S(2)}) copy-start(f32[1,1024]{1,0:T(1,128)} %get-tuple-element.195) | copy-start | bytes 12292
  247.5 36.7 %copy-start.71 = (f32[128]{0:T(128)S(1)}, f32[128]{0:T(128)}, u32[]{:S(2)}) copy-start(f32[128]{0:T(128)} %copy-done.70) | copy-start | bytes 1540
  247.5 36.7 %copy-start.75 = (f32[128]{0:T(128)S(1)}, f32[128]{0:T(128)}, u32[]{:S(2)}) copy-start(f32[128]{0:T(128)} %copy-done.74) | copy-start | bytes 1540
  288.0 11.9 %copy-start.43 = (f32[1024]{0:T(1024)}, f32[1024]{0:T(1024)S(1)}, u32[]{:S(2)}) copy-start(f32[1024]{0:T(1024)S(1)} %get-tuple-element.172) | copy-start | bytes 12292
  288.0 18.8 %copy-start.15 = (bf16[128,1024]{1,0:T(8,128)(2,1)}, bf16[128,1024]{1,0:T(8,128)(2,1)S(1)}, u32[]{:S(2)}) copy-start(bf16[128,1024]{1,0:T(8,128)(2,1)S(1)} %get-tuple-element.173.refs_11_) | copy-start | bytes 786436
  312.1 180.5 %copy-start.62 = (f32[32,9]{0,1:T(8,128)S(1)}, f32[32,9]{0,1:T(8,128)}, u32[]{:S(2)}) copy-start(f32[32,9]{0,1:T(8,128)} %param.40) | copy-start | bytes 3460
  312.1 180.6 %copy-start.63 = (f32[32,9]{0,1:T(8,128)S(1)}, f32[32,9]{0,1:T(8,128)}, u32[]{:S(2)}) copy-start(f32[32,9]{0,1:T(8,128)} %param.45) | copy-start | bytes 3460
  312.1 180.6 %copy-start.47 = (f32[32,9]{0,1:T(8,128)S(1)}, f32[32,9]{0,1:T(8,128)}, u32[]{:S(2)}) copy-start(f32[32,9]{0,1:T(8,128)} %param.35) | copy-start | bytes 3460
  312.1 186.6 %copy-start.31 = (f32[32,944]{1,0:T(8,128)S(1)}, f32[32,944]{1,0:T(8,128)}, u32[]{:S(2)}) copy-start(f32[32,944]{1,0:T(8,128)} %param.34) | copy-start | bytes 362500
  312.1 186.6 %copy-start.39 = (f32[32,944]{1,0:T(8,128)S(1)}, f32[32,944]{1,0:T(8,128)}, u32[]{:S(2)}) copy-start(f32[32,944]{1,0:T(8,128)} %param.44) | copy-start | bytes 362500
  312.2 186.6 %copy-start.40 = (f32[32,944]{1,0:T(8,128)S(1)}, f32[32,944]{1,0:T(8,128)}, u32[]{:S(2)}) copy-start(f32[32,944]{1,0:T(8,128)} %param.39) | copy-start | bytes 362500
  312.2 187.4 %copy-start.20 = (f32[32,8192]{1,0:T(8,128)S(1)}, f32[32,8192]{1,0:T(8,128)}, u32[]{:S(2)}) copy-start(f32[32,8192]{1,0:T(8,128)} %param.43) | copy-start | bytes 3145732
  489.8 9.8 %copy-start.13 = (f32[32,8192]{1,0:T(8,128)S(1)}, f32[32,8192]{1,0:T(8,128)}, u32[]{:S(2)}) copy-start(f32[32,8192]{1,0:T(8,128)} %param.33) | copy-start | bytes 3145732
  (54 other events, 174.2 us)
